TPU v7x, 32 devices: a whole 2x2x4 slice. The times are simulated.
32 devices in a mesh: lat: 4 (over x, core), lon: 8 (over z, y).
Axes of the slice: x: 2, y: 2, z: 4, core: 2. Of those that a mesh axis runs over, the one named last changes fastest.
Arguments:
- tokens: bfloat16 [1, 48, 96, 512], P(None, 'lat', 'lon'), may hold values from -8 to 8
- gain_first: float32 [512], replicated, may hold values from 0.1 to 1.9
- qkv_first: bfloat16 [512, 1536], replicated, may hold values from -16 to 16
- proj_first: bfloat16 [512, 512], replicated, may hold values from -0.25 to 0.25
- bias_first: float32 [4, 16, 529], P('lat'), may hold values from -6 to 6
- gain_second: float32 [512], replicated, may hold values from 0.1 to 1.9
- qkv_second: bfloat16 [512, 1536], replicated, may hold values from -16 to 16
- proj_second: bfloat16 [512, 512], replicated, may hold values from -0.25 to 0.25
- bias_second: float32 [4, 16, 529], P('lat'), may hold values from -6 to 6
Outputs:
- mixed: bfloat16 [1, 48, 96, 512], P(None, 'lat', 'lon')
All inputs are finite; a program needn't handle non-finite values.
Results may differ from a plain program's by a relative error of at most 0.012.
The roundings to bfloat16 on the way count: a program that leaves them out, or rounds other values in their place, can miss the bound.
Values may be sent and summed in bfloat16 or wider, within the bound.
No kernel may reach another device: no remote copies, remote signals or barrier semaphores. Data moves between devices by JAX's collectives and lax.ppermute only.
A program may use at most 64 MiB of HBM per device.

v0:
```python
import jax
import jax.numpy as jnp
from jax import lax
from jax.sharding import PartitionSpec as P

HEADS = 16
LEV = 1
WH = 12
WW = 12


def shifted(block, axis, distance):
    devices = range(lax.axis_size(axis))
    route = [((i - distance) % len(devices), i) for i in devices]
    return lax.ppermute(block, axis, route)


def offsets():
    count = LEV * WH * WW
    index = jnp.arange(count, dtype=jnp.int32)
    level = index // (WH * WW)
    row = index // WW % WH
    column = index % WW
    first = level[:, None] - level[None, :] + LEV - 1
    second = row[:, None] - row[None, :] + WH - 1
    third = column[:, None] - column[None, :] + WW - 1
    return (first * (2 * WH - 1) + second) * (2 * WW - 1) + third


def to_windows(tile):
    levels, rows, cols, width = tile.shape
    shaped = tile.reshape(levels, rows, cols // WW, WW, width)
    return shaped.transpose(2, 0, 1, 3, 4).reshape(cols // WW, levels * rows * WW, width)


def from_windows(wins, cols):
    width = wins.shape[-1]
    shaped = wins.reshape(cols // WW, LEV, WH, WW, width)
    return shaped.transpose(1, 2, 0, 3, 4).reshape(LEV, WH, cols, width)


def norm_rows(values, gain):
    data = values.astype(jnp.float32)
    mean = jnp.mean(data, axis=-1, keepdims=True)
    centred = data - mean
    var = jnp.mean(centred * centred, axis=-1, keepdims=True)
    return (centred * lax.rsqrt(var + 1e-05) * gain).astype(jnp.bfloat16)


def project_all(normed, wqkv):
    width = normed.shape[-1]
    flat = jnp.dot(normed.reshape(-1, width), wqkv, preferred_element_type=jnp.float32)
    return flat.reshape(normed.shape[:-1] + (3 * width,))


def attend_split(query, keys, values, wproj, bias, allowed):
    count, size, width = query.shape
    head_dim = width // HEADS
    query = query.reshape(count, size, HEADS, head_dim)
    keys = keys.reshape(count, size, HEADS, head_dim)
    values = values.reshape(count, size, HEADS, head_dim)
    scores = jnp.einsum("wqhd,wkhd->whqk", query, keys, precision=lax.Precision.HIGHEST)
    scores = scores * head_dim ** (-0.5) + bias[None]
    if allowed is not None:
        scores = jnp.where(allowed[None, None], scores, -1e30)
    top = jnp.max(scores, axis=-1, keepdims=True)
    expo = jnp.exp(scores - top)
    weights = (expo / jnp.sum(expo, axis=-1, keepdims=True)).astype(jnp.bfloat16)
    heads_out = jnp.einsum("whqk,wkhd->wqhd", weights, values, preferred_element_type=jnp.float32)
    heads_out = heads_out.reshape(count * size, width).astype(jnp.bfloat16)
    return jnp.dot(heads_out, wproj, preferred_element_type=jnp.float32).reshape(count, size, width)


def attend_tokens(wins, gain, wqkv, wproj, bias, allowed):
    width = wins.shape[-1]
    mixed = project_all(norm_rows(wins, gain), wqkv)
    query = mixed[..., :width]
    keys = mixed[..., width : 2 * width]
    values = mixed[..., 2 * width :].astype(jnp.bfloat16)
    return attend_split(query, keys, values, wproj, bias, allowed)


def shards(
    tokens,
    gain_first,
    qkv_first,
    proj_first,
    bias_first,
    gain_second,
    qkv_second,
    proj_second,
    bias_second,
):
    levels, rows, cols, width = tokens.shape
    rel = offsets()
    count = LEV * WH * WW
    half_rows = WH // 2
    half_cols = WW // 2
    wins = to_windows(tokens)
    bias_one = jnp.take(bias_first[0], rel, axis=1)
    result = wins.astype(jnp.float32) + attend_tokens(
        wins, gain_first, qkv_first, proj_first, bias_one, None
    )
    first = from_windows(result.astype(jnp.bfloat16), cols)
    index = jnp.arange(count, dtype=jnp.int32)
    lower = index // WW % WH >= half_rows
    polar = lax.axis_index("lat") == lax.axis_size("lat") - 1
    group = jnp.logical_and(lower, polar)
    allowed = group[:, None] == group[None, :]
    bias_two = jnp.take(bias_second[0], rel, axis=1)
    east = shifted(first[:, :, :half_cols], "lon", -1)
    shifted_cols = jnp.concatenate([first[:, :, half_cols:], east], axis=2)
    south = shifted(shifted_cols[:, :half_rows], "lat", -1)
    window = to_windows(jnp.concatenate([shifted_cols[:, half_rows:], south], axis=1))
    branch = window.astype(jnp.float32) + attend_tokens(
        window, gain_second, qkv_second, proj_second, bias_two, allowed
    )
    back = from_windows(branch.astype(jnp.bfloat16), cols)
    north = shifted(back[:, half_rows:], "lat", 1)
    rows_back = jnp.concatenate([north, back[:, :half_rows]], axis=1)
    west = shifted(rows_back[:, :, cols - half_cols :], "lon", 1)
    mixed_out = jnp.concatenate([west, rows_back[:, :, : cols - half_cols]], axis=2)
    return mixed_out


def solution(mesh):
    placed = (
        P(None, "lat", "lon", None),
        P(),
        P(),
        P(),
        P("lat", None, None),
        P(),
        P(),
        P(),
        P("lat", None, None),
    )
    return jax.shard_map(
        shards, mesh=mesh, in_specs=placed, out_specs=P(None, "lat", "lon", None), check_vma=False
    )
```

profile of v0, /device:TPU:0, one launch (start us, length us, event | category | flops | bytes accessed | tf_op | source)
XLA Modules:
  0.0 163.2 jit_solution(9387984917359832487)
XLA Ops:
  0.0 0.0 copy-start
  0.0 1.1 reshape.438
  1.1 1.0 reshape.439
  2.0 1.0 convert_reduce_fusion
  3.1 0.1 div.75
  3.2 0.2 multiply_reduce_fusion
  3.4 0.0 copy-done
  3.4 0.0 copy-start.9
  3.5 1.1 convolution_bitcast_fusion.1
  4.6 0.8 fusion.25
  5.4 0.1 compare_select_fusion
  5.5 0.2 compare_and_fusion
  5.7 0.9 copy.20
  6.5 0.0 copy-done.9
  6.6 0.1 copy.24
  6.7 0.1 reshape.462
  6.9 38.7 %gather_fusion = f32[20736,16]{1,0:T(8,128)} fusion(f32[16,529]{0,1:T(8,128)S(1)} %bitcast.52, s32[21504]{0:T(1024)S(1)} %pad_clamp_fusion), kind=kCustom, calls=%fused_computation.clone | custom fusion | bytes 2737152 | tf_op jit(solution)/shard_map/jit(_take)/gather | solution.py:100
  45.5 12.2 %copy.26 = f32[144,144,16]{0,1,2:T(8,128)} copy(f32[144,144,16]{2,1,0:T(8,128)} %bitcast.55) | data formatting | bytes 2654208 | tf_op jit(solution)/shard_map/jit(_take)/gather | solution.py:100
  57.7 0.2 copy.21
  57.9 1.2 copy.22
  59.1 0.1 copy.23
  59.2 4.1 %bitcast_add_fusion.1 = f32[16,144,144]{1,2,0:T(8,128)S(1)} fusion(f32[144,144,16]{0,1,2:T(8,128)} %copy.26, f32[144,16,32]{0,2,1:T(8,128)S(1)} %bitcast.56, f32[144,16,32]{0,2,1:T(8,128)S(1)} %bitcast.58, pred[144,144]{0,1:T(8,128)(4,1)S(1)} %copy.23), kind=kOutput, calls=%fused_computation.8 | convolution fusion | flops 128397312 | bytes 3264768 | tf_op jit(solution)/shard_map/wqhd,wkhd->whqk/dot_general | solution.py:62
  63.3 0.0 copy-start.2
  63.3 1.4 copy-done.2
  64.7 0.5 fusion.28
  65.2 0.5 copy-done.7
  65.7 3.1 %convolution_convert_fusion.1 = bf16[16,32,144]{2,1,0:T(8,128)(2,1)S(1)} fusion(bf16[144,16,32]{0,2,1:T(8,128)(2,1)S(1)} %bitcast.62, f32[16,144]{1,0:T(8,128)S(1)} %fusion.28, f32[16,144,144]{1,2,0:T(8,128)} %copy-done.2), kind=kOutput, calls=%fused_computation.14 | convolution fusion | flops 22305168 | bytes 1631232 | tf_op jit(solution)/shard_map/whqk,wkhd->wqhd/dot_general | solution.py:69
  68.8 0.0 copy-start.10
  68.8 0.3 fusion.3
  69.1 0.1 reshape_transpose_reshape.10
  69.2 0.3 fusion.26
  69.5 6.1 %collective-permute-start = (bf16[1,12,6,512]{3,0,2,1:T(2,128)(2,1)S(1)}, bf16[1,12,6,512]{3,0,2,1:T(2,128)(2,1)S(1)}, u32[]{:S(2)}, u32[]{:S(2)}) collective-permute-start(bf16[1,12,6,512]{3,0,2,1:T(2,128)(2,1)S(1)} %get-tuple-element.16), channel_id=1, source_target_pairs={{1,0},{2,1},{3,2},{4,3},{5,4},{6,5},{7,6},{0,7},{9,8},{10,9},{11,1... | collective-permute-start | bytes 221192 | tf_op jit(solution)/shard_map/ppermute | solution.py:15
  75.6 3.1 %collective-permute-done = bf16[1,12,6,512]{3,0,2,1:T(2,128)(2,1)S(1)} collective-permute-done((bf16[1,12,6,512]{3,0,2,1:T(2,128)(2,1)S(1)}, bf16[1,12,6,512]{3,0,2,1:T(2,128)(2,1)S(1)}, u32[]{:S(2)}, u32[]{:S(2)}) %collective-permute-start) | collective-permute-done | bytes 73760 | tf_op jit(solution)/shard_map/ppermute | solution.py:15
  78.7 1.1 fusion.8
  79.8 0.1 collective-permute-start.1
  79.9 0.1 broadcast_compare_fusion
  80.0 0.0 copy-done.10
  80.0 0.1 copy.34
  80.1 38.7 %gather_fusion.1 = f32[20736,16]{1,0:T(8,128)} fusion(f32[16,529]{0,1:T(8,128)S(1)} %bitcast.53, s32[21504]{0:T(1024)S(1)} %pad_clamp_fusion), kind=kCustom, calls=%fused_computation.1.clone | custom fusion | bytes 2737152 | tf_op jit(solution)/shard_map/jit(_take)/gather | solution.py:110
  118.8 12.2 %copy.36 = f32[144,144,16]{0,1,2:T(8,128)} copy(f32[144,144,16]{2,1,0:T(8,128)} %bitcast.54) | data formatting | bytes 2654208 | tf_op jit(solution)/shard_map/jit(_take)/gather | solution.py:110
  131.0 0.0 collective-permute-done.1
  131.0 3.6 %fusion.23 = (f32[12,12]{1,0:T(8,128)S(1)}, f32[12,12,512]{2,1,0:T(8,128)}, f32[1,12,12,512]{3,0,2,1:T(1,128)}) fusion(bf16[1,6,12,512]{3,0,2,1:T(2,128)(2,1)} %collective-permute-done.1, bf16[1,6,12,512]{3,0,2,1:T(2,128)(2,1)S(1)} %copy-done.4), kind=kLoop, calls=%fused_computation.68 | loop fusion | flops 221040 | bytes 737856 | tf_op jit(solution)/shard_map/reduce_sum | solution.py:44
  134.6 1.0 reshape.440
  135.6 0.1 div.82
  135.7 2.9 %fusion.6 = f32[144]{0:T(256)S(1)} fusion(f32[1,12,12,512]{3,0,2,1:T(1,128)} %get-tuple-element.8, f32[144]{0:T(256)S(1)} %div.82), kind=kLoop, calls=%fused_computation.30 | loop fusion | flops 221040 | bytes 296064 | tf_op jit(solution)/shard_map/reduce_sum | solution.py:46
  138.6 0.0 copy-done.11
  138.6 0.0 copy-done.3
  138.7 0.4 convolution_bitcast_fusion
  139.2 0.8 copy.30
  140.0 0.2 copy.31
  140.2 0.2 copy.32
  140.4 4.3 %fusion.2 = f32[16,144,144]{1,2,0:T(8,128)S(1)} fusion(f32[144,144,16]{0,1,2:T(8,128)} %copy.36, f32[144,16,32]{0,2,1:T(8,128)S(1)} %bitcast.57, f32[144,16,32]{0,2,1:T(8,128)S(1)} %bitcast.59, pred[144,144]{0,1:T(8,128)(4,1)S(1)} %copy.23, pred[144,144]{0,1:T(8,128)(4,1)S(1)} %broadcast_compare_fusion), kind=kOutput, calls=%fused_computation.7 | convolution fusion | flops 128729088 | bytes 3285504 | tf_op jit(solution)/shard_map/wqhd,wkhd->whqk/dot_general | solution.py:62
  144.7 0.0 copy-start.1
  144.7 1.4 copy-done.1
  146.1 0.5 fusion.29
  146.6 0.5 copy-done.8
  147.1 3.1 %convolution_convert_fusion = bf16[16,32,144]{2,1,0:T(8,128)(2,1)S(1)} fusion(bf16[144,16,32]{0,2,1:T(8,128)(2,1)S(1)} %bitcast.63, f32[16,144]{1,0:T(8,128)S(1)} %fusion.29, f32[16,144,144]{1,2,0:T(8,128)} %copy-done.1), kind=kOutput, calls=%fused_computation.13 | convolution fusion | flops 22305168 | bytes 1631232 | tf_op jit(solution)/shard_map/whqk,wkhd->wqhd/dot_general | solution.py:69
  150.2 0.0 copy-done.6
  150.2 0.3 fusion.4
  150.5 0.5 collective-permute-start.2
  151.0 3.6 %collective-permute-done.2 = bf16[1,6,12,512]{3,2,1,0:T(8,128)(2,1)S(1)} collective-permute-done((bf16[1,6,12,512]{3,2,1,0:T(8,128)(2,1)S(1)}, bf16[1,6,12,512]{3,2,1,0:T(8,128)(2,1)S(1)}, u32[]{:S(2)}, u32[]{:S(2)}) %collective-permute-start.2) | collective-permute-done | bytes 73760 | tf_op jit(solution)/shard_map/ppermute | solution.py:15
  154.6 0.4 collective-permute-start.3
  155.0 7.4 %collective-permute-done.3 = bf16[1,12,6,512]{3,2,1,0:T(8,128)(2,1)S(1)} collective-permute-done((bf16[1,12,6,512]{3,2,1,0:T(8,128)(2,1)S(1)}, bf16[1,12,6,512]{3,2,1,0:T(8,128)(2,1)S(1)}, u32[]{:S(2)}, u32[]{:S(2)}) %collective-permute-start.3) | collective-permute-done | bytes 73760 | tf_op jit(solution)/shard_map/ppermute | solution.py:15
  162.5 0.8 fusion.7
  (23 shorter events, 0.3 us)
Async XLA Ops:
  0.0 3.4 %copy-start = (bf16[512,1536]{1,0:T(8,128)(2,1)S(1)}, bf16[512,1536]{1,0:T(8,128)(2,1)}, u32[]{:S(2)}) copy-start(bf16[512,1536]{1,0:T(8,128)(2,1)} %param.13) | copy-start | bytes 4718596
  3.4 3.1 %copy-start.9 = (f32[1,16,529]{2,1,0:T(8,128)S(1)}, f32[1,16,529]{2,1,0:T(8,128)}, u32[]{:S(2)}) copy-start(f32[1,16,529]{2,1,0:T(8,128)} %param.15) | copy-start | bytes 101572
  63.3 1.4 copy-start.2
  64.7 0.9 copy-start.7
  65.7 3.1 %copy-start.5 = (bf16[512,512]{1,0:T(8,128)(2,1)S(1)}, bf16[512,512]{1,0:T(8,128)(2,1)}, u32[]{:S(2)}) copy-start(bf16[512,512]{1,0:T(8,128)(2,1)} %param.14) | copy-start | bytes 1572868
  68.8 11.2 %copy-start.10 = (f32[1,16,529]{2,1,0:T(8,128)S(1)}, f32[1,16,529]{2,1,0:T(8,128)}, u32[]{:S(2)}) copy-start(f32[1,16,529]{2,1,0:T(8,128)} %param.19) | copy-start | bytes 101572
  69.5 9.2 %collective-permute-start = (bf16[1,12,6,512]{3,0,2,1:T(2,128)(2,1)S(1)}, bf16[1,12,6,512]{3,0,2,1:T(2,128)(2,1)S(1)}, u32[]{:S(2)}, u32[]{:S(2)}) collective-permute-start(bf16[1,12,6,512]{3,0,2,1:T(2,128)(2,1)S(1)} %get-tuple-element.16), channel_id=1, source_target_pairs={{1,0},{2,1},{3,2},{4,3},{5,4},{6,5},{7,6},{0,7},{9,8},{10,9},{11,1... | collective-permute-start | bytes 221192 | tf_op jit(solution)/shard_map/ppermute | solution.py:15
  79.8 51.2 %collective-permute-start.1 = (bf16[1,6,12,512]{3,0,2,1:T(2,128)(2,1)}, bf16[1,6,12,512]{3,0,2,1:T(2,128)(2,1)}, u32[]{:S(2)}, u32[]{:S(2)}) collective-permute-start(bf16[1,6,12,512]{3,0,2,1:T(2,128)(2,1)} %get-tuple-element.14), channel_id=1, source_target_pairs={{8,0},{16,8},{24,16},{0,24},{9,1},{17,9},{25,17},{1,25},{10,2},{18... | collective-permute-start | bytes 221192 | tf_op jit(solution)/shard_map/ppermute | solution.py:15
  118.8 12.2 %copy-start.4 = (bf16[1,6,12,512]{3,0,2,1:T(2,128)(2,1)S(1)}, bf16[1,6,12,512]{3,0,2,1:T(2,128)(2,1)}, u32[]{:S(2)}) copy-start(bf16[1,6,12,512]{3,0,2,1:T(2,128)(2,1)} %get-tuple-element.13) | copy-start | bytes 221188
  118.8 19.9 %copy-start.11 = (f32[512]{0:T(512)S(1)}, f32[512]{0:T(512)}, u32[]{:S(2)}) copy-start(f32[512]{0:T(512)} %param.16) | copy-start | bytes 6148
  131.0 7.6 %copy-start.3 = (bf16[512,1536]{1,0:T(8,128)(2,1)S(1)}, bf16[512,1536]{1,0:T(8,128)(2,1)}, u32[]{:S(2)}) copy-start(bf16[512,1536]{1,0:T(8,128)(2,1)} %param.17) | copy-start | bytes 4718596
  144.7 1.4 copy-start.1
  146.1 0.9 copy-start.8
  147.1 3.1 %copy-start.6 = (bf16[512,512]{1,0:T(8,128)(2,1)S(1)}, bf16[512,512]{1,0:T(8,128)(2,1)}, u32[]{:S(2)}) copy-start(bf16[512,512]{1,0:T(8,128)(2,1)} %param.18) | copy-start | bytes 1572868
  150.5 4.1 %collective-permute-start.2 = (bf16[1,6,12,512]{3,2,1,0:T(8,128)(2,1)S(1)}, bf16[1,6,12,512]{3,2,1,0:T(8,128)(2,1)S(1)}, u32[]{:S(2)}, u32[]{:S(2)}) collective-permute-start(bf16[1,6,12,512]{3,2,1,0:T(8,128)(2,1)S(1)} %get-tuple-element.17), channel_id=1, source_target_pairs={{24,0},{0,8},{8,16},{16,24},{25,1},{1,9},{9,17},{17,25},{26,2},{2,... | collective-permute-start | bytes 221192 | tf_op jit(solution)/shard_map/ppermute | solution.py:15
  154.6 7.8 %collective-permute-start.3 = (bf16[1,12,6,512]{3,2,1,0:T(8,128)(2,1)S(1)}, bf16[1,12,6,512]{3,2,1,0:T(8,128)(2,1)S(1)}, u32[]{:S(2)}, u32[]{:S(2)}) collective-permute-start(bf16[1,12,6,512]{3,2,1,0:T(8,128)(2,1)S(1)} %fusion.15), channel_id=1, source_target_pairs={{7,0},{0,1},{1,2},{2,3},{3,4},{4,5},{5,6},{6,7},{15,8},{8,9},{9,10... | collective-permute-start | bytes 221192 | tf_op jit(solution)/shard_map/ppermute | solution.py:15
where the time goes:
time: 164 us; the launch traced here: 163 us
  local copies, waits for them, and re-layouts  114 us (70%)
  matrix products  16.7 us (10%)
  waiting for transfers between devices  14.1 us (9%)
  other arithmetic  11.1 us (7%)
  starting transfers between devices  7.05 us (4%)
    gather x2, local copies, waits for them, and re-layouts, shards(): bias_two = jnp.take(bias_second[0], rel, axis=1)  50.9 us
    gather x2, local copies, waits for them, and re-layouts, shards(): bias_one = jnp.take(bias_first[0], rel, axis=1)  50.9 us
    ppermute x4, waiting for transfers between devices, shifted(): return lax.ppermute(block, axis, route)  14.1 us
    dot_general x2, matrix products, attend_split(): jnp.einsum('wqhd,wkhd->whqk', query, keys, precision=lax.Precision.HIGHEST)  8.36 us
    ppermute x4, starting transfers between devices, shifted(): return lax.ppermute(block, axis, route)  7.05 us
    dot_general x2, matrix products, attend_split(): jnp.einsum('whqk,wkhd->wqhd', weights, values, preferred_element_type=jnp...  6.21 us
    reduce_sum x2, other arithmetic, norm_rows(): mean = jnp.mean(data, axis=-1, keepdims=True)  4.62 us
    unnamed x26, local copies, waits for them, and re-layouts  4.03 us
  transfers between devices with their start and end apart: 4, of which 3 were waited for; matrix products, arithmetic and copies ran while one was open for 31% of the time, Pallas kernels for 0%

commit v1 on v0

v1 whole, which is shorter than its diff:
```python
import functools

import jax
import jax.numpy as jnp
from jax import lax
from jax.experimental import pallas as pl
from jax.experimental.pallas import tpu as pltpu
from jax.sharding import PartitionSpec as P

HEADS = 16
WH = 12
WW = 12
LANES = 128
SUB = 8
PITCH = 16
KEYS = 256
SPAN_R = 2 * WH - 1
SPAN_C = 2 * WW - 1
HALF_R = WH // 2
HALF_C = WW // 2
REST = WW - SUB
NEG = -1e30
F32 = jnp.float32
BF16 = jnp.bfloat16


def iota(shape, dim):
    return lax.broadcasted_iota(jnp.int32, shape, dim)


def bias_strips(table, tab, strips):
    heads = table.shape[1]
    count = table.shape[2]
    tab[...] = jnp.zeros_like(tab)
    tab[:, :count] = table[0]
    lane = iota((SUB, LANES), 1)
    row = iota((SUB, LANES), 0)
    plans = []
    for tile in range(2):
        for k in range(3):
            u = lane + k * LANES
            j = u // PITCH
            key_col = u % PITCH
            if tile == 0:
                col = row
                step = j
            else:
                second = row >= REST
                col = SUB + jnp.where(second, row - REST, row)
                step = jnp.where(second, j - 1, j)
            good = (key_col < WW) & (step >= 0) & (step < SPAN_R)
            index = (SPAN_R - 1 - step) * SPAN_C + col - key_col + WW - 1
            index = jnp.where(good, index, 0)
            top = (SPAN_R - 1 - max(8 * k - tile, 0)) * SPAN_C + SPAN_C - 1
            low = max(SPAN_R - 1 - (8 * k + 7), 0) * SPAN_C
            sources = range(low // LANES, top // LANES + 1)
            plans.append((tile, k, index % LANES, index // LANES, good, sources))
    for h in range(heads):
        rows = {}
        for tile, k, inner, outer, good, sources in plans:
            value = jnp.full((SUB, LANES), NEG, F32)
            for s in sources:
                if s not in rows:
                    rows[s] = jnp.broadcast_to(tab[h : h + 1, s * LANES : (s + 1) * LANES], (SUB, LANES))
                taken = jnp.take_along_axis(rows[s], inner, axis=1)
                value = jnp.where(good & (outer == s), taken, value)
            strips[h, tile, :, k * LANES : (k + 1) * LANES] = value


def head_bias(strips, h):
    turned = {}
    lane = iota((SUB, LANES), 1)

    def turn(tile, k, by):
        key = (tile, k, by)
        if key not in turned:
            part = strips[h, tile, :, k * LANES : (k + 1) * LANES]
            turned[key] = pltpu.roll(part, LANES - by, 1) if by else part
        return turned[key]

    def window(tile, start):
        first, by = divmod(start, LANES)
        out = []
        for k in (first, first + 1):
            left = turn(tile, k % 3, by)
            out.append(jnp.where(lane < LANES - by, left, turn(tile, (k + 1) % 3, by)) if by else left)
        return out

    tiles = [window(0, PITCH * (WH - 1 - r)) for r in range(WH)]
    tiles += [window(1, PITCH * (WH - 1 - r)) for r in range(0, WH, 2)]
    return tiles


def masks(polar):
    lane = iota((SUB, LANES), 1)
    row = iota((SUB, LANES), 0)
    out = []
    for t in range(WH + WH // 2):
        if t < WH:
            r = jnp.full((SUB, LANES), t, jnp.int32)
        else:
            r = 2 * (t - WH) + jnp.where(row >= REST, 1, 0)
        pair = []
        for k in range(2):
            key_row = (lane + k * LANES) // PITCH
            bad = key_row >= WH
            if polar is not None:
                bad = bad | (((r >= HALF_R) != (key_row >= HALF_R)) & polar)
            pair.append(jnp.where(bad, NEG, 0.0).astype(F32))
        out.append(pair)
    return out


def compact(value):
    width = value.shape[-1]
    tiles = value.reshape(WH, 2, SUB, width)
    row = iota((SUB, width), 0)
    parts = [tiles[r, 0] for r in range(WH)]
    for r in range(0, WH, 2):
        parts.append(jnp.where(row < REST, tiles[r, 1], pltpu.roll(tiles[r + 1, 1], REST, 0)))
    return jnp.concatenate(parts, axis=0)


def attend(xs, ys, table, gain, wqkv, wproj, tab, strips, probs, polar):
    width = xs.shape[-1]
    heads = HEADS
    head_dim = width // heads
    group = LANES // head_dim
    tokens = WH * WW
    x = xs[...].reshape(WH * PITCH, width)
    mean = jnp.mean(x, axis=-1, keepdims=True)
    centred = x - mean
    var = jnp.mean(centred * centred, axis=-1, keepdims=True)
    normed = (centred * lax.rsqrt(var + 1e-05) * gain[...]).astype(BF16)
    bias_strips(table, tab, strips)
    mixed = jnp.dot(normed, wqkv[...], preferred_element_type=F32)
    query = compact(mixed[:, :width]) * head_dim ** (-0.5)
    keys = mixed[:, width : 2 * width]
    pad = jnp.zeros((KEYS - WH * PITCH, width), BF16)
    values = jnp.concatenate([mixed[:, 2 * width :].astype(BF16), pad], axis=0)
    q_hi = query.astype(BF16)
    q_lo = (query - q_hi.astype(F32)).astype(BF16)
    k_hi = keys.astype(BF16)
    k_lo = (keys - k_hi.astype(F32)).astype(BF16)
    k_hi = jnp.concatenate([k_hi, pad], axis=0)
    k_lo = jnp.concatenate([k_lo, pad], axis=0)
    lane = iota((1, LANES), 1)
    extra = masks(polar)
    outs = []
    for g in range(heads // group):
        part = slice(g * LANES, (g + 1) * LANES)
        left = jnp.concatenate([q_hi[:, part], q_lo[:, part], q_hi[:, part]], axis=1)
        rights = []
        for i in range(group):
            own = (lane // head_dim == i).astype(BF16)
            kh = k_hi[:, part] * own
            kl = k_lo[:, part] * own
            right = jnp.concatenate([kh, kh, kl], axis=1)
            scores = lax.dot_general(left, right, (((1,), (1,)), ((), ())), preferred_element_type=F32)
            tiles = head_bias(strips, g * group + i)
            for t in range(0, len(tiles), 2):
                pair = []
                for u in (t, t + 1):
                    rows = slice(u * SUB, (u + 1) * SUB)
                    s0 = scores[rows, :LANES] + tiles[u][0]
                    s1 = scores[rows, LANES:] + tiles[u][1] + extra[u][1]
                    if polar is not None:
                        s0 = s0 + extra[u][0]
                    top = jnp.max(jnp.maximum(s0, s1), axis=-1, keepdims=True)
                    e0 = jnp.exp(s0 - top)
                    e1 = jnp.exp(s1 - top)
                    total = jnp.sum(e0 + e1, axis=-1, keepdims=True)
                    inverse = 1.0 / total
                    pair.append(jnp.concatenate([e0 * inverse, e1 * inverse], axis=1))
                probs[t * SUB : (t + 2) * SUB, i * KEYS : (i + 1) * KEYS] = jnp.concatenate(pair, axis=0).astype(BF16)
            rights.append(values[:, part] * own)
        outs.append(jnp.dot(probs[...], jnp.concatenate(rights, axis=0), preferred_element_type=F32))
    heads_out = jnp.concatenate(outs, axis=1).astype(BF16)
    branch = jnp.dot(heads_out, wproj[...], preferred_element_type=F32)
    for r in range(WH):
        ys[r, :SUB, :] = xs[r, :SUB, :] + branch[r * SUB : (r + 1) * SUB]
        at = WH * SUB + r * REST
        ys[r, SUB:WW, :] = xs[r, SUB:WW, :] + branch[at : at + REST]


def quadrants(ys, outs):
    at = 0
    for r in (0, HALF_R):
        for c in (0, HALF_C):
            outs[at][...] = ys[r : r + HALF_R, c : c + HALF_C, :].astype(BF16)
            at += 1


def first_kernel(tokens, table, gain, wqkv, wproj, nw, ne, sw, se, xs, ys, tab, strips, probs):
    xs[:, WW:, :] = jnp.zeros((WH, PITCH - WW, xs.shape[-1]), F32)
    xs[:, :WW, :] = tokens[0].astype(F32)
    attend(xs, ys, table, gain, wqkv, wproj, tab, strips, probs, None)
    quadrants(ys, (nw, ne, sw, se))


def second_kernel(nw_in, ne_in, sw_in, se_in, table, gain, wqkv, wproj, nw, ne, sw, se, xs, ys, tab, strips, probs):
    polar = lax.axis_index("lat") == lax.axis_size("lat") - 1
    xs[:, WW:, :] = jnp.zeros((WH, PITCH - WW, xs.shape[-1]), F32)
    at = 0
    pieces = (nw_in, ne_in, sw_in, se_in)
    for r in (0, HALF_R):
        for c in (0, HALF_C):
            xs[r : r + HALF_R, c : c + HALF_C, :] = pieces[at][...].astype(F32)
            at += 1
    attend(xs, ys, table, gain, wqkv, wproj, tab, strips, probs, polar)
    quadrants(ys, (nw, ne, sw, se))


def block(kernel, pieces, table, gain, wqkv, wproj):
    width = wproj.shape[0]
    heads, count = table.shape[1:]
    lanes = -(-count // LANES) * LANES
    piece = jax.ShapeDtypeStruct((HALF_R, HALF_C, width), BF16)
    args = (*pieces, table, gain.reshape(1, width), wqkv, wproj)
    vmem = pl.BlockSpec(memory_space=pltpu.VMEM)
    return pl.pallas_call(
        kernel,
        out_shape=(piece,) * 4,
        in_specs=[vmem] * len(args),
        out_specs=(vmem,) * 4,
        scratch_shapes=[
            pltpu.VMEM((WH, PITCH, width), F32),
            pltpu.VMEM((WH, PITCH, width), F32),
            pltpu.VMEM((heads, lanes), F32),
            pltpu.VMEM((heads, 2, SUB, 3 * LANES), F32),
            pltpu.VMEM((WH * WW, LANES // (width // heads) * KEYS), BF16),
        ],
        compiler_params=pltpu.CompilerParams(vmem_limit_bytes=24 << 20),
        cost_estimate=pl.CostEstimate(flops=400_000_000, bytes_accessed=2_500_000, transcendentals=600_000),
    )(*args)


def moved(piece, lat, lon):
    rows, cols = lax.axis_size("lat"), lax.axis_size("lon")
    route = [
        (((i + lat) % rows) * cols + (j + lon) % cols, i * cols + j) for i in range(rows) for j in range(cols)
    ]
    return lax.ppermute(piece, ("lat", "lon"), route)


def shards(
    tokens,
    gain_first,
    qkv_first,
    proj_first,
    bias_first,
    gain_second,
    qkv_second,
    proj_second,
    bias_second,
):
    nw, ne, sw, se = block(first_kernel, (tokens,), bias_first, gain_first, qkv_first, proj_first)
    window = (se, moved(sw, 0, 1), moved(ne, 1, 0), moved(nw, 1, 1))
    nw, ne, sw, se = block(second_kernel, window, bias_second, gain_second, qkv_second, proj_second)
    west, north, corner = moved(ne, 0, -1), moved(sw, -1, 0), moved(se, -1, -1)
    upper = jnp.concatenate([corner, north], axis=1)
    lower = jnp.concatenate([west, nw], axis=1)
    return jnp.concatenate([upper, lower], axis=0)[None]


def solution(mesh):
    placed = (
        P(None, "lat", "lon", None),
        P(),
        P(),
        P(),
        P("lat", None, None),
        P(),
        P(),
        P(),
        P("lat", None, None),
    )
    return jax.shard_map(
        shards, mesh=mesh, in_specs=placed, out_specs=P(None, "lat", "lon", None), check_vma=False
    )
```

time: 164 us -> 32.2 us (0.20)
  local copies, waits for them, and re-layouts: 114 us -> 4.85 us
  matrix products: 16.7 us -> 0 us
  other arithmetic: 11.1 us -> 0.75 us
  Pallas kernels: 0 us -> 7.73 us
  waiting for transfers between devices: 14.1 us -> 10.1 us
    gather x4 -> x0, local copies, waits for them, and re-layouts: 102 us -> none  [the longest x2 50.9 us: shards(): bias_two = jnp.take(bias_second[0], rel, axis=1)]
    dot_general x8 -> x0, matrix products: 16.7 us -> none  [the longest x2 8.36 us: attend_split(): jnp.einsum('wqhd,wkhd->whqk', query, keys, precision=lax.Precision.HIGHEST)]
    reduce_sum x4 -> x0, other arithmetic: 7.73 us -> none  [the longest x2 4.62 us: norm_rows(): mean = jnp.mean(data, axis=-1, keepdims=True)]
    pallas_call x0 -> x2, Pallas kernels: none -> 7.73 us  [block(): pl.pallas_call(kernel, out_shape=(piece,) * 4, in_specs=[vmem] * len(args...]
    slice x12 -> x0, local copies, waits for them, and re-layouts: 4.61 us -> none  [the longest x4 2.16 us: attend_tokens(): keys = mixed[..., width:2 * width]]
    ppermute x4 -> x6, waiting for transfers between devices: 14.1 us -> 10.1 us  [moved(): return lax.ppermute(piece, ('lat', 'lon'), route)]
    convert_element_type x3 -> x0, local copies, waits for them, and re-layouts: 3.07 us -> none  [the longest x2 2.04 us: shards(): wins.astype(jnp.float32)]
    concatenate x3 -> x0, other arithmetic: 1.91 us -> none  [the longest x1 1.11 us: shards(): shifted_cols = jnp.concatenate([first[:, :, half_cols:], east], axis=2)]
  transfers between devices with their start and end apart: 4 -> 6, of which waited for: 3 -> 5; matrix products, arithmetic and copies ran while one was open for 31% -> 0% of each run, Pallas kernels for 0% -> 0%
where the time goes in v1:
time: 32.2 us; the launch traced here: 32 us
  waiting for transfers between devices  10.1 us (31%)
  starting transfers between devices  8.5 us (26%)
  Pallas kernels  7.73 us (24%)
  local copies, waits for them, and re-layouts  4.85 us (15%)
  other arithmetic  0.75 us (2%)
    ppermute x6, waiting for transfers between devices, moved(): return lax.ppermute(piece, ('lat', 'lon'), route)  10.1 us
    ppermute x6, starting transfers between devices, moved(): return lax.ppermute(piece, ('lat', 'lon'), route)  8.5 us
    pallas_call x2, Pallas kernels, block(): pl.pallas_call(kernel, out_shape=(piece,) * 4, in_specs=[vmem] * len(args...  7.73 us
    unnamed x18, local copies, waits for them, and re-layouts  4.85 us
    broadcast_in_dim x1, other arithmetic, shards(): return jnp.concatenate([upper, lower], axis=0)[None]  0.75 us
  transfers between devices with their start and end apart: 6, of which 5 were waited for; matrix products, arithmetic and copies ran while one was open for 0% of the time, Pallas kernels for 0%

profile of v1, /device:TPU:0, one launch (start us, length us, event | category | flops | bytes accessed | tf_op | source)
XLA Modules:
  0.0 32.0 jit_solution(15959588009488345337)
XLA Ops:
  0.0 0.0 copy-start
  0.0 1.4 %copy-done = bf16[512,1536]{1,0:T(8,128)(2,1)S(1)} copy-done((bf16[512,1536]{1,0:T(8,128)(2,1)S(1)}, bf16[512,1536]{1,0:T(8,128)(2,1)}, u32[]{:S(2)}) %copy-start) | copy-done | bytes 1572888
  1.4 0.0 copy-start.2
  1.4 1.0 %copy-done.2 = bf16[512,512]{1,0:T(8,128)(2,1)S(1)} copy-done((bf16[512,512]{1,0:T(8,128)(2,1)S(1)}, bf16[512,512]{1,0:T(8,128)(2,1)}, u32[]{:S(2)}) %copy-start.2) | copy-done | bytes 524312
  2.5 0.0 copy-start.4
  2.5 0.9 %copy-done.4 = bf16[1,12,12,512]{3,2,1,0:T(8,128)(2,1)S(1)} copy-done((bf16[1,12,12,512]{3,2,1,0:T(8,128)(2,1)S(1)}, bf16[1,12,12,512]{3,2,1,0:T(8,128)(2,1)}, u32[]{:S(2)}) %copy-start.4) | copy-done | bytes 147480
  3.4 0.0 copy-start.5
  3.4 0.8 %copy-done.5 = f32[1,16,529]{2,1,0:T(8,128)S(1)} copy-done((f32[1,16,529]{2,1,0:T(8,128)S(1)}, f32[1,16,529]{2,1,0:T(8,128)}, u32[]{:S(2)}) %copy-start.5) | copy-done | bytes 33880
  4.2 0.0 copy-start.7
  4.2 0.7 %copy-done.7 = f32[512]{0:T(512)S(1)} copy-done((f32[512]{0:T(512)S(1)}, f32[512]{0:T(512)}, u32[]{:S(2)}) %copy-start.7) | copy-done | bytes 2072
  4.8 0.0 copy-start.1
  4.8 0.0 copy-start.3
  4.8 0.0 copy-start.6
  4.8 0.0 copy-start.8
  4.9 3.9 %shard_map.91 = (bf16[6,6,512]{2,1,0:T(8,128)(2,1)S(1)}, bf16[6,6,512]{2,1,0:T(8,128)(2,1)S(1)}, bf16[6,6,512]{2,1,0:T(8,128)(2,1)S(1)}, bf16[6,6,512]{2,1,0:T(8,128)(2,1)S(1)}) custom-call(bf16[1,12,12,512]{3,2,1,0:T(8,128)(2,1)S(1)} %copy-done.4, f32[1,16,529]{2,1,0:T(8,128)S(1)} %copy-done.5, f32[1,512]{1,0:T(1,128)S(1)} %bitcast.4, ...), custom_call_target="tpu_custom_call" | custom-call | flops 400000000 | bytes 2500000 | tf_op jit(solution)/shard_map/pallas_call | solution.py:221
  8.7 6.1 %collective-permute-start = (bf16[6,6,512]{2,1,0:T(8,128)(2,1)S(1)}, bf16[6,6,512]{2,1,0:T(8,128)(2,1)S(1)}, u32[]{:S(2)}, u32[]{:S(2)}) collective-permute-start(bf16[6,6,512]{2,1,0:T(8,128)(2,1)S(1)} %get-tuple-element.14), channel_id=1, source_target_pairs={{1,0},{2,1},{3,2},{4,3},{5,4},{6,5},{7,6},{0,7},{9,8},{10,9},{11,1... | collective-permute-start | bytes 110600 | tf_op jit(solution)/shard_map/ppermute | solution.py:243
  14.8 0.7 %collective-permute-start.1 = (bf16[6,6,512]{2,1,0:T(8,128)(2,1)S(1)}, bf16[6,6,512]{2,1,0:T(8,128)(2,1)S(1)}, u32[]{:S(2)}, u32[]{:S(2)}) collective-permute-start(bf16[6,6,512]{2,1,0:T(8,128)(2,1)S(1)} %get-tuple-element.15), channel_id=1, source_target_pairs={{8,0},{9,1},{10,2},{11,3},{12,4},{13,5},{14,6},{15,7},{16,8},{17,9... | collective-permute-start | bytes 110600 | tf_op jit(solution)/shard_map/ppermute | solution.py:243
  15.5 0.9 %collective-permute-start.2 = (bf16[6,6,512]{2,1,0:T(8,128)(2,1)S(1)}, bf16[6,6,512]{2,1,0:T(8,128)(2,1)S(1)}, u32[]{:S(2)}, u32[]{:S(2)}) collective-permute-start(bf16[6,6,512]{2,1,0:T(8,128)(2,1)S(1)} %get-tuple-element.16), channel_id=1, source_target_pairs={{9,0},{10,1},{11,2},{12,3},{13,4},{14,5},{15,6},{8,7},{17,8},{18,9... | collective-permute-start | bytes 110600 | tf_op jit(solution)/shard_map/ppermute | solution.py:243
  16.4 0.2 collective-permute-done.ne_in
  16.6 0.7 %collective-permute-done.1.sw_in = bf16[6,6,512]{2,1,0:T(8,128)(2,1)S(1)} collective-permute-done((bf16[6,6,512]{2,1,0:T(8,128)(2,1)S(1)}, bf16[6,6,512]{2,1,0:T(8,128)(2,1)S(1)}, u32[]{:S(2)}, u32[]{:S(2)}) %collective-permute-start.1) | collective-permute-done | bytes 36896 | tf_op jit(solution)/shard_map/ppermute | solution.py:243
  17.2 1.8 %collective-permute-done.2.se_in = bf16[6,6,512]{2,1,0:T(8,128)(2,1)S(1)} collective-permute-done((bf16[6,6,512]{2,1,0:T(8,128)(2,1)S(1)}, bf16[6,6,512]{2,1,0:T(8,128)(2,1)S(1)}, u32[]{:S(2)}, u32[]{:S(2)}) %collective-permute-start.2) | collective-permute-done | bytes 36896 | tf_op jit(solution)/shard_map/ppermute | solution.py:243
  19.0 0.0 copy-done.1
  19.0 0.0 copy-done.3
  19.0 0.0 copy-done.6
  19.0 0.0 copy-done.8
  19.0 3.8 %shard_map.92 = (bf16[6,6,512]{2,1,0:T(8,128)(2,1)S(1)}, bf16[6,6,512]{2,1,0:T(8,128)(2,1)S(1)}, bf16[6,6,512]{2,1,0:T(8,128)(2,1)S(1)}, bf16[6,6,512]{2,1,0:T(8,128)(2,1)S(1)}) custom-call(bf16[6,6,512]{2,1,0:T(8,128)(2,1)S(1)} %get-tuple-element.13.nw_in, bf16[6,6,512]{2,1,0:T(8,128)(2,1)S(1)} %collective-permute-done.ne_in, ...), custom_call_target="tpu_custom_call" | custom-call | flops 400000000 | bytes 2500000 | tf_op jit(solution)/shard_map/pallas_call | solution.py:221
  22.9 0.1 collective-permute-start.3
  22.9 0.8 %collective-permute-start.4 = (bf16[6,6,512]{2,1,0:T(8,128)(2,1)S(1)}, bf16[6,6,512]{2,1,0:T(8,128)(2,1)S(1)}, u32[]{:S(2)}, u32[]{:S(2)}) collective-permute-start(bf16[6,6,512]{2,1,0:T(8,128)(2,1)S(1)} %get-tuple-element.18), channel_id=1, source_target_pairs={{24,0},{25,1},{26,2},{27,3},{28,4},{29,5},{30,6},{31,7},{0,8},{1,9... | collective-permute-start | bytes 110600 | tf_op jit(solution)/shard_map/ppermute | solution.py:243
  23.7 0.0 collective-permute-start.5
  23.7 6.8 %collective-permute-done.3 = bf16[6,6,512]{2,1,0:T(8,128)(2,1)S(1)} collective-permute-done((bf16[6,6,512]{2,1,0:T(8,128)(2,1)S(1)}, bf16[6,6,512]{2,1,0:T(8,128)(2,1)S(1)}, u32[]{:S(2)}, u32[]{:S(2)}) %collective-permute-start.3) | collective-permute-done | bytes 36896 | tf_op jit(solution)/shard_map/ppermute | solution.py:243
  30.5 0.0 collective-permute-done.4
  30.5 0.7 %collective-permute-done.5 = bf16[6,6,512]{2,1,0:T(8,128)(2,1)S(1)} collective-permute-done((bf16[6,6,512]{2,1,0:T(8,128)(2,1)S(1)}, bf16[6,6,512]{2,1,0:T(8,128)(2,1)S(1)}, u32[]{:S(2)}, u32[]{:S(2)}) %collective-permute-start.5) | collective-permute-done | bytes 36896 | tf_op jit(solution)/shard_map/ppermute | solution.py:243
  31.2 0.7 %maximum_bitcast_fusion = bf16[1,12,12,512]{3,2,1,0:T(8,128)(2,1)} fusion(bf16[6,6,512]{2,1,0:T(8,128)(2,1)S(1)} %get-tuple-element.20, bf16[6,6,512]{2,1,0:T(8,128)(2,1)S(1)} %collective-permute-done.5, bf16[6,6,512]{2,1,0:T(8,128)(2,1)S(1)} %collective-permute-done.4, bf16[6,6,512]{2,1,0:T(8,128)(2,1)S(1)} %collective-permute-done.3), kind=kLoop, calls=%fused_computation | loop fusion | flops 589824 | bytes 294912 | tf_op jit(solution)/shard_map/broadcast_in_dim | solution.py:263
Async XLA Ops:
  0.0 1.4 %copy-start = (bf16[512,1536]{1,0:T(8,128)(2,1)S(1)}, bf16[512,1536]{1,0:T(8,128)(2,1)}, u32[]{:S(2)}) copy-start(bf16[512,1536]{1,0:T(8,128)(2,1)} %wqkv.2) | copy-start | bytes 4718596
  1.4 1.0 %copy-start.2 = (bf16[512,512]{1,0:T(8,128)(2,1)S(1)}, bf16[512,512]{1,0:T(8,128)(2,1)}, u32[]{:S(2)}) copy-start(bf16[512,512]{1,0:T(8,128)(2,1)} %wproj.2) | copy-start | bytes 1572868
  2.5 0.9 %copy-start.4 = (bf16[1,12,12,512]{3,2,1,0:T(8,128)(2,1)S(1)}, bf16[1,12,12,512]{3,2,1,0:T(8,128)(2,1)}, u32[]{:S(2)}) copy-start(bf16[1,12,12,512]{3,2,1,0:T(8,128)(2,1)} %tokens.1) | copy-start | bytes 442372
  3.4 0.8 %copy-start.5 = (f32[1,16,529]{2,1,0:T(8,128)S(1)}, f32[1,16,529]{2,1,0:T(8,128)}, u32[]{:S(2)}) copy-start(f32[1,16,529]{2,1,0:T(8,128)} %table.2) | copy-start | bytes 101572
  4.2 0.7 %copy-start.7 = (f32[512]{0:T(512)S(1)}, f32[512]{0:T(512)}, u32[]{:S(2)}) copy-start(f32[512]{0:T(512)} %param.10) | copy-start | bytes 6148
  4.8 14.2 %copy-start.1 = (bf16[512,1536]{1,0:T(8,128)(2,1)S(1)}, bf16[512,1536]{1,0:T(8,128)(2,1)}, u32[]{:S(2)}) copy-start(bf16[512,1536]{1,0:T(8,128)(2,1)} %wqkv.3) | copy-start | bytes 4718596
  4.8 14.2 %copy-start.3 = (bf16[512,512]{1,0:T(8,128)(2,1)S(1)}, bf16[512,512]{1,0:T(8,128)(2,1)}, u32[]{:S(2)}) copy-start(bf16[512,512]{1,0:T(8,128)(2,1)} %wproj.3) | copy-start | bytes 1572868
  4.8 14.2 %copy-start.6 = (f32[1,16,529]{2,1,0:T(8,128)S(1)}, f32[1,16,529]{2,1,0:T(8,128)}, u32[]{:S(2)}) copy-start(f32[1,16,529]{2,1,0:T(8,128)} %table.3) | copy-start | bytes 101572
  4.8 14.2 %copy-start.8 = (f32[512]{0:T(512)S(1)}, f32[512]{0:T(512)}, u32[]{:S(2)}) copy-start(f32[512]{0:T(512)} %param.14) | copy-start | bytes 6148
  8.7 7.8 %collective-permute-start = (bf16[6,6,512]{2,1,0:T(8,128)(2,1)S(1)}, bf16[6,6,512]{2,1,0:T(8,128)(2,1)S(1)}, u32[]{:S(2)}, u32[]{:S(2)}) collective-permute-start(bf16[6,6,512]{2,1,0:T(8,128)(2,1)S(1)} %get-tuple-element.14), channel_id=1, source_target_pairs={{1,0},{2,1},{3,2},{4,3},{5,4},{6,5},{7,6},{0,7},{9,8},{10,9},{11,1... | collective-permute-start | bytes 110600 | tf_op jit(solution)/shard_map/ppermute | solution.py:243
  14.8 2.4 %collective-permute-start.1 = (bf16[6,6,512]{2,1,0:T(8,128)(2,1)S(1)}, bf16[6,6,512]{2,1,0:T(8,128)(2,1)S(1)}, u32[]{:S(2)}, u32[]{:S(2)}) collective-permute-start(bf16[6,6,512]{2,1,0:T(8,128)(2,1)S(1)} %get-tuple-element.15), channel_id=1, source_target_pairs={{8,0},{9,1},{10,2},{11,3},{12,4},{13,5},{14,6},{15,7},{16,8},{17,9... | collective-permute-start | bytes 110600 | tf_op jit(solution)/shard_map/ppermute | solution.py:243
  15.5 3.5 %collective-permute-start.2 = (bf16[6,6,512]{2,1,0:T(8,128)(2,1)S(1)}, bf16[6,6,512]{2,1,0:T(8,128)(2,1)S(1)}, u32[]{:S(2)}, u32[]{:S(2)}) collective-permute-start(bf16[6,6,512]{2,1,0:T(8,128)(2,1)S(1)} %get-tuple-element.16), channel_id=1, source_target_pairs={{9,0},{10,1},{11,2},{12,3},{13,4},{14,5},{15,6},{8,7},{17,8},{18,9... | collective-permute-start | bytes 110600 | tf_op jit(solution)/shard_map/ppermute | solution.py:243
  22.9 7.7 %collective-permute-start.3 = (bf16[6,6,512]{2,1,0:T(8,128)(2,1)S(1)}, bf16[6,6,512]{2,1,0:T(8,128)(2,1)S(1)}, u32[]{:S(2)}, u32[]{:S(2)}) collective-permute-start(bf16[6,6,512]{2,1,0:T(8,128)(2,1)S(1)} %get-tuple-element.17), channel_id=1, source_target_pairs={{31,0},{24,1},{25,2},{26,3},{27,4},{28,5},{29,6},{30,7},{7,8},{0,9... | collective-permute-start | bytes 110600 | tf_op jit(solution)/shard_map/ppermute | solution.py:243
  22.9 7.6 %collective-permute-start.4 = (bf16[6,6,512]{2,1,0:T(8,128)(2,1)S(1)}, bf16[6,6,512]{2,1,0:T(8,128)(2,1)S(1)}, u32[]{:S(2)}, u32[]{:S(2)}) collective-permute-start(bf16[6,6,512]{2,1,0:T(8,128)(2,1)S(1)} %get-tuple-element.18), channel_id=1, source_target_pairs={{24,0},{25,1},{26,2},{27,3},{28,4},{29,5},{30,6},{31,7},{0,8},{1,9... | collective-permute-start | bytes 110600 | tf_op jit(solution)/shard_map/ppermute | solution.py:243
  23.7 7.5 %collective-permute-start.5 = (bf16[6,6,512]{2,1,0:T(8,128)(2,1)S(1)}, bf16[6,6,512]{2,1,0:T(8,128)(2,1)S(1)}, u32[]{:S(2)}, u32[]{:S(2)}) collective-permute-start(bf16[6,6,512]{2,1,0:T(8,128)(2,1)S(1)} %get-tuple-element.19), channel_id=1, source_target_pairs={{7,0},{0,1},{1,2},{2,3},{3,4},{4,5},{5,6},{6,7},{15,8},{8,9},{9,10... | collective-permute-start | bytes 110600 | tf_op jit(solution)/shard_map/ppermute | solution.py:243

commit v2 on v1

v2 whole, which is shorter than its diff:
```python
import functools

import jax
import jax.numpy as jnp
from jax import lax
from jax.experimental import pallas as pl
from jax.experimental.pallas import tpu as pltpu
from jax.sharding import PartitionSpec as P

HEADS = 16
WH = 12
WW = 12
LANES = 128
SUB = 8
PITCH = 16
SPAN_C = 2 * WW - 1
HALF_R = WH // 2
HALF_C = WW // 2
REST = WW - SUB
NEG = -1e30
F32 = jnp.float32
BF16 = jnp.bfloat16


def iota(shape, dim):
    return lax.broadcasted_iota(jnp.int32, shape, dim)


def bias_strips(table, tab, strips):
    heads = table.shape[1]
    count = table.shape[2]
    tab[...] = jnp.zeros_like(tab)
    tab[:, :count] = table[0]
    lane = iota((SUB, LANES), 1)
    row = iota((SUB, LANES), 0)
    plans = []
    for tile in range(2):
        for k in range(3):
            u = lane + k * LANES
            step = u // PITCH
            if tile == 0:
                col = row
            else:
                second = row >= REST
                col = SUB + jnp.where(second, row - REST, row)
                step = jnp.where(second, step - 1, step)
            index = step * SPAN_C + u % PITCH - col + WW - 1
            index = jnp.clip(index, 0, count - 1)
            low = max(8 * k - tile, 0) * SPAN_C
            top = min((8 * k + 7) * SPAN_C + PITCH + WW - 2, count - 1)
            sources = range(low // LANES, top // LANES + 1)
            plans.append((tile, k, index % LANES, index // LANES, sources))
    for h in range(heads):
        rows = {}
        for tile, k, inner, outer, sources in plans:
            value = None
            for s in sources:
                if s not in rows:
                    rows[s] = jnp.broadcast_to(tab[h : h + 1, s * LANES : (s + 1) * LANES], (SUB, LANES))
                taken = jnp.take_along_axis(rows[s], inner, axis=1)
                value = taken if value is None else jnp.where(outer == s, taken, value)
            strips[h, tile, :, k * LANES : (k + 1) * LANES] = value


def bias_tiles(strips, h):
    turned = {}
    lane = iota((SUB, LANES), 1)
    per_head = WH * PITCH

    def turn(head, tile, k, by):
        key = (head, tile, k, by)
        if key not in turned:
            part = strips[head, tile, :, k * LANES : (k + 1) * LANES]
            turned[key] = pltpu.roll(part, LANES - by, 1) if by else part
        return turned[key]

    def window(tile, start, t):
        cuts = []
        at = t * LANES
        while at < (t + 1) * LANES:
            which, query = divmod(at, per_head)
            u = start + query
            k = u // LANES
            end = min(at + (k + 1) * LANES - u, (which + 1) * per_head, (t + 1) * LANES)
            cuts.append((end - t * LANES, turn(h + which, tile, k, (u - at) % LANES)))
            at = end
        value = cuts[-1][1]
        for end, part in reversed(cuts[:-1]):
            value = jnp.where(lane < end, part, value)
        return value

    starts = [(0, PITCH * (WH - 1 - r)) for r in range(WH)]
    starts += [(1, PITCH * (WH - 1 - r)) for r in range(0, WH, 2)]
    return [[window(tile, start, t) for tile, start in starts] for t in range(2 * per_head // LANES)]


def halves(polar):
    lane = iota((SUB, LANES), 1)
    out = []
    for t in range(2 * WH * PITCH // LANES):
        query = (lane + t * LANES) % (WH * PITCH) // PITCH >= HALF_R
        out.append([jnp.where((query != lower) & polar, NEG, 0.0).astype(F32) for lower in (False, True)])
    return out


def compact(value):
    width = value.shape[-1]
    tiles = value.reshape(WH, 2, SUB, width)
    row = iota((SUB, width), 0)
    parts = [tiles[r, 0] for r in range(WH)]
    for r in range(0, WH, 2):
        parts.append(jnp.where(row < REST, tiles[r, 1], pltpu.roll(tiles[r + 1, 1], REST, 0)))
    return jnp.concatenate(parts, axis=0)


def split(value):
    high = value.astype(BF16)
    return high, (value - high.astype(F32)).astype(BF16)


def soft(scores, bias, mask, probs, at):
    count = len(bias)
    tiles = []
    for u in range(count):
        s = scores[u * SUB : (u + 1) * SUB] + bias[u]
        if mask is not None:
            lower = u >= HALF_R if u < WH else 2 * (u - WH) >= HALF_R
            s = s + mask[int(lower)]
        tiles.append(s)
    top = functools.reduce(jnp.maximum, tiles)
    top = jnp.max(top, axis=0, keepdims=True)
    tiles = [jnp.exp(s - top) for s in tiles]
    total = functools.reduce(jnp.add, tiles)
    inverse = 1.0 / jnp.sum(total, axis=0, keepdims=True)
    for u in range(0, count, 2):
        pair = jnp.concatenate([tiles[u] * inverse, tiles[u + 1] * inverse], axis=0)
        probs[u * SUB : (u + 2) * SUB, at : at + LANES] = pair.astype(BF16)


def attend(xs, ys, gain, weights, strips, probs, polar):
    width = xs.shape[-1]
    head_dim = width // HEADS
    group = LANES // head_dim
    per_head = WH * PITCH
    x = xs[...].reshape(per_head, width)
    mean = jnp.mean(x, axis=-1, keepdims=True)
    centred = x - mean
    var = jnp.mean(centred * centred, axis=-1, keepdims=True)
    normed = (centred * lax.rsqrt(var + 1e-05) * gain[...]).astype(BF16)
    wqkv = weights(0)
    mixed = jnp.dot(normed, wqkv[...], preferred_element_type=F32)
    q_hi, q_lo = split(mixed[:, :width] * head_dim ** (-0.5))
    k_hi, k_lo = split(compact(mixed[:, width : 2 * width]))
    values = compact(mixed[:, 2 * width :]).astype(BF16)
    lane = iota((1, LANES), 1)
    masks = None if polar is None else halves(polar)

    def product(g):
        part = slice(g * LANES, (g + 1) * LANES)
        left = jnp.concatenate([k_hi[:, part], k_hi[:, part], k_lo[:, part]], axis=1)
        rights = []
        for i in range(group):
            own = (lane // head_dim == i).astype(BF16)
            high = q_hi[:, part] * own
            rights.append(jnp.concatenate([high, q_lo[:, part] * own, high], axis=1))
        right = jnp.concatenate(rights, axis=0)
        return lax.dot_general(left, right, (((1,), (1,)), ((), ())), preferred_element_type=F32)

    outs = []
    groups = HEADS // group
    ahead = product(0)
    for g in range(groups):
        scores = ahead
        if g + 1 < groups:
            ahead = product(g + 1)
        for i in range(0, group, 2):
            bias = bias_tiles(strips, g * group + i)
            for t in range(len(bias)):
                at = i * per_head + t * LANES
                soft(scores[:, at : at + LANES], bias[t], masks and masks[t], probs.at[g], at)
        part = slice(g * LANES, (g + 1) * LANES)
        mixed_v = lax.dot_general(
            values[:, part], probs[g], (((0,), (0,)), ((), ())), preferred_element_type=F32
        )
        heads_out = []
        for i in range(group):
            rows = slice(i * head_dim, (i + 1) * head_dim)
            first, by = divmod(i * per_head, LANES)
            own = mixed_v[rows, first * LANES : (first + 2) * LANES]
            heads_out.append(pltpu.roll(own, 2 * LANES - by, 1) if by else own)
        outs.append(jnp.concatenate(heads_out, axis=0).T)
    heads_out = jnp.concatenate(outs, axis=1)[:per_head].astype(BF16)
    wproj = weights(1)
    branch = jnp.dot(heads_out, wproj[...], preferred_element_type=F32)
    ys[...] = xs[...] + branch.reshape(xs.shape)


def quadrants(ys, outs):
    at = 0
    for r in (0, HALF_R):
        for c in (0, HALF_C):
            outs[at][...] = ys[r : r + HALF_R, c : c + HALF_C, :].astype(BF16)
            at += 1


def first_kernel(tokens, table, gain, wqkv, wproj, nw, ne, sw, se, xs, ys, tab, strips, probs, *here):
    here, sems = here[:-1], here[-1]
    copies = [
        pltpu.make_async_copy(a, b, sems.at[i]) for i, (a, b) in enumerate(zip((table, tokens, gain, wqkv, wproj), here))
    ]
    for copy in copies:
        copy.start()
    xs[:, WW:, :] = jnp.zeros((WH, PITCH - WW, xs.shape[-1]), F32)
    copies[0].wait()
    bias_strips(here[0], tab, strips)
    copies[1].wait()
    xs[:, :WW, :] = here[1][0].astype(F32)
    copies[2].wait()

    def weights(i):
        copies[3 + i].wait()
        return here[3 + i]

    attend(xs, ys, here[2], weights, strips, probs, None)
    quadrants(ys, (nw, ne, sw, se))


def second_kernel(nw_in, ne_in, sw_in, se_in, table, gain, wqkv, wproj, nw, ne, sw, se, xs, ys, tab, strips, probs):
    polar = lax.axis_index("lat") == lax.axis_size("lat") - 1
    xs[:, WW:, :] = jnp.zeros((WH, PITCH - WW, xs.shape[-1]), F32)
    at = 0
    pieces = (nw_in, ne_in, sw_in, se_in)
    for r in (0, HALF_R):
        for c in (0, HALF_C):
            xs[r : r + HALF_R, c : c + HALF_C, :] = pieces[at][...].astype(F32)
            at += 1
    bias_strips(table, tab, strips)
    attend(xs, ys, gain, lambda i: (wqkv, wproj)[i], strips, probs, polar)
    quadrants(ys, (nw, ne, sw, se))


def block(kernel, pieces, table, gain, wqkv, wproj, fetch):
    width = wproj.shape[0]
    heads, count = table.shape[1:]
    lanes = -(-count // LANES) * LANES
    group = LANES * heads // width
    piece = jax.ShapeDtypeStruct((HALF_R, HALF_C, width), BF16)
    args = (*pieces, table, gain.reshape(1, width), wqkv, wproj)
    vmem = pl.BlockSpec(memory_space=pltpu.VMEM)
    scratch = [
        pltpu.VMEM((WH, PITCH, width), F32),
        pltpu.VMEM((WH, PITCH, width), F32),
        pltpu.VMEM((heads, lanes), F32),
        pltpu.VMEM((heads, 2, SUB, 3 * LANES), F32),
        pltpu.VMEM((heads // group, WH * WW, group * WH * PITCH), BF16),
    ]
    if fetch:
        order = (args[1], args[0], *args[2:])
        scratch += [pltpu.VMEM(a.shape, a.dtype) for a in order]
        scratch += [pltpu.SemaphoreType.DMA((len(order),))]
    source = pl.BlockSpec(memory_space=pltpu.HBM) if fetch else vmem
    return pl.pallas_call(
        kernel,
        out_shape=(piece,) * 4,
        in_specs=[source] * len(args),
        out_specs=(vmem,) * 4,
        scratch_shapes=scratch,
        compiler_params=pltpu.CompilerParams(vmem_limit_bytes=24 << 20),
        cost_estimate=pl.CostEstimate(flops=400_000_000, bytes_accessed=2_500_000, transcendentals=600_000),
    )(*args)


def moved(piece, lat, lon):
    rows, cols = lax.axis_size("lat"), lax.axis_size("lon")
    route = [
        (((i + lat) % rows) * cols + (j + lon) % cols, i * cols + j) for i in range(rows) for j in range(cols)
    ]
    return lax.ppermute(piece, ("lat", "lon"), route)


def shards(
    tokens,
    gain_first,
    qkv_first,
    proj_first,
    bias_first,
    gain_second,
    qkv_second,
    proj_second,
    bias_second,
):
    nw, ne, sw, se = block(first_kernel, (tokens,), bias_first, gain_first, qkv_first, proj_first, True)
    window = (se, moved(sw, 0, 1), moved(ne, 1, 0), moved(nw, 1, 1))
    nw, ne, sw, se = block(second_kernel, window, bias_second, gain_second, qkv_second, proj_second, False)
    west, north, corner = moved(ne, 0, -1), moved(sw, -1, 0), moved(se, -1, -1)
    upper = jnp.concatenate([corner, north], axis=1)
    lower = jnp.concatenate([west, nw], axis=1)
    return jnp.concatenate([upper, lower], axis=0)[None]


def solution(mesh):
    placed = (
        P(None, "lat", "lon", None),
        P(),
        P(),
        P(),
        P("lat", None, None),
        P(),
        P(),
        P(),
        P("lat", None, None),
    )
    return jax.shard_map(
        shards, mesh=mesh, in_specs=placed, out_specs=P(None, "lat", "lon", None), check_vma=False
    )
```

time: 32.2 us -> 30.4 us (0.944)
  Pallas kernels: 7.73 us -> 5.84 us
    pallas_call x2, Pallas kernels: 7.73 us -> 5.84 us  [block(): pl.pallas_call(kernel, out_shape=(piece,) * 4, in_specs=[source] * len(ar...]
where the time goes in v2:
time: 30.4 us; the launch traced here: 30.1 us
  waiting for transfers between devices  10.1 us (33%)
  starting transfers between devices  8.5 us (28%)
  Pallas kernels  5.84 us (19%)
  local copies, waits for them, and re-layouts  4.85 us (16%)
  other arithmetic  0.75 us (2%)
    ppermute x6, waiting for transfers between devices, moved(): return lax.ppermute(piece, ('lat', 'lon'), route)  10.1 us
    ppermute x6, starting transfers between devices, moved(): return lax.ppermute(piece, ('lat', 'lon'), route)  8.5 us
    pallas_call x2, Pallas kernels, block(): pl.pallas_call(kernel, out_shape=(piece,) * 4, in_specs=[source] * len(ar...  5.84 us
    unnamed x18, local copies, waits for them, and re-layouts  4.85 us
    broadcast_in_dim x1, other arithmetic, shards(): return jnp.concatenate([upper, lower], axis=0)[None]  0.75 us
  transfers between devices with their start and end apart: 6, of which 5 were waited for; matrix products, arithmetic and copies ran while one was open for 0% of the time, Pallas kernels for 0%

profile of v2, /device:TPU:0, one launch (start us, length us, event | category | flops | bytes accessed | tf_op | source)
XLA Modules:
  0.0 30.1 jit_solution(10986767096860548426)
XLA Ops:
  0.0 0.0 copy-start
  0.0 1.4 %copy-done = bf16[512,1536]{1,0:T(8,128)(2,1)S(1)} copy-done((bf16[512,1536]{1,0:T(8,128)(2,1)S(1)}, bf16[512,1536]{1,0:T(8,128)(2,1)}, u32[]{:S(2)}) %copy-start) | copy-done | bytes 1572888
  1.4 0.0 copy-start.2
  1.4 1.0 %copy-done.2 = bf16[512,512]{1,0:T(8,128)(2,1)S(1)} copy-done((bf16[512,512]{1,0:T(8,128)(2,1)S(1)}, bf16[512,512]{1,0:T(8,128)(2,1)}, u32[]{:S(2)}) %copy-start.2) | copy-done | bytes 524312
  2.5 0.0 copy-start.4
  2.5 0.9 %copy-done.4 = bf16[1,12,12,512]{3,2,1,0:T(8,128)(2,1)S(1)} copy-done((bf16[1,12,12,512]{3,2,1,0:T(8,128)(2,1)S(1)}, bf16[1,12,12,512]{3,2,1,0:T(8,128)(2,1)}, u32[]{:S(2)}) %copy-start.4) | copy-done | bytes 147480
  3.4 0.0 copy-start.5
  3.4 0.8 %copy-done.5 = f32[1,16,529]{2,1,0:T(8,128)S(1)} copy-done((f32[1,16,529]{2,1,0:T(8,128)S(1)}, f32[1,16,529]{2,1,0:T(8,128)}, u32[]{:S(2)}) %copy-start.5) | copy-done | bytes 33880
  4.2 0.0 copy-start.7
  4.2 0.7 %copy-done.7 = f32[512]{0:T(512)S(1)} copy-done((f32[512]{0:T(512)S(1)}, f32[512]{0:T(512)}, u32[]{:S(2)}) %copy-start.7) | copy-done | bytes 2072
  4.8 0.0 copy-start.1
  4.8 0.0 copy-start.3
  4.8 0.0 copy-start.6
  4.8 0.0 copy-start.8
  4.9 3.5 %shard_map.91 = (bf16[6,6,512]{2,1,0:T(8,128)(2,1)S(1)}, bf16[6,6,512]{2,1,0:T(8,128)(2,1)S(1)}, bf16[6,6,512]{2,1,0:T(8,128)(2,1)S(1)}, bf16[6,6,512]{2,1,0:T(8,128)(2,1)S(1)}) custom-call(bf16[1,12,12,512]{3,2,1,0:T(8,128)(2,1)S(1)} %copy-done.4, f32[1,16,529]{2,1,0:T(8,128)S(1)} %copy-done.5, f32[1,512]{1,0:T(1,128)S(1)} %bitcast.4, ...), custom_call_target="tpu_custom_call" | custom-call | flops 400000000 | bytes 2500000 | tf_op jit(solution)/shard_map/pallas_call | solution.py:262
  8.3 6.1 %collective-permute-start = (bf16[6,6,512]{2,1,0:T(8,128)(2,1)S(1)}, bf16[6,6,512]{2,1,0:T(8,128)(2,1)S(1)}, u32[]{:S(2)}, u32[]{:S(2)}) collective-permute-start(bf16[6,6,512]{2,1,0:T(8,128)(2,1)S(1)} %get-tuple-element.14), channel_id=1, source_target_pairs={{1,0},{2,1},{3,2},{4,3},{5,4},{6,5},{7,6},{0,7},{9,8},{10,9},{11,1... | collective-permute-start | bytes 110600 | tf_op jit(solution)/shard_map/ppermute | solution.py:278
  14.4 0.7 %collective-permute-start.1 = (bf16[6,6,512]{2,1,0:T(8,128)(2,1)S(1)}, bf16[6,6,512]{2,1,0:T(8,128)(2,1)S(1)}, u32[]{:S(2)}, u32[]{:S(2)}) collective-permute-start(bf16[6,6,512]{2,1,0:T(8,128)(2,1)S(1)} %get-tuple-element.15), channel_id=1, source_target_pairs={{8,0},{9,1},{10,2},{11,3},{12,4},{13,5},{14,6},{15,7},{16,8},{17,9... | collective-permute-start | bytes 110600 | tf_op jit(solution)/shard_map/ppermute | solution.py:278
  15.1 0.9 %collective-permute-start.2 = (bf16[6,6,512]{2,1,0:T(8,128)(2,1)S(1)}, bf16[6,6,512]{2,1,0:T(8,128)(2,1)S(1)}, u32[]{:S(2)}, u32[]{:S(2)}) collective-permute-start(bf16[6,6,512]{2,1,0:T(8,128)(2,1)S(1)} %get-tuple-element.16), channel_id=1, source_target_pairs={{9,0},{10,1},{11,2},{12,3},{13,4},{14,5},{15,6},{8,7},{17,8},{18,9... | collective-permute-start | bytes 110600 | tf_op jit(solution)/shard_map/ppermute | solution.py:278
  16.0 0.2 collective-permute-done.ne_in
  16.2 0.7 %collective-permute-done.1.sw_in = bf16[6,6,512]{2,1,0:T(8,128)(2,1)S(1)} collective-permute-done((bf16[6,6,512]{2,1,0:T(8,128)(2,1)S(1)}, bf16[6,6,512]{2,1,0:T(8,128)(2,1)S(1)}, u32[]{:S(2)}, u32[]{:S(2)}) %collective-permute-start.1) | collective-permute-done | bytes 36896 | tf_op jit(solution)/shard_map/ppermute | solution.py:278
  16.8 1.8 %collective-permute-done.2.se_in = bf16[6,6,512]{2,1,0:T(8,128)(2,1)S(1)} collective-permute-done((bf16[6,6,512]{2,1,0:T(8,128)(2,1)S(1)}, bf16[6,6,512]{2,1,0:T(8,128)(2,1)S(1)}, u32[]{:S(2)}, u32[]{:S(2)}) %collective-permute-start.2) | collective-permute-done | bytes 36896 | tf_op jit(solution)/shard_map/ppermute | solution.py:278
  18.6 0.0 copy-done.1
  18.6 0.0 copy-done.3
  18.6 0.0 copy-done.6
  18.6 0.0 copy-done.8
  18.6 2.4 %shard_map.92 = (bf16[6,6,512]{2,1,0:T(8,128)(2,1)S(1)}, bf16[6,6,512]{2,1,0:T(8,128)(2,1)S(1)}, bf16[6,6,512]{2,1,0:T(8,128)(2,1)S(1)}, bf16[6,6,512]{2,1,0:T(8,128)(2,1)S(1)}) custom-call(bf16[6,6,512]{2,1,0:T(8,128)(2,1)S(1)} %get-tuple-element.13.nw_in, bf16[6,6,512]{2,1,0:T(8,128)(2,1)S(1)} %collective-permute-done.ne_in, ...), custom_call_target="tpu_custom_call" | custom-call | flops 400000000 | bytes 2500000 | tf_op jit(solution)/shard_map/pallas_call | solution.py:262
  21.0 0.1 collective-permute-start.3
  21.0 0.8 %collective-permute-start.4 = (bf16[6,6,512]{2,1,0:T(8,128)(2,1)S(1)}, bf16[6,6,512]{2,1,0:T(8,128)(2,1)S(1)}, u32[]{:S(2)}, u32[]{:S(2)}) collective-permute-start(bf16[6,6,512]{2,1,0:T(8,128)(2,1)S(1)} %get-tuple-element.18), channel_id=1, source_target_pairs={{24,0},{25,1},{26,2},{27,3},{28,4},{29,5},{30,6},{31,7},{0,8},{1,9... | collective-permute-start | bytes 110600 | tf_op jit(solution)/shard_map/ppermute | solution.py:278
  21.8 0.0 collective-permute-start.5
  21.9 6.8 %collective-permute-done.3 = bf16[6,6,512]{2,1,0:T(8,128)(2,1)S(1)} collective-permute-done((bf16[6,6,512]{2,1,0:T(8,128)(2,1)S(1)}, bf16[6,6,512]{2,1,0:T(8,128)(2,1)S(1)}, u32[]{:S(2)}, u32[]{:S(2)}) %collective-permute-start.3) | collective-permute-done | bytes 36896 | tf_op jit(solution)/shard_map/ppermute | solution.py:278
  28.6 0.0 collective-permute-done.4
  28.6 0.7 %collective-permute-done.5 = bf16[6,6,512]{2,1,0:T(8,128)(2,1)S(1)} collective-permute-done((bf16[6,6,512]{2,1,0:T(8,128)(2,1)S(1)}, bf16[6,6,512]{2,1,0:T(8,128)(2,1)S(1)}, u32[]{:S(2)}, u32[]{:S(2)}) %collective-permute-start.5) | collective-permute-done | bytes 36896 | tf_op jit(solution)/shard_map/ppermute | solution.py:278
  29.3 0.7 %maximum_bitcast_fusion = bf16[1,12,12,512]{3,2,1,0:T(8,128)(2,1)} fusion(bf16[6,6,512]{2,1,0:T(8,128)(2,1)S(1)} %get-tuple-element.20, bf16[6,6,512]{2,1,0:T(8,128)(2,1)S(1)} %collective-permute-done.5, bf16[6,6,512]{2,1,0:T(8,128)(2,1)S(1)} %collective-permute-done.4, bf16[6,6,512]{2,1,0:T(8,128)(2,1)S(1)} %collective-permute-done.3), kind=kLoop, calls=%fused_computation | loop fusion | flops 589824 | bytes 294912 | tf_op jit(solution)/shard_map/broadcast_in_dim | solution.py:298
Async XLA Ops:
  0.0 1.4 %copy-start = (bf16[512,1536]{1,0:T(8,128)(2,1)S(1)}, bf16[512,1536]{1,0:T(8,128)(2,1)}, u32[]{:S(2)}) copy-start(bf16[512,1536]{1,0:T(8,128)(2,1)} %wqkv.2) | copy-start | bytes 4718596
  1.4 1.0 %copy-start.2 = (bf16[512,512]{1,0:T(8,128)(2,1)S(1)}, bf16[512,512]{1,0:T(8,128)(2,1)}, u32[]{:S(2)}) copy-start(bf16[512,512]{1,0:T(8,128)(2,1)} %wproj.2) | copy-start | bytes 1572868
  2.5 0.9 %copy-start.4 = (bf16[1,12,12,512]{3,2,1,0:T(8,128)(2,1)S(1)}, bf16[1,12,12,512]{3,2,1,0:T(8,128)(2,1)}, u32[]{:S(2)}) copy-start(bf16[1,12,12,512]{3,2,1,0:T(8,128)(2,1)} %tokens.1) | copy-start | bytes 442372
  3.4 0.8 %copy-start.5 = (f32[1,16,529]{2,1,0:T(8,128)S(1)}, f32[1,16,529]{2,1,0:T(8,128)}, u32[]{:S(2)}) copy-start(f32[1,16,529]{2,1,0:T(8,128)} %table.2) | copy-start | bytes 101572
  4.2 0.7 %copy-start.7 = (f32[512]{0:T(512)S(1)}, f32[512]{0:T(512)}, u32[]{:S(2)}) copy-start(f32[512]{0:T(512)} %param.10) | copy-start | bytes 6148
  4.8 13.7 %copy-start.1 = (bf16[512,1536]{1,0:T(8,128)(2,1)S(1)}, bf16[512,1536]{1,0:T(8,128)(2,1)}, u32[]{:S(2)}) copy-start(bf16[512,1536]{1,0:T(8,128)(2,1)} %wqkv.3) | copy-start | bytes 4718596
  4.8 13.7 %copy-start.3 = (bf16[512,512]{1,0:T(8,128)(2,1)S(1)}, bf16[512,512]{1,0:T(8,128)(2,1)}, u32[]{:S(2)}) copy-start(bf16[512,512]{1,0:T(8,128)(2,1)} %wproj.3) | copy-start | bytes 1572868
  4.8 13.7 %copy-start.6 = (f32[1,16,529]{2,1,0:T(8,128)S(1)}, f32[1,16,529]{2,1,0:T(8,128)}, u32[]{:S(2)}) copy-start(f32[1,16,529]{2,1,0:T(8,128)} %table.3) | copy-start | bytes 101572
  4.8 13.7 %copy-start.8 = (f32[512]{0:T(512)S(1)}, f32[512]{0:T(512)}, u32[]{:S(2)}) copy-start(f32[512]{0:T(512)} %param.14) | copy-start | bytes 6148
  8.3 7.8 %collective-permute-start = (bf16[6,6,512]{2,1,0:T(8,128)(2,1)S(1)}, bf16[6,6,512]{2,1,0:T(8,128)(2,1)S(1)}, u32[]{:S(2)}, u32[]{:S(2)}) collective-permute-start(bf16[6,6,512]{2,1,0:T(8,128)(2,1)S(1)} %get-tuple-element.14), channel_id=1, source_target_pairs={{1,0},{2,1},{3,2},{4,3},{5,4},{6,5},{7,6},{0,7},{9,8},{10,9},{11,1... | collective-permute-start | bytes 110600 | tf_op jit(solution)/shard_map/ppermute | solution.py:278
  14.4 2.4 %collective-permute-start.1 = (bf16[6,6,512]{2,1,0:T(8,128)(2,1)S(1)}, bf16[6,6,512]{2,1,0:T(8,128)(2,1)S(1)}, u32[]{:S(2)}, u32[]{:S(2)}) collective-permute-start(bf16[6,6,512]{2,1,0:T(8,128)(2,1)S(1)} %get-tuple-element.15), channel_id=1, source_target_pairs={{8,0},{9,1},{10,2},{11,3},{12,4},{13,5},{14,6},{15,7},{16,8},{17,9... | collective-permute-start | bytes 110600 | tf_op jit(solution)/shard_map/ppermute | solution.py:278
  15.1 3.5 %collective-permute-start.2 = (bf16[6,6,512]{2,1,0:T(8,128)(2,1)S(1)}, bf16[6,6,512]{2,1,0:T(8,128)(2,1)S(1)}, u32[]{:S(2)}, u32[]{:S(2)}) collective-permute-start(bf16[6,6,512]{2,1,0:T(8,128)(2,1)S(1)} %get-tuple-element.16), channel_id=1, source_target_pairs={{9,0},{10,1},{11,2},{12,3},{13,4},{14,5},{15,6},{8,7},{17,8},{18,9... | collective-permute-start | bytes 110600 | tf_op jit(solution)/shard_map/ppermute | solution.py:278
  21.0 7.7 %collective-permute-start.3 = (bf16[6,6,512]{2,1,0:T(8,128)(2,1)S(1)}, bf16[6,6,512]{2,1,0:T(8,128)(2,1)S(1)}, u32[]{:S(2)}, u32[]{:S(2)}) collective-permute-start(bf16[6,6,512]{2,1,0:T(8,128)(2,1)S(1)} %get-tuple-element.17), channel_id=1, source_target_pairs={{31,0},{24,1},{25,2},{26,3},{27,4},{28,5},{29,6},{30,7},{7,8},{0,9... | collective-permute-start | bytes 110600 | tf_op jit(solution)/shard_map/ppermute | solution.py:278
  21.0 7.6 %collective-permute-start.4 = (bf16[6,6,512]{2,1,0:T(8,128)(2,1)S(1)}, bf16[6,6,512]{2,1,0:T(8,128)(2,1)S(1)}, u32[]{:S(2)}, u32[]{:S(2)}) collective-permute-start(bf16[6,6,512]{2,1,0:T(8,128)(2,1)S(1)} %get-tuple-element.18), channel_id=1, source_target_pairs={{24,0},{25,1},{26,2},{27,3},{28,4},{29,5},{30,6},{31,7},{0,8},{1,9... | collective-permute-start | bytes 110600 | tf_op jit(solution)/shard_map/ppermute | solution.py:278
  21.8 7.5 %collective-permute-start.5 = (bf16[6,6,512]{2,1,0:T(8,128)(2,1)S(1)}, bf16[6,6,512]{2,1,0:T(8,128)(2,1)S(1)}, u32[]{:S(2)}, u32[]{:S(2)}) collective-permute-start(bf16[6,6,512]{2,1,0:T(8,128)(2,1)S(1)} %get-tuple-element.19), channel_id=1, source_target_pairs={{7,0},{0,1},{1,2},{2,3},{3,4},{4,5},{5,6},{6,7},{15,8},{8,9},{9,10... | collective-permute-start | bytes 110600 | tf_op jit(solution)/shard_map/ppermute | solution.py:278

commit v3 on v2

--- a/solution.py
+++ b/solution.py
@@ -258,6 +258,7 @@
         order = (args[1], args[0], *args[2:])
         scratch += [pltpu.VMEM(a.shape, a.dtype) for a in order]
         scratch += [pltpu.SemaphoreType.DMA((len(order),))]
+        args = tuple(pltpu.with_memory_space_constraint(a, pltpu.HBM) for a in args)
     source = pl.BlockSpec(memory_space=pltpu.HBM) if fetch else vmem
     return pl.pallas_call(
         kernel,

time: 30.4 us -> 25.8 us (0.85)
  local copies, waits for them, and re-layouts: 4.85 us -> 0.01 us
  Pallas kernels: 5.84 us -> 6.3 us
    unnamed x18 -> x8, local copies, waits for them, and re-layouts: 4.85 us -> 0.01 us
    pallas_call x2, Pallas kernels: 5.84 us -> 6.3 us  [block(): pl.pallas_call(kernel, out_shape=(piece,) * 4, in_specs=[source] * len(ar...]
where the time goes in v3:
time: 25.8 us; the launch traced here: 25.7 us
  waiting for transfers between devices  10.1 us (39%)
  starting transfers between devices  8.52 us (33%)
  Pallas kernels  6.3 us (24%)
  other arithmetic  0.74 us (3%)
    ppermute x6, waiting for transfers between devices, moved(): return lax.ppermute(piece, ('lat', 'lon'), route)  10.1 us
    ppermute x6, starting transfers between devices, moved(): return lax.ppermute(piece, ('lat', 'lon'), route)  8.52 us
    pallas_call x2, Pallas kernels, block(): pl.pallas_call(kernel, out_shape=(piece,) * 4, in_specs=[source] * len(ar...  6.3 us
    broadcast_in_dim x1, other arithmetic, shards(): return jnp.concatenate([upper, lower], axis=0)[None]  0.74 us
  transfers between devices with their start and end apart: 6, of which 5 were waited for; matrix products, arithmetic and copies ran while one was open for 0% of the time, Pallas kernels for 0%

profile of v3, /device:TPU:0, one launch (start us, length us, event | category | flops | bytes accessed | tf_op | source)
XLA Modules:
  0.0 25.7 jit_solution(7665482924518448330)
XLA Ops:
  0.0 0.0 copy-start.2
  0.0 0.0 copy-start.1
  0.0 0.0 copy-start
  0.0 0.0 copy-start.3
  0.0 3.9 %shard_map.91 = (bf16[6,6,512]{2,1,0:T(8,128)(2,1)S(1)}, bf16[6,6,512]{2,1,0:T(8,128)(2,1)S(1)}, bf16[6,6,512]{2,1,0:T(8,128)(2,1)S(1)}, bf16[6,6,512]{2,1,0:T(8,128)(2,1)S(1)}) custom-call(bf16[1,12,12,512]{3,2,1,0:T(8,128)(2,1)} %tokens.1, f32[1,16,529]{2,1,0:T(8,128)} %table.2, f32[1,512]{1,0:T(1,128)} %bitcast.5, bf16[512,1536]{1,0:T(8,128)(2,1)} %wqkv.2, ...), custom_call_target="tpu_custom_call" | custom-call | flops 400000000 | bytes 2500000 | tf_op jit(solution)/shard_map/pallas_call | solution.py:263
  4.0 6.1 %collective-permute-start = (bf16[6,6,512]{2,1,0:T(8,128)(2,1)S(1)}, bf16[6,6,512]{2,1,0:T(8,128)(2,1)S(1)}, u32[]{:S(2)}, u32[]{:S(2)}) collective-permute-start(bf16[6,6,512]{2,1,0:T(8,128)(2,1)S(1)} %get-tuple-element.14), channel_id=1, source_target_pairs={{1,0},{2,1},{3,2},{4,3},{5,4},{6,5},{7,6},{0,7},{9,8},{10,9},{11,1... | collective-permute-start | bytes 110600 | tf_op jit(solution)/shard_map/ppermute | solution.py:279
  10.0 0.7 %collective-permute-start.1 = (bf16[6,6,512]{2,1,0:T(8,128)(2,1)S(1)}, bf16[6,6,512]{2,1,0:T(8,128)(2,1)S(1)}, u32[]{:S(2)}, u32[]{:S(2)}) collective-permute-start(bf16[6,6,512]{2,1,0:T(8,128)(2,1)S(1)} %get-tuple-element.15), channel_id=1, source_target_pairs={{8,0},{9,1},{10,2},{11,3},{12,4},{13,5},{14,6},{15,7},{16,8},{17,9... | collective-permute-start | bytes 110600 | tf_op jit(solution)/shard_map/ppermute | solution.py:279
  10.7 0.9 %collective-permute-start.2 = (bf16[6,6,512]{2,1,0:T(8,128)(2,1)S(1)}, bf16[6,6,512]{2,1,0:T(8,128)(2,1)S(1)}, u32[]{:S(2)}, u32[]{:S(2)}) collective-permute-start(bf16[6,6,512]{2,1,0:T(8,128)(2,1)S(1)} %get-tuple-element.16), channel_id=1, source_target_pairs={{9,0},{10,1},{11,2},{12,3},{13,4},{14,5},{15,6},{8,7},{17,8},{18,9... | collective-permute-start | bytes 110600 | tf_op jit(solution)/shard_map/ppermute | solution.py:279
  11.6 0.2 collective-permute-done.ne_in
  11.8 0.7 %collective-permute-done.1.sw_in = bf16[6,6,512]{2,1,0:T(8,128)(2,1)S(1)} collective-permute-done((bf16[6,6,512]{2,1,0:T(8,128)(2,1)S(1)}, bf16[6,6,512]{2,1,0:T(8,128)(2,1)S(1)}, u32[]{:S(2)}, u32[]{:S(2)}) %collective-permute-start.1) | collective-permute-done | bytes 36896 | tf_op jit(solution)/shard_map/ppermute | solution.py:279
  12.4 1.8 %collective-permute-done.2.se_in = bf16[6,6,512]{2,1,0:T(8,128)(2,1)S(1)} collective-permute-done((bf16[6,6,512]{2,1,0:T(8,128)(2,1)S(1)}, bf16[6,6,512]{2,1,0:T(8,128)(2,1)S(1)}, u32[]{:S(2)}, u32[]{:S(2)}) %collective-permute-start.2) | collective-permute-done | bytes 36896 | tf_op jit(solution)/shard_map/ppermute | solution.py:279
  14.2 0.0 copy-done.2
  14.2 0.0 copy-done.1
  14.2 0.0 copy-done
  14.2 0.0 copy-done.3
  14.2 2.4 %shard_map.92 = (bf16[6,6,512]{2,1,0:T(8,128)(2,1)S(1)}, bf16[6,6,512]{2,1,0:T(8,128)(2,1)S(1)}, bf16[6,6,512]{2,1,0:T(8,128)(2,1)S(1)}, bf16[6,6,512]{2,1,0:T(8,128)(2,1)S(1)}) custom-call(bf16[6,6,512]{2,1,0:T(8,128)(2,1)S(1)} %get-tuple-element.13.nw_in, bf16[6,6,512]{2,1,0:T(8,128)(2,1)S(1)} %collective-permute-done.ne_in, ...), custom_call_target="tpu_custom_call" | custom-call | flops 400000000 | bytes 2500000 | tf_op jit(solution)/shard_map/pallas_call | solution.py:263
  16.6 0.1 collective-permute-start.3
  16.7 0.8 %collective-permute-start.4 = (bf16[6,6,512]{2,1,0:T(8,128)(2,1)S(1)}, bf16[6,6,512]{2,1,0:T(8,128)(2,1)S(1)}, u32[]{:S(2)}, u32[]{:S(2)}) collective-permute-start(bf16[6,6,512]{2,1,0:T(8,128)(2,1)S(1)} %get-tuple-element.18), channel_id=1, source_target_pairs={{24,0},{25,1},{26,2},{27,3},{28,4},{29,5},{30,6},{31,7},{0,8},{1,9... | collective-permute-start | bytes 110600 | tf_op jit(solution)/shard_map/ppermute | solution.py:279
  17.5 0.0 collective-permute-start.5
  17.5 6.8 %collective-permute-done.3 = bf16[6,6,512]{2,1,0:T(8,128)(2,1)S(1)} collective-permute-done((bf16[6,6,512]{2,1,0:T(8,128)(2,1)S(1)}, bf16[6,6,512]{2,1,0:T(8,128)(2,1)S(1)}, u32[]{:S(2)}, u32[]{:S(2)}) %collective-permute-start.3) | collective-permute-done | bytes 36896 | tf_op jit(solution)/shard_map/ppermute | solution.py:279
  24.3 0.0 collective-permute-done.4
  24.3 0.7 %collective-permute-done.5 = bf16[6,6,512]{2,1,0:T(8,128)(2,1)S(1)} collective-permute-done((bf16[6,6,512]{2,1,0:T(8,128)(2,1)S(1)}, bf16[6,6,512]{2,1,0:T(8,128)(2,1)S(1)}, u32[]{:S(2)}, u32[]{:S(2)}) %collective-permute-start.5) | collective-permute-done | bytes 36896 | tf_op jit(solution)/shard_map/ppermute | solution.py:279
  24.9 0.7 %maximum_bitcast_fusion = bf16[1,12,12,512]{3,2,1,0:T(8,128)(2,1)} fusion(bf16[6,6,512]{2,1,0:T(8,128)(2,1)S(1)} %get-tuple-element.20, bf16[6,6,512]{2,1,0:T(8,128)(2,1)S(1)} %collective-permute-done.5, bf16[6,6,512]{2,1,0:T(8,128)(2,1)S(1)} %collective-permute-done.4, bf16[6,6,512]{2,1,0:T(8,128)(2,1)S(1)} %collective-permute-done.3), kind=kLoop, calls=%fused_computation | loop fusion | flops 589824 | bytes 294912 | tf_op jit(solution)/shard_map/broadcast_in_dim | solution.py:299
Async XLA Ops:
  0.0 14.2 %copy-start.2 = (f32[1,16,529]{2,1,0:T(8,128)S(1)}, f32[1,16,529]{2,1,0:T(8,128)}, u32[]{:S(2)}) copy-start(f32[1,16,529]{2,1,0:T(8,128)} %table.3) | copy-start | bytes 101572
  0.0 14.2 %copy-start.1 = (bf16[512,512]{1,0:T(8,128)(2,1)S(1)}, bf16[512,512]{1,0:T(8,128)(2,1)}, u32[]{:S(2)}) copy-start(bf16[512,512]{1,0:T(8,128)(2,1)} %wproj.3) | copy-start | bytes 1572868
  0.0 14.2 %copy-start = (bf16[512,1536]{1,0:T(8,128)(2,1)S(1)}, bf16[512,1536]{1,0:T(8,128)(2,1)}, u32[]{:S(2)}) copy-start(bf16[512,1536]{1,0:T(8,128)(2,1)} %wqkv.3) | copy-start | bytes 4718596
  0.0 14.2 %copy-start.3 = (f32[512]{0:T(512)S(1)}, f32[512]{0:T(512)}, u32[]{:S(2)}) copy-start(f32[512]{0:T(512)} %param.14) | copy-start | bytes 6148
  4.0 7.8 %collective-permute-start = (bf16[6,6,512]{2,1,0:T(8,128)(2,1)S(1)}, bf16[6,6,512]{2,1,0:T(8,128)(2,1)S(1)}, u32[]{:S(2)}, u32[]{:S(2)}) collective-permute-start(bf16[6,6,512]{2,1,0:T(8,128)(2,1)S(1)} %get-tuple-element.14), channel_id=1, source_target_pairs={{1,0},{2,1},{3,2},{4,3},{5,4},{6,5},{7,6},{0,7},{9,8},{10,9},{11,1... | collective-permute-start | bytes 110600 | tf_op jit(solution)/shard_map/ppermute | solution.py:279
  10.0 2.4 %collective-permute-start.1 = (bf16[6,6,512]{2,1,0:T(8,128)(2,1)S(1)}, bf16[6,6,512]{2,1,0:T(8,128)(2,1)S(1)}, u32[]{:S(2)}, u32[]{:S(2)}) collective-permute-start(bf16[6,6,512]{2,1,0:T(8,128)(2,1)S(1)} %get-tuple-element.15), channel_id=1, source_target_pairs={{8,0},{9,1},{10,2},{11,3},{12,4},{13,5},{14,6},{15,7},{16,8},{17,9... | collective-permute-start | bytes 110600 | tf_op jit(solution)/shard_map/ppermute | solution.py:279
  10.7 3.5 %collective-permute-start.2 = (bf16[6,6,512]{2,1,0:T(8,128)(2,1)S(1)}, bf16[6,6,512]{2,1,0:T(8,128)(2,1)S(1)}, u32[]{:S(2)}, u32[]{:S(2)}) collective-permute-start(bf16[6,6,512]{2,1,0:T(8,128)(2,1)S(1)} %get-tuple-element.16), channel_id=1, source_target_pairs={{9,0},{10,1},{11,2},{12,3},{13,4},{14,5},{15,6},{8,7},{17,8},{18,9... | collective-permute-start | bytes 110600 | tf_op jit(solution)/shard_map/ppermute | solution.py:279
  16.6 7.6 %collective-permute-start.3 = (bf16[6,6,512]{2,1,0:T(8,128)(2,1)S(1)}, bf16[6,6,512]{2,1,0:T(8,128)(2,1)S(1)}, u32[]{:S(2)}, u32[]{:S(2)}) collective-permute-start(bf16[6,6,512]{2,1,0:T(8,128)(2,1)S(1)} %get-tuple-element.17), channel_id=1, source_target_pairs={{31,0},{24,1},{25,2},{26,3},{27,4},{28,5},{29,6},{30,7},{7,8},{0,9... | collective-permute-start | bytes 110600 | tf_op jit(solution)/shard_map/ppermute | solution.py:279
  16.7 7.6 %collective-permute-start.4 = (bf16[6,6,512]{2,1,0:T(8,128)(2,1)S(1)}, bf16[6,6,512]{2,1,0:T(8,128)(2,1)S(1)}, u32[]{:S(2)}, u32[]{:S(2)}) collective-permute-start(bf16[6,6,512]{2,1,0:T(8,128)(2,1)S(1)} %get-tuple-element.18), channel_id=1, source_target_pairs={{24,0},{25,1},{26,2},{27,3},{28,4},{29,5},{30,6},{31,7},{0,8},{1,9... | collective-permute-start | bytes 110600 | tf_op jit(solution)/shard_map/ppermute | solution.py:279
  17.5 7.5 %collective-permute-start.5 = (bf16[6,6,512]{2,1,0:T(8,128)(2,1)S(1)}, bf16[6,6,512]{2,1,0:T(8,128)(2,1)S(1)}, u32[]{:S(2)}, u32[]{:S(2)}) collective-permute-start(bf16[6,6,512]{2,1,0:T(8,128)(2,1)S(1)} %get-tuple-element.19), channel_id=1, source_target_pairs={{7,0},{0,1},{1,2},{2,3},{3,4},{4,5},{5,6},{6,7},{15,8},{8,9},{9,10... | collective-permute-start | bytes 110600 | tf_op jit(solution)/shard_map/ppermute | solution.py:279

commit v4 on v3

--- a/solution.py
+++ b/solution.py
@@ -6,6 +6,7 @@
 from jax.experimental import pallas as pl
 from jax.experimental.pallas import tpu as pltpu
 from jax.sharding import PartitionSpec as P
+
 
 HEADS = 16
 WH = 12
@@ -203,43 +204,89 @@
             at += 1
 
 
-def first_kernel(tokens, table, gain, wqkv, wproj, nw, ne, sw, se, xs, ys, tab, strips, probs, *here):
-    here, sems = here[:-1], here[-1]
-    copies = [
-        pltpu.make_async_copy(a, b, sems.at[i]) for i, (a, b) in enumerate(zip((table, tokens, gain, wqkv, wproj), here))
-    ]
-    for copy in copies:
-        copy.start()
-    xs[:, WW:, :] = jnp.zeros((WH, PITCH - WW, xs.shape[-1]), F32)
-    copies[0].wait()
-    bias_strips(here[0], tab, strips)
-    copies[1].wait()
-    xs[:, :WW, :] = here[1][0].astype(F32)
-    copies[2].wait()
-
-    def weights(i):
-        copies[3 + i].wait()
-        return here[3 + i]
-
-    attend(xs, ys, here[2], weights, strips, probs, None)
-    quadrants(ys, (nw, ne, sw, se))
-
-
-def second_kernel(nw_in, ne_in, sw_in, se_in, table, gain, wqkv, wproj, nw, ne, sw, se, xs, ys, tab, strips, probs):
+def edge(first):
+    return lax.axis_index("lon") == (0 if first else lax.axis_size("lon") - 1)
+
+
+def keep(mine, done, outs):
+    @pl.when(mine)
+    def _():
+        for a, b in zip(done, outs):
+            b[...] = a[...]
+
+
+def first_kernel(early, *refs):
+    tokens, table, gain, wqkv, wproj, *refs = refs
+    if not early:
+        done, refs = refs[:4], refs[4:]
+    (nw, ne, sw, se), refs = refs[:4], refs[4:]
+    if early:
+        (nw_wrap, sw_wrap), refs = refs[:2], refs[2:]
+    xs, ys, tab, strips, probs, *here, sems = refs
+    mine = edge(True)
+
+    @pl.when(mine if early else jnp.logical_not(mine))
+    def _():
+        copies = [
+            pltpu.make_async_copy(a, b, sems.at[i])
+            for i, (a, b) in enumerate(zip((table, tokens, gain, wqkv, wproj), here))
+        ]
+        for copy in copies:
+            copy.start()
+        xs[:, WW:, :] = jnp.zeros((WH, PITCH - WW, xs.shape[-1]), F32)
+        copies[0].wait()
+        bias_strips(here[0], tab, strips)
+        copies[1].wait()
+        xs[:, :WW, :] = here[1][0].astype(F32)
+        copies[2].wait()
+
+        def weights(i):
+            copies[3 + i].wait()
+            return here[3 + i]
+
+        attend(xs, ys, here[2], weights, strips, probs, None)
+        quadrants(ys, (nw, ne, sw, se))
+        if early:
+            nw_wrap[...] = nw[...]
+            sw_wrap[...] = sw[...]
+
+    if not early:
+        keep(mine, done, (nw, ne, sw, se))
+
+
+def second_kernel(early, *refs):
+    nw_in, sw_in, ne_in, se_in, ne_wrap_in, se_wrap_in, table, gain, wqkv, wproj, *refs = refs
+    if not early:
+        done, refs = refs[:4], refs[4:]
+    (nw, ne, sw, se), refs = refs[:4], refs[4:]
+    if early:
+        (ne_wrap, se_wrap), refs = refs[:2], refs[2:]
+    xs, ys, tab, strips, probs = refs
+    last = edge(False)
     polar = lax.axis_index("lat") == lax.axis_size("lat") - 1
-    xs[:, WW:, :] = jnp.zeros((WH, PITCH - WW, xs.shape[-1]), F32)
-    at = 0
-    pieces = (nw_in, ne_in, sw_in, se_in)
-    for r in (0, HALF_R):
-        for c in (0, HALF_C):
-            xs[r : r + HALF_R, c : c + HALF_C, :] = pieces[at][...].astype(F32)
-            at += 1
-    bias_strips(table, tab, strips)
-    attend(xs, ys, gain, lambda i: (wqkv, wproj)[i], strips, probs, polar)
-    quadrants(ys, (nw, ne, sw, se))
-
-
-def block(kernel, pieces, table, gain, wqkv, wproj, fetch):
+
+    @pl.when(last if early else jnp.logical_not(last))
+    def _():
+        xs[:, WW:, :] = jnp.zeros((WH, PITCH - WW, xs.shape[-1]), F32)
+        east = (ne_wrap_in, se_wrap_in) if early else (ne_in, se_in)
+        pieces = (nw_in, east[0], sw_in, east[1])
+        at = 0
+        for r in (0, HALF_R):
+            for c in (0, HALF_C):
+                xs[r : r + HALF_R, c : c + HALF_C, :] = pieces[at][...].astype(F32)
+                at += 1
+        bias_strips(table, tab, strips)
+        attend(xs, ys, gain, lambda i: (wqkv, wproj)[i], strips, probs, polar)
+        quadrants(ys, (nw, ne, sw, se))
+        if early:
+            ne_wrap[...] = ne[...]
+            se_wrap[...] = se[...]
+
+    if not early:
+        keep(last, done, (nw, ne, sw, se))
+
+
+def block(kernel, pieces, table, gain, wqkv, wproj, fetch, done=()):
     width = wproj.shape[0]
     heads, count = table.shape[1:]
     lanes = -(-count // LANES) * LANES
@@ -260,21 +307,25 @@
         scratch += [pltpu.SemaphoreType.DMA((len(order),))]
         args = tuple(pltpu.with_memory_space_constraint(a, pltpu.HBM) for a in args)
     source = pl.BlockSpec(memory_space=pltpu.HBM) if fetch else vmem
+    outs = 4 if done else 6
     return pl.pallas_call(
-        kernel,
-        out_shape=(piece,) * 4,
-        in_specs=[source] * len(args),
-        out_specs=(vmem,) * 4,
+        functools.partial(kernel, not done),
+        out_shape=(piece,) * outs,
+        in_specs=[source] * len(args) + [vmem] * len(done),
+        out_specs=(vmem,) * outs,
         scratch_shapes=scratch,
         compiler_params=pltpu.CompilerParams(vmem_limit_bytes=24 << 20),
         cost_estimate=pl.CostEstimate(flops=400_000_000, bytes_accessed=2_500_000, transcendentals=600_000),
-    )(*args)
-
-
-def moved(piece, lat, lon):
+    )(*args, *done)
+
+
+def moved(piece, lat, lon, wrap):
     rows, cols = lax.axis_size("lat"), lax.axis_size("lon")
     route = [
-        (((i + lat) % rows) * cols + (j + lon) % cols, i * cols + j) for i in range(rows) for j in range(cols)
+        (((i + lat) % rows) * cols + (j + lon) % cols, i * cols + j)
+        for i in range(rows)
+        for j in range(cols)
+        if lon == 0 or (0 <= j + lon < cols) != wrap
     ]
     return lax.ppermute(piece, ("lat", "lon"), route)
 
@@ -290,10 +341,26 @@
     proj_second,
     bias_second,
 ):
-    nw, ne, sw, se = block(first_kernel, (tokens,), bias_first, gain_first, qkv_first, proj_first, True)
-    window = (se, moved(sw, 0, 1), moved(ne, 1, 0), moved(nw, 1, 1))
-    nw, ne, sw, se = block(second_kernel, window, bias_second, gain_second, qkv_second, proj_second, False)
-    west, north, corner = moved(ne, 0, -1), moved(sw, -1, 0), moved(se, -1, -1)
+    first = (bias_first, gain_first, qkv_first, proj_first, True)
+    second = (bias_second, gain_second, qkv_second, proj_second, False)
+    *done, nw_wrap, sw_wrap = block(first_kernel, (tokens,), *first)
+    east_wrap = moved(sw_wrap, 0, 1, True)
+    corner_wrap = moved(nw_wrap, 1, 1, True)
+    nw, ne, sw, se = block(first_kernel, (tokens,), *first, done)
+    south = moved(ne, 1, 0, False)
+    east = moved(sw, 0, 1, False)
+    corner = moved(nw, 1, 1, False)
+    window = (se, south, east, corner, east_wrap, corner_wrap)
+    *done, ne_wrap, se_wrap = block(second_kernel, window, *second)
+    west_wrap = moved(ne_wrap, 0, -1, True)
+    corner_wrap = moved(se_wrap, -1, -1, True)
+    nw, ne, sw, se = block(second_kernel, window, *second, done)
+    north = moved(sw, -1, 0, False)
+    west = moved(ne, 0, -1, False)
+    corner = moved(se, -1, -1, False)
+    head = edge(True)
+    west = jnp.where(head, west_wrap, west)
+    corner = jnp.where(head, corner_wrap, corner)
     upper = jnp.concatenate([corner, north], axis=1)
     lower = jnp.concatenate([west, nw], axis=1)
     return jnp.concatenate([upper, lower], axis=0)[None]

time: 25.8 us -> 37.9 us (1.47)
  starting transfers between devices: 8.52 us -> 21.1 us
  waiting for transfers between devices: 10.1 us -> 9.3 us
    ppermute x6 -> x10, starting transfers between devices: 8.52 us -> 21.1 us  [moved(): return lax.ppermute(piece, ('lat', 'lon'), route)]
    ppermute x6 -> x10, waiting for transfers between devices: 10.1 us -> 9.3 us  [moved(): return lax.ppermute(piece, ('lat', 'lon'), route)]
    pallas_call x2 -> x4, Pallas kernels: 6.3 us -> 6.27 us  [block(): pl.pallas_call(functools.partial(kernel, not done), out_shape=(piece,) *...]
  transfers between devices with their start and end apart: 6 -> 10, of which waited for: 5 -> 4; matrix products, arithmetic and copies ran while one was open for 0% -> 0% of each run, Pallas kernels for 0% -> 0%
where the time goes in v4:
time: 37.9 us; the launch traced here: 37.6 us
  starting transfers between devices  21.1 us (56%)
  waiting for transfers between devices  9.3 us (25%)
  Pallas kernels  6.27 us (17%)
  other arithmetic  0.76 us (2%)
    ppermute x10, starting transfers between devices, moved(): return lax.ppermute(piece, ('lat', 'lon'), route)  21.1 us
    ppermute x10, waiting for transfers between devices, moved(): return lax.ppermute(piece, ('lat', 'lon'), route)  9.3 us
    pallas_call x4, Pallas kernels, block(): pl.pallas_call(functools.partial(kernel, not done), out_shape=(piece,) *...  6.27 us
  transfers between devices with their start and end apart: 10, of which 4 were waited for; matrix products, arithmetic and copies ran while one was open for 0% of the time, Pallas kernels for 0%

profile of v4, /device:TPU:0, one launch (start us, length us, event | category | flops | bytes accessed | tf_op | source)
XLA Modules:
  0.0 37.6 jit_solution(6626348822051853329)
XLA Ops:
  0.0 3.8 %shard_map.91 = (bf16[6,6,512]{2,1,0:T(8,128)(2,1)S(1)}, bf16[6,6,512]{2,1,0:T(8,128)(2,1)S(1)}, bf16[6,6,512]{2,1,0:T(8,128)(2,1)S(1)}, bf16[6,6,512]{2,1,0:T(8...) custom-call(bf16[1,12,12,512]{3,2,1,0:T(8,128)(2,1)} %refs_0_.3, f32[1,16,529]{2,1,0:T(8,128)} %refs_1_.3, ...), custom_call_target="tpu_custom_call" | custom-call | flops 400000000 | bytes 2500000 | tf_op jit(solution)/shard_map/pallas_call | solution.py:311
  3.8 0.0 copy-start
  3.8 0.0 copy-start.1
  3.8 0.0 copy-start.2
  3.8 0.0 copy-start.3
  3.8 0.1 shard_map.92
  3.9 2.5 %collective-permute-start = (bf16[6,6,512]{2,1,0:T(8,128)(2,1)S(1)}, bf16[6,6,512]{2,1,0:T(8,128)(2,1)S(1)}, u32[]{:S(2)}, u32[]{:S(2)}) collective-permute-start(bf16[6,6,512]{2,1,0:T(8,128)(2,1)S(1)} %get-tuple-element.30), channel_id=1, source_target_pairs={{8,0},{9,1},{10,2},{11,3},{12,4},{13,5},{14,6},{15,7},{16,8},{17,9... | collective-permute-start | bytes 110600 | tf_op jit(solution)/shard_map/ppermute | solution.py:330
  6.4 1.3 %collective-permute-start.1 = (bf16[6,6,512]{2,1,0:T(8,128)(2,1)S(1)}, bf16[6,6,512]{2,1,0:T(8,128)(2,1)S(1)}, u32[]{:S(2)}, u32[]{:S(2)}) collective-permute-start(bf16[6,6,512]{2,1,0:T(8,128)(2,1)S(1)} %get-tuple-element.31), channel_id=1, source_target_pairs={{1,0},{2,1},{3,2},{4,3},{5,4},{6,5},{7,6},{9,8},{10,9},{11,10},{12... | collective-permute-start | bytes 110600 | tf_op jit(solution)/shard_map/ppermute | solution.py:330
  7.7 1.3 %collective-permute-start.2 = (bf16[6,6,512]{2,1,0:T(8,128)(2,1)S(1)}, bf16[6,6,512]{2,1,0:T(8,128)(2,1)S(1)}, u32[]{:S(2)}, u32[]{:S(2)}) collective-permute-start(bf16[6,6,512]{2,1,0:T(8,128)(2,1)S(1)} %get-tuple-element.32), channel_id=1, source_target_pairs={{9,0},{10,1},{11,2},{12,3},{13,4},{14,5},{15,6},{17,8},{18,9},{19,... | collective-permute-start | bytes 110600 | tf_op jit(solution)/shard_map/ppermute | solution.py:330
  9.0 9.5 %collective-permute-start.3 = (bf16[6,6,512]{2,1,0:T(8,128)(2,1)S(1)}, bf16[6,6,512]{2,1,0:T(8,128)(2,1)S(1)}, u32[]{:S(2)}, u32[]{:S(2)}) collective-permute-start(bf16[6,6,512]{2,1,0:T(8,128)(2,1)S(1)} %get-tuple-element.33), channel_id=1, source_target_pairs={{0,7},{8,15},{16,23},{24,31}} | collective-permute-start | bytes 110600 | tf_op jit(solution)/shard_map/ppermute | solution.py:330
  18.5 1.3 %collective-permute-start.4 = (bf16[6,6,512]{2,1,0:T(8,128)(2,1)S(1)}, bf16[6,6,512]{2,1,0:T(8,128)(2,1)S(1)}, u32[]{:S(2)}, u32[]{:S(2)}) collective-permute-start(bf16[6,6,512]{2,1,0:T(8,128)(2,1)S(1)} %get-tuple-element.34), channel_id=1, source_target_pairs={{8,7},{16,15},{24,23},{0,31}} | collective-permute-start | bytes 110600 | tf_op jit(solution)/shard_map/ppermute | solution.py:330
  19.8 0.0 collective-permute-done.refs_1_
  19.8 0.0 collective-permute-done.1.refs_2_
  19.9 0.0 collective-permute-done.2.refs_3_
  19.9 0.4 %collective-permute-done.3.refs_4_ = bf16[6,6,512]{2,1,0:T(8,128)(2,1)S(1)} collective-permute-done((bf16[6,6,512]{2,1,0:T(8,128)(2,1)S(1)}, bf16[6,6,512]{2,1,0:T(8,128)(2,1)S(1)}, u32[]{:S(2)}, u32[]{:S(2)}) %collective-permute-start.3) | collective-permute-done | bytes 36896 | tf_op jit(solution)/shard_map/ppermute | solution.py:330
  20.3 1.3 %collective-permute-done.4.refs_5_ = bf16[6,6,512]{2,1,0:T(8,128)(2,1)S(1)} collective-permute-done((bf16[6,6,512]{2,1,0:T(8,128)(2,1)S(1)}, bf16[6,6,512]{2,1,0:T(8,128)(2,1)S(1)}, u32[]{:S(2)}, u32[]{:S(2)}) %collective-permute-start.4) | collective-permute-done | bytes 36896 | tf_op jit(solution)/shard_map/ppermute | solution.py:330
  21.6 0.0 copy-done
  21.6 0.0 copy-done.1
  21.6 0.0 copy-done.2
  21.6 0.0 copy-done.3
  21.6 2.4 %shard_map.94 = (bf16[6,6,512]{2,1,0:T(8,128)(2,1)S(1)}, bf16[6,6,512]{2,1,0:T(8,128)(2,1)S(1)}, bf16[6,6,512]{2,1,0:T(8,128)(2,1)S(1)}, bf16[6,6,512]{2,1,0:T(8,128)(2,1)S(1)}) custom-call(bf16[6,6,512]{2,1,0:T(8,128)(2,1)S(1)} %get-tuple-element.29.refs_0_, bf16[6,6,512]{2,1,0:T(8,128)(2,1)S(1)} %collective-permute-done.refs_1_, ...), custom_call_target="tpu_custom_call" | custom-call | flops 400000000 | bytes 2500000 | tf_op jit(solution)/shard_map/pallas_call | solution.py:311
  24.0 1.3 %collective-permute-start.6 = (bf16[6,6,512]{2,1,0:T(8,128)(2,1)S(1)}, bf16[6,6,512]{2,1,0:T(8,128)(2,1)S(1)}, u32[]{:S(2)}, u32[]{:S(2)}) collective-permute-start(bf16[6,6,512]{2,1,0:T(8,128)(2,1)S(1)} %get-tuple-element.40), channel_id=1, source_target_pairs={{24,1},{25,2},{26,3},{27,4},{28,5},{29,6},{30,7},{0,9},{1,10},{2,1... | collective-permute-start | bytes 110600 | tf_op jit(solution)/shard_map/ppermute | solution.py:330
  25.3 1.3 %collective-permute-start.5 = (bf16[6,6,512]{2,1,0:T(8,128)(2,1)S(1)}, bf16[6,6,512]{2,1,0:T(8,128)(2,1)S(1)}, u32[]{:S(2)}, u32[]{:S(2)}) collective-permute-start(bf16[6,6,512]{2,1,0:T(8,128)(2,1)S(1)} %get-tuple-element.35), channel_id=1, source_target_pairs={{31,0},{7,8},{15,16},{23,24}} | collective-permute-start | bytes 110600 | tf_op jit(solution)/shard_map/ppermute | solution.py:330
  26.6 1.3 %collective-permute-start.9 = (bf16[6,6,512]{2,1,0:T(8,128)(2,1)S(1)}, bf16[6,6,512]{2,1,0:T(8,128)(2,1)S(1)}, u32[]{:S(2)}, u32[]{:S(2)}) collective-permute-start(bf16[6,6,512]{2,1,0:T(8,128)(2,1)S(1)} %get-tuple-element.43), channel_id=1, source_target_pairs={{0,1},{1,2},{2,3},{3,4},{4,5},{5,6},{6,7},{8,9},{9,10},{10,11},{11... | collective-permute-start | bytes 110600 | tf_op jit(solution)/shard_map/ppermute | solution.py:330
  27.9 1.3 %collective-permute-start.8 = (bf16[6,6,512]{2,1,0:T(8,128)(2,1)S(1)}, bf16[6,6,512]{2,1,0:T(8,128)(2,1)S(1)}, u32[]{:S(2)}, u32[]{:S(2)}) collective-permute-start(bf16[6,6,512]{2,1,0:T(8,128)(2,1)S(1)} %get-tuple-element.42), channel_id=1, source_target_pairs={{7,0},{15,8},{23,16},{31,24}} | collective-permute-start | bytes 110600 | tf_op jit(solution)/shard_map/ppermute | solution.py:330
  29.2 0.1 collective-permute-start.7
  29.3 0.0 collective-permute-done.6
  29.3 5.0 %collective-permute-done.5 = bf16[6,6,512]{2,1,0:T(8,128)(2,1)S(1)} collective-permute-done((bf16[6,6,512]{2,1,0:T(8,128)(2,1)S(1)}, bf16[6,6,512]{2,1,0:T(8,128)(2,1)S(1)}, u32[]{:S(2)}, u32[]{:S(2)}) %collective-permute-start.5) | collective-permute-done | bytes 36896 | tf_op jit(solution)/shard_map/ppermute | solution.py:330
  34.3 0.0 collective-permute-done.9
  34.3 2.6 %collective-permute-done.8 = bf16[6,6,512]{2,1,0:T(8,128)(2,1)S(1)} collective-permute-done((bf16[6,6,512]{2,1,0:T(8,128)(2,1)S(1)}, bf16[6,6,512]{2,1,0:T(8,128)(2,1)S(1)}, u32[]{:S(2)}, u32[]{:S(2)}) %collective-permute-start.8) | collective-permute-done | bytes 36896 | tf_op jit(solution)/shard_map/ppermute | solution.py:330
  36.9 0.0 collective-permute-done.7
  36.9 0.7 %maximum_bitcast_fusion = bf16[1,12,12,512]{3,2,1,0:T(8,128)(2,1)} fusion(bf16[6,6,512]{2,1,0:T(8,128)(2,1)S(1)} %get-tuple-element.44, bf16[6,6,512]{2,1,0:T(8,128)(2,1)S(1)} %broadcast_select_fusion, bf16[6,6,512]{2,1,0:T(8,128)(2,1)S(1)} %collective-permute-done.7, bf16[6,6,512]{2,1,0:T(8,128)(2,1)S(1)} %broadcast_select_fusion.1), kind=kLoop, calls=%fused_computation | loop fusion | flops 589824 | bytes 294912 | tf_op jit(solution)/shard_map/broadcast_in_dim | solution.py:366
  (3 shorter events, 0.0 us)
Async XLA Ops:
  3.8 17.8 %copy-start = (bf16[512,1536]{1,0:T(8,128)(2,1)S(1)}, bf16[512,1536]{1,0:T(8,128)(2,1)}, u32[]{:S(2)}) copy-start(bf16[512,1536]{1,0:T(8,128)(2,1)} %refs_8_.3) | copy-start | bytes 4718596
  3.8 17.8 %copy-start.1 = (bf16[512,512]{1,0:T(8,128)(2,1)S(1)}, bf16[512,512]{1,0:T(8,128)(2,1)}, u32[]{:S(2)}) copy-start(bf16[512,512]{1,0:T(8,128)(2,1)} %refs_9_.3) | copy-start | bytes 1572868
  3.8 17.7 %copy-start.2 = (f32[1,16,529]{2,1,0:T(8,128)S(1)}, f32[1,16,529]{2,1,0:T(8,128)}, u32[]{:S(2)}) copy-start(f32[1,16,529]{2,1,0:T(8,128)} %refs_6_.3) | copy-start | bytes 101572
  3.8 17.7 %copy-start.3 = (f32[512]{0:T(512)S(1)}, f32[512]{0:T(512)}, u32[]{:S(2)}) copy-start(f32[512]{0:T(512)} %param.14) | copy-start | bytes 6148
  3.9 15.9 %collective-permute-start = (bf16[6,6,512]{2,1,0:T(8,128)(2,1)S(1)}, bf16[6,6,512]{2,1,0:T(8,128)(2,1)S(1)}, u32[]{:S(2)}, u32[]{:S(2)}) collective-permute-start(bf16[6,6,512]{2,1,0:T(8,128)(2,1)S(1)} %get-tuple-element.30), channel_id=1, source_target_pairs={{8,0},{9,1},{10,2},{11,3},{12,4},{13,5},{14,6},{15,7},{16,8},{17,9... | collective-permute-start | bytes 110600 | tf_op jit(solution)/shard_map/ppermute | solution.py:330
  6.4 13.4 %collective-permute-start.1 = (bf16[6,6,512]{2,1,0:T(8,128)(2,1)S(1)}, bf16[6,6,512]{2,1,0:T(8,128)(2,1)S(1)}, u32[]{:S(2)}, u32[]{:S(2)}) collective-permute-start(bf16[6,6,512]{2,1,0:T(8,128)(2,1)S(1)} %get-tuple-element.31), channel_id=1, source_target_pairs={{1,0},{2,1},{3,2},{4,3},{5,4},{6,5},{7,6},{9,8},{10,9},{11,10},{12... | collective-permute-start | bytes 110600 | tf_op jit(solution)/shard_map/ppermute | solution.py:330
  7.7 12.2 %collective-permute-start.2 = (bf16[6,6,512]{2,1,0:T(8,128)(2,1)S(1)}, bf16[6,6,512]{2,1,0:T(8,128)(2,1)S(1)}, u32[]{:S(2)}, u32[]{:S(2)}) collective-permute-start(bf16[6,6,512]{2,1,0:T(8,128)(2,1)S(1)} %get-tuple-element.32), channel_id=1, source_target_pairs={{9,0},{10,1},{11,2},{12,3},{13,4},{14,5},{15,6},{17,8},{18,9},{19,... | collective-permute-start | bytes 110600 | tf_op jit(solution)/shard_map/ppermute | solution.py:330
  9.0 11.3 %collective-permute-start.3 = (bf16[6,6,512]{2,1,0:T(8,128)(2,1)S(1)}, bf16[6,6,512]{2,1,0:T(8,128)(2,1)S(1)}, u32[]{:S(2)}, u32[]{:S(2)}) collective-permute-start(bf16[6,6,512]{2,1,0:T(8,128)(2,1)S(1)} %get-tuple-element.33), channel_id=1, source_target_pairs={{0,7},{8,15},{16,23},{24,31}} | collective-permute-start | bytes 110600 | tf_op jit(solution)/shard_map/ppermute | solution.py:330
  18.5 3.0 %collective-permute-start.4 = (bf16[6,6,512]{2,1,0:T(8,128)(2,1)S(1)}, bf16[6,6,512]{2,1,0:T(8,128)(2,1)S(1)}, u32[]{:S(2)}, u32[]{:S(2)}) collective-permute-start(bf16[6,6,512]{2,1,0:T(8,128)(2,1)S(1)} %get-tuple-element.34), channel_id=1, source_target_pairs={{8,7},{16,15},{24,23},{0,31}} | collective-permute-start | bytes 110600 | tf_op jit(solution)/shard_map/ppermute | solution.py:330
  24.0 5.3 %collective-permute-start.6 = (bf16[6,6,512]{2,1,0:T(8,128)(2,1)S(1)}, bf16[6,6,512]{2,1,0:T(8,128)(2,1)S(1)}, u32[]{:S(2)}, u32[]{:S(2)}) collective-permute-start(bf16[6,6,512]{2,1,0:T(8,128)(2,1)S(1)} %get-tuple-element.40), channel_id=1, source_target_pairs={{24,1},{25,2},{26,3},{27,4},{28,5},{29,6},{30,7},{0,9},{1,10},{2,1... | collective-permute-start | bytes 110600 | tf_op jit(solution)/shard_map/ppermute | solution.py:330
  25.3 9.0 %collective-permute-start.5 = (bf16[6,6,512]{2,1,0:T(8,128)(2,1)S(1)}, bf16[6,6,512]{2,1,0:T(8,128)(2,1)S(1)}, u32[]{:S(2)}, u32[]{:S(2)}) collective-permute-start(bf16[6,6,512]{2,1,0:T(8,128)(2,1)S(1)} %get-tuple-element.35), channel_id=1, source_target_pairs={{31,0},{7,8},{15,16},{23,24}} | collective-permute-start | bytes 110600 | tf_op jit(solution)/shard_map/ppermute | solution.py:330
  26.6 7.7 %collective-permute-start.9 = (bf16[6,6,512]{2,1,0:T(8,128)(2,1)S(1)}, bf16[6,6,512]{2,1,0:T(8,128)(2,1)S(1)}, u32[]{:S(2)}, u32[]{:S(2)}) collective-permute-start(bf16[6,6,512]{2,1,0:T(8,128)(2,1)S(1)} %get-tuple-element.43), channel_id=1, source_target_pairs={{0,1},{1,2},{2,3},{3,4},{4,5},{5,6},{6,7},{8,9},{9,10},{10,11},{11... | collective-permute-start | bytes 110600 | tf_op jit(solution)/shard_map/ppermute | solution.py:330
  27.9 9.0 %collective-permute-start.8 = (bf16[6,6,512]{2,1,0:T(8,128)(2,1)S(1)}, bf16[6,6,512]{2,1,0:T(8,128)(2,1)S(1)}, u32[]{:S(2)}, u32[]{:S(2)}) collective-permute-start(bf16[6,6,512]{2,1,0:T(8,128)(2,1)S(1)} %get-tuple-element.42), channel_id=1, source_target_pairs={{7,0},{15,8},{23,16},{31,24}} | collective-permute-start | bytes 110600 | tf_op jit(solution)/shard_map/ppermute | solution.py:330
  29.2 7.7 %collective-permute-start.7 = (bf16[6,6,512]{2,1,0:T(8,128)(2,1)S(1)}, bf16[6,6,512]{2,1,0:T(8,128)(2,1)S(1)}, u32[]{:S(2)}, u32[]{:S(2)}) collective-permute-start(bf16[6,6,512]{2,1,0:T(8,128)(2,1)S(1)} %get-tuple-element.41), channel_id=1, source_target_pairs={{24,0},{25,1},{26,2},{27,3},{28,4},{29,5},{30,6},{31,7},{0,8},{1,9... | collective-permute-start | bytes 110600 | tf_op jit(solution)/shard_map/ppermute | solution.py:330

commit v5 on v3

--- a/solution.py
+++ b/solution.py
@@ -1,4 +1,5 @@
 import functools
+import math
 
 import jax
 import jax.numpy as jnp
@@ -6,6 +7,7 @@
 from jax.experimental import pallas as pl
 from jax.experimental.pallas import tpu as pltpu
 from jax.sharding import PartitionSpec as P
+
 
 HEADS = 16
 WH = 12
@@ -18,6 +20,7 @@
 HALF_C = WW // 2
 REST = WW - SUB
 NEG = -1e30
+LOG2E = math.log2(math.e)
 F32 = jnp.float32
 BF16 = jnp.bfloat16
 
@@ -59,7 +62,7 @@
                     rows[s] = jnp.broadcast_to(tab[h : h + 1, s * LANES : (s + 1) * LANES], (SUB, LANES))
                 taken = jnp.take_along_axis(rows[s], inner, axis=1)
                 value = taken if value is None else jnp.where(outer == s, taken, value)
-            strips[h, tile, :, k * LANES : (k + 1) * LANES] = value
+            strips[h, tile, :, k * LANES : (k + 1) * LANES] = value * LOG2E
 
 
 def bias_tiles(strips, h):
@@ -129,7 +132,7 @@
         tiles.append(s)
     top = functools.reduce(jnp.maximum, tiles)
     top = jnp.max(top, axis=0, keepdims=True)
-    tiles = [jnp.exp(s - top) for s in tiles]
+    tiles = [jnp.exp2(s - top) for s in tiles]
     total = functools.reduce(jnp.add, tiles)
     inverse = 1.0 / jnp.sum(total, axis=0, keepdims=True)
     for u in range(0, count, 2):
@@ -137,11 +140,12 @@
         probs[u * SUB : (u + 2) * SUB, at : at + LANES] = pair.astype(BF16)
 
 
-def attend(xs, ys, gain, weights, strips, probs, polar):
+def attend(xs, ys, gain, weights, bias, probs, polar):
     width = xs.shape[-1]
     head_dim = width // HEADS
     group = LANES // head_dim
     per_head = WH * PITCH
+    tiles_of = bias()
     x = xs[...].reshape(per_head, width)
     mean = jnp.mean(x, axis=-1, keepdims=True)
     centred = x - mean
@@ -149,7 +153,7 @@
     normed = (centred * lax.rsqrt(var + 1e-05) * gain[...]).astype(BF16)
     wqkv = weights(0)
     mixed = jnp.dot(normed, wqkv[...], preferred_element_type=F32)
-    q_hi, q_lo = split(mixed[:, :width] * head_dim ** (-0.5))
+    q_hi, q_lo = split(mixed[:, :width] * (head_dim ** (-0.5) * LOG2E))
     k_hi, k_lo = split(compact(mixed[:, width : 2 * width]))
     values = compact(mixed[:, 2 * width :]).astype(BF16)
     lane = iota((1, LANES), 1)
@@ -166,18 +170,7 @@
         right = jnp.concatenate(rights, axis=0)
         return lax.dot_general(left, right, (((1,), (1,)), ((), ())), preferred_element_type=F32)
 
-    outs = []
-    groups = HEADS // group
-    ahead = product(0)
-    for g in range(groups):
-        scores = ahead
-        if g + 1 < groups:
-            ahead = product(g + 1)
-        for i in range(0, group, 2):
-            bias = bias_tiles(strips, g * group + i)
-            for t in range(len(bias)):
-                at = i * per_head + t * LANES
-                soft(scores[:, at : at + LANES], bias[t], masks and masks[t], probs.at[g], at)
+    def gather(g):
         part = slice(g * LANES, (g + 1) * LANES)
         mixed_v = lax.dot_general(
             values[:, part], probs[g], (((0,), (0,)), ((), ())), preferred_element_type=F32
@@ -188,7 +181,23 @@
             first, by = divmod(i * per_head, LANES)
             own = mixed_v[rows, first * LANES : (first + 2) * LANES]
             heads_out.append(pltpu.roll(own, 2 * LANES - by, 1) if by else own)
-        outs.append(jnp.concatenate(heads_out, axis=0).T)
+        return jnp.concatenate(heads_out, axis=0).T
+
+    outs = []
+    groups = HEADS // group
+    ahead = product(0)
+    for g in range(groups):
+        scores = ahead
+        if g + 1 < groups:
+            ahead = product(g + 1)
+        if g:
+            outs.append(gather(g - 1))
+        for i in range(0, group, 2):
+            tiles = tiles_of(g * group + i)
+            for t in range(len(tiles)):
+                at = i * per_head + t * LANES
+                soft(scores[:, at : at + LANES], tiles[t], masks and masks[t], probs.at[g], at)
+    outs.append(gather(groups - 1))
     heads_out = jnp.concatenate(outs, axis=1)[:per_head].astype(BF16)
     wproj = weights(1)
     branch = jnp.dot(heads_out, wproj[...], preferred_element_type=F32)
@@ -203,29 +212,41 @@
             at += 1
 
 
-def first_kernel(tokens, table, gain, wqkv, wproj, nw, ne, sw, se, xs, ys, tab, strips, probs, *here):
+def first_kernel(tokens, table, gain, wqkv, wproj, nw, ne, sw, se, xs, ys, probs, tab, strips, *here):
     here, sems = here[:-1], here[-1]
     copies = [
-        pltpu.make_async_copy(a, b, sems.at[i]) for i, (a, b) in enumerate(zip((table, tokens, gain, wqkv, wproj), here))
+        pltpu.make_async_copy(a, b, sems.at[i])
+        for i, (a, b) in enumerate(zip((tokens, gain, wqkv, table, wproj), here))
     ]
     for copy in copies:
         copy.start()
     xs[:, WW:, :] = jnp.zeros((WH, PITCH - WW, xs.shape[-1]), F32)
     copies[0].wait()
-    bias_strips(here[0], tab, strips)
+    xs[:, :WW, :] = here[0][0].astype(F32)
     copies[1].wait()
-    xs[:, :WW, :] = here[1][0].astype(F32)
-    copies[2].wait()
 
     def weights(i):
-        copies[3 + i].wait()
-        return here[3 + i]
-
-    attend(xs, ys, here[2], weights, strips, probs, None)
+        copies[2 * i + 2].wait()
+        return here[2 * i + 2]
+
+    def bias():
+        copies[3].wait()
+        bias_strips(here[3], tab, strips)
+        return functools.partial(bias_tiles, strips)
+
+    attend(xs, ys, here[1], weights, bias, probs, None)
     quadrants(ys, (nw, ne, sw, se))
 
 
-def second_kernel(nw_in, ne_in, sw_in, se_in, table, gain, wqkv, wproj, nw, ne, sw, se, xs, ys, tab, strips, probs):
+def bias_kernel(table, out, tab, strips):
+    bias_strips(table, tab, strips)
+    for pair in range(out.shape[0]):
+        for t, tiles in enumerate(bias_tiles(strips, 2 * pair)):
+            for u, tile in enumerate(tiles):
+                out[pair, t, u] = tile
+
+
+def second_kernel(nw_in, ne_in, sw_in, se_in, bias, gain, wqkv, wproj, nw, ne, sw, se, xs, ys, probs):
     polar = lax.axis_index("lat") == lax.axis_size("lat") - 1
     xs[:, WW:, :] = jnp.zeros((WH, PITCH - WW, xs.shape[-1]), F32)
     at = 0
@@ -234,37 +255,60 @@
         for c in (0, HALF_C):
             xs[r : r + HALF_R, c : c + HALF_C, :] = pieces[at][...].astype(F32)
             at += 1
-    bias_strips(table, tab, strips)
-    attend(xs, ys, gain, lambda i: (wqkv, wproj)[i], strips, probs, polar)
+
+    def tiles_of(h):
+        return [[bias[h // 2, t, u] for u in range(bias.shape[2])] for t in range(bias.shape[1])]
+
+    attend(xs, ys, gain, lambda i: (wqkv, wproj)[i], lambda: tiles_of, probs, polar)
     quadrants(ys, (nw, ne, sw, se))
 
 
-def block(kernel, pieces, table, gain, wqkv, wproj, fetch):
+VMEM = pl.BlockSpec(memory_space=pltpu.VMEM)
+
+
+def bias_room(table):
+    _, heads, count = table.shape
+    lanes = -(-count // LANES) * LANES
+    return [pltpu.VMEM((heads, lanes), F32), pltpu.VMEM((heads, 2, SUB, 3 * LANES), F32)]
+
+
+def expand(table):
+    heads = table.shape[1]
+    lane_tiles = 2 * WH * PITCH // LANES
+    shape = (heads // 2, lane_tiles, WH * WW // SUB, SUB, LANES)
+    return pl.pallas_call(
+        bias_kernel,
+        out_shape=jax.ShapeDtypeStruct(shape, F32),
+        in_specs=[VMEM],
+        out_specs=VMEM,
+        scratch_shapes=bias_room(table),
+        compiler_params=pltpu.CompilerParams(vmem_limit_bytes=8 << 20),
+        cost_estimate=pl.CostEstimate(flops=2_000_000, bytes_accessed=1_800_000, transcendentals=0),
+    )(table)
+
+
+def block(kernel, pieces, bias, gain, wqkv, wproj, fetch):
     width = wproj.shape[0]
-    heads, count = table.shape[1:]
-    lanes = -(-count // LANES) * LANES
-    group = LANES * heads // width
+    group = LANES * HEADS // width
     piece = jax.ShapeDtypeStruct((HALF_R, HALF_C, width), BF16)
-    args = (*pieces, table, gain.reshape(1, width), wqkv, wproj)
-    vmem = pl.BlockSpec(memory_space=pltpu.VMEM)
+    args = (*pieces, bias, gain.reshape(1, width), wqkv, wproj)
     scratch = [
         pltpu.VMEM((WH, PITCH, width), F32),
         pltpu.VMEM((WH, PITCH, width), F32),
-        pltpu.VMEM((heads, lanes), F32),
-        pltpu.VMEM((heads, 2, SUB, 3 * LANES), F32),
-        pltpu.VMEM((heads // group, WH * WW, group * WH * PITCH), BF16),
+        pltpu.VMEM((HEADS // group, WH * WW, group * WH * PITCH), BF16),
     ]
     if fetch:
-        order = (args[1], args[0], *args[2:])
+        order = (args[0], args[2], args[3], args[1], args[4])
+        scratch += bias_room(bias)
         scratch += [pltpu.VMEM(a.shape, a.dtype) for a in order]
         scratch += [pltpu.SemaphoreType.DMA((len(order),))]
         args = tuple(pltpu.with_memory_space_constraint(a, pltpu.HBM) for a in args)
-    source = pl.BlockSpec(memory_space=pltpu.HBM) if fetch else vmem
+    source = pl.BlockSpec(memory_space=pltpu.HBM) if fetch else VMEM
     return pl.pallas_call(
         kernel,
         out_shape=(piece,) * 4,
         in_specs=[source] * len(args),
-        out_specs=(vmem,) * 4,
+        out_specs=(VMEM,) * 4,
         scratch_shapes=scratch,
         compiler_params=pltpu.CompilerParams(vmem_limit_bytes=24 << 20),
         cost_estimate=pl.CostEstimate(flops=400_000_000, bytes_accessed=2_500_000, transcendentals=600_000),
@@ -291,8 +335,15 @@
     bias_second,
 ):
     nw, ne, sw, se = block(first_kernel, (tokens,), bias_first, gain_first, qkv_first, proj_first, True)
-    window = (se, moved(sw, 0, 1), moved(ne, 1, 0), moved(nw, 1, 1))
-    nw, ne, sw, se = block(second_kernel, window, bias_second, gain_second, qkv_second, proj_second, False)
+    sw, qkv_second, proj_second, bias_second = lax.optimization_barrier(
+        (sw, qkv_second, proj_second, bias_second)
+    )
+    bias = expand(bias_second)
+    east = moved(sw, 0, 1)
+    south = moved(ne, 1, 0)
+    corner = moved(nw, 1, 1)
+    window = (se, east, south, corner)
+    nw, ne, sw, se = block(second_kernel, window, bias, gain_second, qkv_second, proj_second, False)
     west, north, corner = moved(ne, 0, -1), moved(sw, -1, 0), moved(se, -1, -1)
     upper = jnp.concatenate([corner, north], axis=1)
     lower = jnp.concatenate([west, nw], axis=1)

time: 25.8 us -> 26 us (level)
  Pallas kernels: 6.3 us -> 7.58 us
  waiting for transfers between devices: 10.1 us -> 8.92 us
    pallas_call x0 -> x1, Pallas kernels: none -> 1.15 us  [expand(): pl.pallas_call(bias_kernel, out_shape=jax.ShapeDtypeStruct(shape, F32), i...]
    ppermute x6, waiting for transfers between devices: 10.1 us -> 8.92 us  [moved(): return lax.ppermute(piece, ('lat', 'lon'), route)]
  transfers between devices with their start and end apart: 6 -> 6, of which waited for: 5 -> 3; matrix products, arithmetic and copies ran while one was open for 0% -> 0% of each run, Pallas kernels for 0% -> 4%
where the time goes in v5:
time: 26 us; the launch traced here: 25.8 us
  waiting for transfers between devices  8.92 us (34%)
  starting transfers between devices  8.51 us (33%)
  Pallas kernels  7.58 us (29%)
  other arithmetic  0.74 us (3%)
    ppermute x6, waiting for transfers between devices, moved(): return lax.ppermute(piece, ('lat', 'lon'), route)  8.92 us
    ppermute x6, starting transfers between devices, moved(): return lax.ppermute(piece, ('lat', 'lon'), route)  8.51 us
    pallas_call x2, Pallas kernels, block(): pl.pallas_call(kernel, out_shape=(piece,) * 4, in_specs=[source] * len(ar...  6.44 us
    pallas_call x1, Pallas kernels, expand(): pl.pallas_call(bias_kernel, out_shape=jax.ShapeDtypeStruct(shape, F32), i...  1.15 us
    broadcast_in_dim x1, other arithmetic, shards(): return jnp.concatenate([upper, lower], axis=0)[None]  0.74 us
  transfers between devices with their start and end apart: 6, of which 3 were waited for; matrix products, arithmetic and copies ran while one was open for 0% of the time, Pallas kernels for 4%

profile of v5, /device:TPU:0, one launch (start us, length us, event | category | flops | bytes accessed | tf_op | source)
XLA Modules:
  0.0 25.8 jit_solution(1329353879410297715)
XLA Ops:
  0.0 0.0 copy-start.2
  0.0 0.0 copy-start
  0.0 0.0 copy-start.1
  0.0 0.0 copy-start.3
  0.0 4.3 %shard_map.91 = (bf16[6,6,512]{2,1,0:T(8,128)(2,1)S(1)}, bf16[6,6,512]{2,1,0:T(8,128)(2,1)S(1)}, bf16[6,6,512]{2,1,0:T(8,128)(2,1)S(1)}, bf16[6,6,512]{2,1,0:T(8,128)(2,1)S(1)}) custom-call(bf16[1,12,12,512]{3,2,1,0:T(8,128)(2,1)} %tokens.1, f32[1,16,529]{2,1,0:T(8,128)} %table.1, f32[1,512]{1,0:T(1,128)} %bitcast.5, bf16[512,1536]{1,0:T(8,128)(2,1)} %wqkv.1, ...), custom_call_target="tpu_custom_call" | custom-call | flops 400000000 | bytes 2500000 | tf_op jit(solution)/shard_map/pallas_call | solution.py:307
  4.3 6.1 %collective-permute-start = (bf16[6,6,512]{2,1,0:T(8,128)(2,1)S(1)}, bf16[6,6,512]{2,1,0:T(8,128)(2,1)S(1)}, u32[]{:S(2)}, u32[]{:S(2)}) collective-permute-start(bf16[6,6,512]{2,1,0:T(8,128)(2,1)S(1)} %get-tuple-element.19), channel_id=1, source_target_pairs={{1,0},{2,1},{3,2},{4,3},{5,4},{6,5},{7,6},{0,7},{9,8},{10,9},{11,1... | collective-permute-start | bytes 110600 | tf_op jit(solution)/shard_map/ppermute | solution.py:323
  10.4 0.7 %collective-permute-start.1 = (bf16[6,6,512]{2,1,0:T(8,128)(2,1)S(1)}, bf16[6,6,512]{2,1,0:T(8,128)(2,1)S(1)}, u32[]{:S(2)}, u32[]{:S(2)}) collective-permute-start(bf16[6,6,512]{2,1,0:T(8,128)(2,1)S(1)} %get-tuple-element.20), channel_id=1, source_target_pairs={{8,0},{9,1},{10,2},{11,3},{12,4},{13,5},{14,6},{15,7},{16,8},{17,9... | collective-permute-start | bytes 110600 | tf_op jit(solution)/shard_map/ppermute | solution.py:323
  11.1 0.9 %collective-permute-start.2 = (bf16[6,6,512]{2,1,0:T(8,128)(2,1)S(1)}, bf16[6,6,512]{2,1,0:T(8,128)(2,1)S(1)}, u32[]{:S(2)}, u32[]{:S(2)}) collective-permute-start(bf16[6,6,512]{2,1,0:T(8,128)(2,1)S(1)} %get-tuple-element.21), channel_id=1, source_target_pairs={{9,0},{10,1},{11,2},{12,3},{13,4},{14,5},{15,6},{8,7},{17,8},{18,9... | collective-permute-start | bytes 110600 | tf_op jit(solution)/shard_map/ppermute | solution.py:323
  12.0 0.0 copy-done.2
  12.0 1.1 %shard_map.92.bias = f32[8,3,18,8,128]{4,3,2,1,0:T(8,128)S(1)} custom-call(f32[1,16,529]{2,1,0:T(8,128)S(1)} %copy-done.2), custom_call_target="tpu_custom_call" | custom-call | flops 2000000 | bytes 1800000 | tf_op jit(solution)/shard_map/pallas_call | solution.py:279
  13.1 0.0 collective-permute-done.ne_in
  13.1 0.0 collective-permute-done.1.sw_in
  13.1 1.4 %collective-permute-done.2.se_in = bf16[6,6,512]{2,1,0:T(8,128)(2,1)S(1)} collective-permute-done((bf16[6,6,512]{2,1,0:T(8,128)(2,1)S(1)}, bf16[6,6,512]{2,1,0:T(8,128)(2,1)S(1)}, u32[]{:S(2)}, u32[]{:S(2)}) %collective-permute-start.2) | collective-permute-done | bytes 36896 | tf_op jit(solution)/shard_map/ppermute | solution.py:323
  14.6 0.0 copy-done
  14.6 0.0 copy-done.1
  14.6 0.0 copy-done.3
  14.6 2.1 %shard_map.93 = (bf16[6,6,512]{2,1,0:T(8,128)(2,1)S(1)}, bf16[6,6,512]{2,1,0:T(8,128)(2,1)S(1)}, bf16[6,6,512]{2,1,0:T(8,128)(2,1)S(1)}, bf16[6,6,512]{2,1,0:T(8,128)(2,1)S(1)}) custom-call(bf16[6,6,512]{2,1,0:T(8,128)(2,1)S(1)} %get-tuple-element.17.nw_in, bf16[6,6,512]{2,1,0:T(8,128)(2,1)S(1)} %collective-permute-done.ne_in, ...), custom_call_target="tpu_custom_call" | custom-call | flops 400000000 | bytes 2500000 | tf_op jit(solution)/shard_map/pallas_call | solution.py:307
  16.7 0.1 collective-permute-start.3
  16.8 0.8 %collective-permute-start.4 = (bf16[6,6,512]{2,1,0:T(8,128)(2,1)S(1)}, bf16[6,6,512]{2,1,0:T(8,128)(2,1)S(1)}, u32[]{:S(2)}, u32[]{:S(2)}) collective-permute-start(bf16[6,6,512]{2,1,0:T(8,128)(2,1)S(1)} %get-tuple-element.26), channel_id=1, source_target_pairs={{24,0},{25,1},{26,2},{27,3},{28,4},{29,5},{30,6},{31,7},{0,8},{1,9... | collective-permute-start | bytes 110600 | tf_op jit(solution)/shard_map/ppermute | solution.py:323
  17.6 0.0 collective-permute-start.5
  17.6 6.8 %collective-permute-done.3 = bf16[6,6,512]{2,1,0:T(8,128)(2,1)S(1)} collective-permute-done((bf16[6,6,512]{2,1,0:T(8,128)(2,1)S(1)}, bf16[6,6,512]{2,1,0:T(8,128)(2,1)S(1)}, u32[]{:S(2)}, u32[]{:S(2)}) %collective-permute-start.3) | collective-permute-done | bytes 36896 | tf_op jit(solution)/shard_map/ppermute | solution.py:323
  24.4 0.0 collective-permute-done.4
  24.4 0.7 %collective-permute-done.5 = bf16[6,6,512]{2,1,0:T(8,128)(2,1)S(1)} collective-permute-done((bf16[6,6,512]{2,1,0:T(8,128)(2,1)S(1)}, bf16[6,6,512]{2,1,0:T(8,128)(2,1)S(1)}, u32[]{:S(2)}, u32[]{:S(2)}) %collective-permute-start.5) | collective-permute-done | bytes 36896 | tf_op jit(solution)/shard_map/ppermute | solution.py:323
  25.1 0.7 %maximum_bitcast_fusion = bf16[1,12,12,512]{3,2,1,0:T(8,128)(2,1)} fusion(bf16[6,6,512]{2,1,0:T(8,128)(2,1)S(1)} %get-tuple-element.28, bf16[6,6,512]{2,1,0:T(8,128)(2,1)S(1)} %collective-permute-done.5, bf16[6,6,512]{2,1,0:T(8,128)(2,1)S(1)} %collective-permute-done.4, bf16[6,6,512]{2,1,0:T(8,128)(2,1)S(1)} %collective-permute-done.3), kind=kLoop, calls=%fused_computation | loop fusion | flops 589824 | bytes 294912 | tf_op jit(solution)/shard_map/broadcast_in_dim | solution.py:350
Async XLA Ops:
  0.0 12.0 %copy-start.2 = (f32[1,16,529]{2,1,0:T(8,128)S(1)}, f32[1,16,529]{2,1,0:T(8,128)}, u32[]{:S(2)}) copy-start(f32[1,16,529]{2,1,0:T(8,128)} %table.2) | copy-start | bytes 101572
  0.0 14.6 %copy-start = (bf16[512,1536]{1,0:T(8,128)(2,1)S(1)}, bf16[512,1536]{1,0:T(8,128)(2,1)}, u32[]{:S(2)}) copy-start(bf16[512,1536]{1,0:T(8,128)(2,1)} %wqkv.2) | copy-start | bytes 4718596
  0.0 14.6 %copy-start.1 = (bf16[512,512]{1,0:T(8,128)(2,1)S(1)}, bf16[512,512]{1,0:T(8,128)(2,1)}, u32[]{:S(2)}) copy-start(bf16[512,512]{1,0:T(8,128)(2,1)} %wproj.2) | copy-start | bytes 1572868
  0.0 14.6 %copy-start.3 = (f32[512]{0:T(512)S(1)}, f32[512]{0:T(512)}, u32[]{:S(2)}) copy-start(f32[512]{0:T(512)} %param.14) | copy-start | bytes 6148
  4.3 8.8 %collective-permute-start = (bf16[6,6,512]{2,1,0:T(8,128)(2,1)S(1)}, bf16[6,6,512]{2,1,0:T(8,128)(2,1)S(1)}, u32[]{:S(2)}, u32[]{:S(2)}) collective-permute-start(bf16[6,6,512]{2,1,0:T(8,128)(2,1)S(1)} %get-tuple-element.19), channel_id=1, source_target_pairs={{1,0},{2,1},{3,2},{4,3},{5,4},{6,5},{7,6},{0,7},{9,8},{10,9},{11,1... | collective-permute-start | bytes 110600 | tf_op jit(solution)/shard_map/ppermute | solution.py:323
  10.4 2.7 %collective-permute-start.1 = (bf16[6,6,512]{2,1,0:T(8,128)(2,1)S(1)}, bf16[6,6,512]{2,1,0:T(8,128)(2,1)S(1)}, u32[]{:S(2)}, u32[]{:S(2)}) collective-permute-start(bf16[6,6,512]{2,1,0:T(8,128)(2,1)S(1)} %get-tuple-element.20), channel_id=1, source_target_pairs={{8,0},{9,1},{10,2},{11,3},{12,4},{13,5},{14,6},{15,7},{16,8},{17,9... | collective-permute-start | bytes 110600 | tf_op jit(solution)/shard_map/ppermute | solution.py:323
  11.1 3.5 %collective-permute-start.2 = (bf16[6,6,512]{2,1,0:T(8,128)(2,1)S(1)}, bf16[6,6,512]{2,1,0:T(8,128)(2,1)S(1)}, u32[]{:S(2)}, u32[]{:S(2)}) collective-permute-start(bf16[6,6,512]{2,1,0:T(8,128)(2,1)S(1)} %get-tuple-element.21), channel_id=1, source_target_pairs={{9,0},{10,1},{11,2},{12,3},{13,4},{14,5},{15,6},{8,7},{17,8},{18,9... | collective-permute-start | bytes 110600 | tf_op jit(solution)/shard_map/ppermute | solution.py:323
  16.7 7.7 %collective-permute-start.3 = (bf16[6,6,512]{2,1,0:T(8,128)(2,1)S(1)}, bf16[6,6,512]{2,1,0:T(8,128)(2,1)S(1)}, u32[]{:S(2)}, u32[]{:S(2)}) collective-permute-start(bf16[6,6,512]{2,1,0:T(8,128)(2,1)S(1)} %get-tuple-element.25), channel_id=1, source_target_pairs={{31,0},{24,1},{25,2},{26,3},{27,4},{28,5},{29,6},{30,7},{7,8},{0,9... | collective-permute-start | bytes 110600 | tf_op jit(solution)/shard_map/ppermute | solution.py:323
  16.8 7.6 %collective-permute-start.4 = (bf16[6,6,512]{2,1,0:T(8,128)(2,1)S(1)}, bf16[6,6,512]{2,1,0:T(8,128)(2,1)S(1)}, u32[]{:S(2)}, u32[]{:S(2)}) collective-permute-start(bf16[6,6,512]{2,1,0:T(8,128)(2,1)S(1)} %get-tuple-element.26), channel_id=1, source_target_pairs={{24,0},{25,1},{26,2},{27,3},{28,4},{29,5},{30,6},{31,7},{0,8},{1,9... | collective-permute-start | bytes 110600 | tf_op jit(solution)/shard_map/ppermute | solution.py:323
  17.6 7.5 %collective-permute-start.5 = (bf16[6,6,512]{2,1,0:T(8,128)(2,1)S(1)}, bf16[6,6,512]{2,1,0:T(8,128)(2,1)S(1)}, u32[]{:S(2)}, u32[]{:S(2)}) collective-permute-start(bf16[6,6,512]{2,1,0:T(8,128)(2,1)S(1)} %get-tuple-element.27), channel_id=1, source_target_pairs={{7,0},{0,1},{1,2},{2,3},{3,4},{4,5},{5,6},{6,7},{15,8},{8,9},{9,10... | collective-permute-start | bytes 110600 | tf_op jit(solution)/shard_map/ppermute | solution.py:323

commit v6 on v5

--- a/solution.py
+++ b/solution.py
@@ -10,6 +10,8 @@
 
 
 HEADS = 16
+CUTS = 4
+CUT_FROM = 1 << 19
 WH = 12
 WW = 12
 LANES = 128
@@ -53,16 +55,16 @@
             top = min((8 * k + 7) * SPAN_C + PITCH + WW - 2, count - 1)
             sources = range(low // LANES, top // LANES + 1)
             plans.append((tile, k, index % LANES, index // LANES, sources))
-    for h in range(heads):
-        rows = {}
-        for tile, k, inner, outer, sources in plans:
-            value = None
-            for s in sources:
-                if s not in rows:
-                    rows[s] = jnp.broadcast_to(tab[h : h + 1, s * LANES : (s + 1) * LANES], (SUB, LANES))
-                taken = jnp.take_along_axis(rows[s], inner, axis=1)
-                value = taken if value is None else jnp.where(outer == s, taken, value)
-            strips[h, tile, :, k * LANES : (k + 1) * LANES] = value * LOG2E
+    for tile, k, inner, outer, sources in plans:
+        values = [None] * heads
+        for s in sources:
+            here = outer == s
+            for h in range(heads):
+                row = jnp.broadcast_to(tab[h : h + 1, s * LANES : (s + 1) * LANES], (SUB, LANES))
+                taken = jnp.take_along_axis(row, inner, axis=1)
+                values[h] = taken if values[h] is None else jnp.where(here, taken, values[h])
+        for h in range(heads):
+            strips[h, tile, :, k * LANES : (k + 1) * LANES] = values[h] * LOG2E
 
 
 def bias_tiles(strips, h):
@@ -140,12 +142,11 @@
         probs[u * SUB : (u + 2) * SUB, at : at + LANES] = pair.astype(BF16)
 
 
-def attend(xs, ys, gain, weights, bias, probs, polar):
+def attend(xs, ys, gain, weights, tiles_of, probs, polar):
     width = xs.shape[-1]
     head_dim = width // HEADS
     group = LANES // head_dim
     per_head = WH * PITCH
-    tiles_of = bias()
     x = xs[...].reshape(per_head, width)
     mean = jnp.mean(x, axis=-1, keepdims=True)
     centred = x - mean
@@ -212,38 +213,51 @@
             at += 1
 
 
+def cuts(shape):
+    if len(shape) == 2 and shape[0] * shape[1] >= CUT_FROM:
+        rows = shape[0] // CUTS
+        return [pl.ds(i * rows, rows) for i in range(CUTS)]
+    return [slice(None)]
+
+
+def pieces_of(source, target):
+    return [(source.at[part], target.at[part]) for part in cuts(source.shape)]
+
+
 def first_kernel(tokens, table, gain, wqkv, wproj, nw, ne, sw, se, xs, ys, probs, tab, strips, *here):
     here, sems = here[:-1], here[-1]
-    copies = [
-        pltpu.make_async_copy(a, b, sems.at[i])
-        for i, (a, b) in enumerate(zip((tokens, gain, wqkv, table, wproj), here))
-    ]
+    pairs = [pair for a, b in zip((table, tokens, gain, wqkv, wproj), here) for pair in pieces_of(a, b)]
+    copies = [pltpu.make_async_copy(a, b, sems.at[i]) for i, (a, b) in enumerate(pairs)]
     for copy in copies:
         copy.start()
     xs[:, WW:, :] = jnp.zeros((WH, PITCH - WW, xs.shape[-1]), F32)
     copies[0].wait()
-    xs[:, :WW, :] = here[0][0].astype(F32)
+    bias_strips(here[0], tab, strips)
     copies[1].wait()
+    xs[:, :WW, :] = here[1][0].astype(F32)
+    copies[2].wait()
 
     def weights(i):
-        copies[2 * i + 2].wait()
-        return here[2 * i + 2]
-
-    def bias():
-        copies[3].wait()
-        bias_strips(here[3], tab, strips)
-        return functools.partial(bias_tiles, strips)
-
-    attend(xs, ys, here[1], weights, bias, probs, None)
+        for copy in (copies[3:-1], copies[-1:])[i]:
+            copy.wait()
+        return here[3 + i]
+
+    attend(xs, ys, here[2], weights, functools.partial(bias_tiles, strips), probs, None)
     quadrants(ys, (nw, ne, sw, se))
 
 
-def bias_kernel(table, out, tab, strips):
+def bias_kernel(table, wqkv, wproj, out, wqkv_out, wproj_out, tab, strips, sems):
+    pairs = pieces_of(wqkv, wqkv_out) + pieces_of(wproj, wproj_out)
+    copies = [pltpu.make_async_copy(a, b, sems.at[i]) for i, (a, b) in enumerate(pairs)]
+    for copy in copies:
+        copy.start()
     bias_strips(table, tab, strips)
     for pair in range(out.shape[0]):
         for t, tiles in enumerate(bias_tiles(strips, 2 * pair)):
             for u, tile in enumerate(tiles):
                 out[pair, t, u] = tile
+    for copy in copies:
+        copy.wait()
 
 
 def second_kernel(nw_in, ne_in, sw_in, se_in, bias, gain, wqkv, wproj, nw, ne, sw, se, xs, ys, probs):
@@ -259,11 +273,12 @@
     def tiles_of(h):
         return [[bias[h // 2, t, u] for u in range(bias.shape[2])] for t in range(bias.shape[1])]
 
-    attend(xs, ys, gain, lambda i: (wqkv, wproj)[i], lambda: tiles_of, probs, polar)
+    attend(xs, ys, gain, lambda i: (wqkv, wproj)[i], tiles_of, probs, polar)
     quadrants(ys, (nw, ne, sw, se))
 
 
 VMEM = pl.BlockSpec(memory_space=pltpu.VMEM)
+HBM = pl.BlockSpec(memory_space=pltpu.HBM)
 
 
 def bias_room(table):
@@ -272,19 +287,24 @@
     return [pltpu.VMEM((heads, lanes), F32), pltpu.VMEM((heads, 2, SUB, 3 * LANES), F32)]
 
 
-def expand(table):
+def expand(table, wqkv, wproj):
     heads = table.shape[1]
     lane_tiles = 2 * WH * PITCH // LANES
     shape = (heads // 2, lane_tiles, WH * WW // SUB, SUB, LANES)
     return pl.pallas_call(
         bias_kernel,
-        out_shape=jax.ShapeDtypeStruct(shape, F32),
-        in_specs=[VMEM],
-        out_specs=VMEM,
-        scratch_shapes=bias_room(table),
+        out_shape=(
+            jax.ShapeDtypeStruct(shape, F32),
+            jax.ShapeDtypeStruct(wqkv.shape, wqkv.dtype),
+            jax.ShapeDtypeStruct(wproj.shape, wproj.dtype),
+        ),
+        in_specs=[VMEM, HBM, HBM],
+        out_specs=(VMEM,) * 3,
+        scratch_shapes=bias_room(table)
+        + [pltpu.SemaphoreType.DMA((len(cuts(wqkv.shape)) + len(cuts(wproj.shape)),))],
         compiler_params=pltpu.CompilerParams(vmem_limit_bytes=8 << 20),
         cost_estimate=pl.CostEstimate(flops=2_000_000, bytes_accessed=1_800_000, transcendentals=0),
-    )(table)
+    )(table, *(pltpu.with_memory_space_constraint(a, pltpu.HBM) for a in (wqkv, wproj)))
 
 
 def block(kernel, pieces, bias, gain, wqkv, wproj, fetch):
@@ -298,12 +318,12 @@
         pltpu.VMEM((HEADS // group, WH * WW, group * WH * PITCH), BF16),
     ]
     if fetch:
-        order = (args[0], args[2], args[3], args[1], args[4])
+        order = (args[1], args[0], *args[2:])
         scratch += bias_room(bias)
         scratch += [pltpu.VMEM(a.shape, a.dtype) for a in order]
-        scratch += [pltpu.SemaphoreType.DMA((len(order),))]
+        scratch += [pltpu.SemaphoreType.DMA((sum(len(cuts(a.shape)) for a in order),))]
         args = tuple(pltpu.with_memory_space_constraint(a, pltpu.HBM) for a in args)
-    source = pl.BlockSpec(memory_space=pltpu.HBM) if fetch else VMEM
+    source = HBM if fetch else VMEM
     return pl.pallas_call(
         kernel,
         out_shape=(piece,) * 4,
@@ -335,14 +355,8 @@
     bias_second,
 ):
     nw, ne, sw, se = block(first_kernel, (tokens,), bias_first, gain_first, qkv_first, proj_first, True)
-    sw, qkv_second, proj_second, bias_second = lax.optimization_barrier(
-        (sw, qkv_second, proj_second, bias_second)
-    )
-    bias = expand(bias_second)
-    east = moved(sw, 0, 1)
-    south = moved(ne, 1, 0)
-    corner = moved(nw, 1, 1)
-    window = (se, east, south, corner)
+    bias, qkv_second, proj_second = expand(bias_second, qkv_second, proj_second)
+    window = (se, moved(sw, 0, 1), moved(ne, 1, 0), moved(nw, 1, 1))
     nw, ne, sw, se = block(second_kernel, window, bias, gain_second, qkv_second, proj_second, False)
     west, north, corner = moved(ne, 0, -1), moved(sw, -1, 0), moved(se, -1, -1)
     upper = jnp.concatenate([corner, north], axis=1)

time: 26 us -> 25.8 us (level)
  waiting for transfers between devices: 8.92 us -> 7.54 us
  starting transfers between devices: 8.51 us -> 9.1 us
  Pallas kernels: 7.58 us -> 8.14 us
    ppermute x6, waiting for transfers between devices: 8.92 us -> 7.54 us  [moved(): return lax.ppermute(piece, ('lat', 'lon'), route)]
    pallas_call x1, Pallas kernels: 1.15 us -> 2.32 us  [expand(): pl.pallas_call(bias_kernel, out_shape=(jax.ShapeDtypeStruct(shape, F32),...]
    pallas_call x2, Pallas kernels: 6.44 us -> 5.82 us  [block(): pl.pallas_call(kernel, out_shape=(piece,) * 4, in_specs=[source] * len(ar...]
    ppermute x6, starting transfers between devices: 8.51 us -> 9.1 us  [moved(): return lax.ppermute(piece, ('lat', 'lon'), route)]
  transfers between devices with their start and end apart: 6 -> 6, of which waited for: 3 -> 3; matrix products, arithmetic and copies ran while one was open for 0% -> 0% of each run, Pallas kernels for 4% -> 9%
where the time goes in v6:
time: 25.8 us; the launch traced here: 25.6 us
  starting transfers between devices  9.1 us (35%)
  Pallas kernels  8.14 us (32%)
  waiting for transfers between devices  7.54 us (29%)
  other arithmetic  0.74 us (3%)
    ppermute x6, starting transfers between devices, moved(): return lax.ppermute(piece, ('lat', 'lon'), route)  9.1 us
    ppermute x6, waiting for transfers between devices, moved(): return lax.ppermute(piece, ('lat', 'lon'), route)  7.54 us
    pallas_call x2, Pallas kernels, block(): pl.pallas_call(kernel, out_shape=(piece,) * 4, in_specs=[source] * len(ar...  5.82 us
    pallas_call x1, Pallas kernels, expand(): pl.pallas_call(bias_kernel, out_shape=(jax.ShapeDtypeStruct(shape, F32),...  2.32 us
    broadcast_in_dim x1, other arithmetic, shards(): return jnp.concatenate([upper, lower], axis=0)[None]  0.74 us
  transfers between devices with their start and end apart: 6, of which 3 were waited for; matrix products, arithmetic and copies ran while one was open for 0% of the time, Pallas kernels for 9%

profile of v6, /device:TPU:0, one launch (start us, length us, event | category | flops | bytes accessed | tf_op | source)
XLA Modules:
  0.0 25.6 jit_solution(223824193676374178)
XLA Ops:
  0.0 0.0 copy-start
  0.0 3.7 %shard_map.91 = (bf16[6,6,512]{2,1,0:T(8,128)(2,1)S(1)}, bf16[6,6,512]{2,1,0:T(8,128)(2,1)S(1)}, bf16[6,6,512]{2,1,0:T(8,128)(2,1)S(1)}, bf16[6,6,512]{2,1,0:T(8,128)(2,1)S(1)}) custom-call(bf16[1,12,12,512]{3,2,1,0:T(8,128)(2,1)} %tokens.1, f32[1,16,529]{2,1,0:T(8,128)} %table.2, f32[1,512]{1,0:T(1,128)} %bitcast.5, bf16[512,1536]{1,0:T(8,128)(2,1)} %wqkv.2, ...), custom_call_target="tpu_custom_call" | custom-call | flops 400000000 | bytes 2500000 | tf_op jit(solution)/shard_map/pallas_call | solution.py:327
  3.7 0.0 copy-start.1
  3.7 6.1 %collective-permute-start = (bf16[6,6,512]{2,1,0:T(8,128)(2,1)S(1)}, bf16[6,6,512]{2,1,0:T(8,128)(2,1)S(1)}, u32[]{:S(2)}, u32[]{:S(2)}) collective-permute-start(bf16[6,6,512]{2,1,0:T(8,128)(2,1)S(1)} %get-tuple-element.17), channel_id=1, source_target_pairs={{1,0},{2,1},{3,2},{4,3},{5,4},{6,5},{7,6},{0,7},{9,8},{10,9},{11,1... | collective-permute-start | bytes 110600 | tf_op jit(solution)/shard_map/ppermute | solution.py:343
  9.8 0.7 %collective-permute-start.1 = (bf16[6,6,512]{2,1,0:T(8,128)(2,1)S(1)}, bf16[6,6,512]{2,1,0:T(8,128)(2,1)S(1)}, u32[]{:S(2)}, u32[]{:S(2)}) collective-permute-start(bf16[6,6,512]{2,1,0:T(8,128)(2,1)S(1)} %get-tuple-element.18), channel_id=1, source_target_pairs={{8,0},{9,1},{10,2},{11,3},{12,4},{13,5},{14,6},{15,7},{16,8},{17,9... | collective-permute-start | bytes 110600 | tf_op jit(solution)/shard_map/ppermute | solution.py:343
  10.4 0.9 %collective-permute-start.2 = (bf16[6,6,512]{2,1,0:T(8,128)(2,1)S(1)}, bf16[6,6,512]{2,1,0:T(8,128)(2,1)S(1)}, u32[]{:S(2)}, u32[]{:S(2)}) collective-permute-start(bf16[6,6,512]{2,1,0:T(8,128)(2,1)S(1)} %get-tuple-element.19), channel_id=1, source_target_pairs={{9,0},{10,1},{11,2},{12,3},{13,4},{14,5},{15,6},{8,7},{17,8},{18,9... | collective-permute-start | bytes 110600 | tf_op jit(solution)/shard_map/ppermute | solution.py:343
  11.3 0.0 copy-done
  11.3 2.3 %shard_map.92 = (f32[8,3,18,8,128]{4,3,2,1,0:T(8,128)S(1)}, bf16[512,1536]{1,0:T(8,128)(2,1)S(1)}, bf16[512,512]{1,0:T(8,128)(2,1)S(1)}) custom-call(f32[1,16,529]{2,1,0:T(8,128)S(1)} %copy-done, bf16[512,1536]{1,0:T(8,128)(2,1)} %wqkv.3, bf16[512,512]{1,0:T(8,128)(2,1)} %wproj.3), custom_call_target="tpu_custom_call" | custom-call | flops 2000000 | bytes 1800000 | tf_op jit(solution)/shard_map/pallas_call | solution.py:294
  13.7 0.0 collective-permute-done.ne_in
  13.7 0.0 collective-permute-done.1.sw_in
  13.7 0.3 %collective-permute-done.2.se_in = bf16[6,6,512]{2,1,0:T(8,128)(2,1)S(1)} collective-permute-done((bf16[6,6,512]{2,1,0:T(8,128)(2,1)S(1)}, bf16[6,6,512]{2,1,0:T(8,128)(2,1)S(1)}, u32[]{:S(2)}, u32[]{:S(2)}) %collective-permute-start.2) | collective-permute-done | bytes 36896 | tf_op jit(solution)/shard_map/ppermute | solution.py:343
  14.0 0.0 copy-done.1
  14.0 2.1 %shard_map.93 = (bf16[6,6,512]{2,1,0:T(8,128)(2,1)S(1)}, bf16[6,6,512]{2,1,0:T(8,128)(2,1)S(1)}, bf16[6,6,512]{2,1,0:T(8,128)(2,1)S(1)}, bf16[6,6,512]{2,1,0:T(8,128)(2,1)S(1)}) custom-call(bf16[6,6,512]{2,1,0:T(8,128)(2,1)S(1)} %get-tuple-element.16.nw_in, bf16[6,6,512]{2,1,0:T(8,128)(2,1)S(1)} %collective-permute-done.ne_in, ...), custom_call_target="tpu_custom_call" | custom-call | flops 400000000 | bytes 2500000 | tf_op jit(solution)/shard_map/pallas_call | solution.py:327
  16.1 0.7 %collective-permute-start.3 = (bf16[6,6,512]{2,1,0:T(8,128)(2,1)S(1)}, bf16[6,6,512]{2,1,0:T(8,128)(2,1)S(1)}, u32[]{:S(2)}, u32[]{:S(2)}) collective-permute-start(bf16[6,6,512]{2,1,0:T(8,128)(2,1)S(1)} %get-tuple-element.23), channel_id=1, source_target_pairs={{31,0},{24,1},{25,2},{26,3},{27,4},{28,5},{29,6},{30,7},{7,8},{0,9... | collective-permute-start | bytes 110600 | tf_op jit(solution)/shard_map/ppermute | solution.py:343
  16.8 0.8 %collective-permute-start.4 = (bf16[6,6,512]{2,1,0:T(8,128)(2,1)S(1)}, bf16[6,6,512]{2,1,0:T(8,128)(2,1)S(1)}, u32[]{:S(2)}, u32[]{:S(2)}) collective-permute-start(bf16[6,6,512]{2,1,0:T(8,128)(2,1)S(1)} %get-tuple-element.24), channel_id=1, source_target_pairs={{24,0},{25,1},{26,2},{27,3},{28,4},{29,5},{30,6},{31,7},{0,8},{1,9... | collective-permute-start | bytes 110600 | tf_op jit(solution)/shard_map/ppermute | solution.py:343
  17.5 0.0 collective-permute-start.5
  17.6 6.2 %collective-permute-done.3 = bf16[6,6,512]{2,1,0:T(8,128)(2,1)S(1)} collective-permute-done((bf16[6,6,512]{2,1,0:T(8,128)(2,1)S(1)}, bf16[6,6,512]{2,1,0:T(8,128)(2,1)S(1)}, u32[]{:S(2)}, u32[]{:S(2)}) %collective-permute-start.3) | collective-permute-done | bytes 36896 | tf_op jit(solution)/shard_map/ppermute | solution.py:343
  23.8 0.0 collective-permute-done.4
  23.8 1.1 %collective-permute-done.5 = bf16[6,6,512]{2,1,0:T(8,128)(2,1)S(1)} collective-permute-done((bf16[6,6,512]{2,1,0:T(8,128)(2,1)S(1)}, bf16[6,6,512]{2,1,0:T(8,128)(2,1)S(1)}, u32[]{:S(2)}, u32[]{:S(2)}) %collective-permute-start.5) | collective-permute-done | bytes 36896 | tf_op jit(solution)/shard_map/ppermute | solution.py:343
  24.9 0.7 %maximum_bitcast_fusion = bf16[1,12,12,512]{3,2,1,0:T(8,128)(2,1)} fusion(bf16[6,6,512]{2,1,0:T(8,128)(2,1)S(1)} %get-tuple-element.26, bf16[6,6,512]{2,1,0:T(8,128)(2,1)S(1)} %collective-permute-done.5, bf16[6,6,512]{2,1,0:T(8,128)(2,1)S(1)} %collective-permute-done.4, bf16[6,6,512]{2,1,0:T(8,128)(2,1)S(1)} %collective-permute-done.3), kind=kLoop, calls=%fused_computation | loop fusion | flops 589824 | bytes 294912 | tf_op jit(solution)/shard_map/broadcast_in_dim | solution.py:364
Async XLA Ops:
  0.0 11.3 %copy-start = (f32[1,16,529]{2,1,0:T(8,128)S(1)}, f32[1,16,529]{2,1,0:T(8,128)}, u32[]{:S(2)}) copy-start(f32[1,16,529]{2,1,0:T(8,128)} %table.3) | copy-start | bytes 101572
  3.7 10.3 %copy-start.1 = (f32[512]{0:T(512)S(1)}, f32[512]{0:T(512)}, u32[]{:S(2)}) copy-start(f32[512]{0:T(512)} %param.14) | copy-start | bytes 6148
  3.7 10.0 %collective-permute-start = (bf16[6,6,512]{2,1,0:T(8,128)(2,1)S(1)}, bf16[6,6,512]{2,1,0:T(8,128)(2,1)S(1)}, u32[]{:S(2)}, u32[]{:S(2)}) collective-permute-start(bf16[6,6,512]{2,1,0:T(8,128)(2,1)S(1)} %get-tuple-element.17), channel_id=1, source_target_pairs={{1,0},{2,1},{3,2},{4,3},{5,4},{6,5},{7,6},{0,7},{9,8},{10,9},{11,1... | collective-permute-start | bytes 110600 | tf_op jit(solution)/shard_map/ppermute | solution.py:343
  9.8 3.9 %collective-permute-start.1 = (bf16[6,6,512]{2,1,0:T(8,128)(2,1)S(1)}, bf16[6,6,512]{2,1,0:T(8,128)(2,1)S(1)}, u32[]{:S(2)}, u32[]{:S(2)}) collective-permute-start(bf16[6,6,512]{2,1,0:T(8,128)(2,1)S(1)} %get-tuple-element.18), channel_id=1, source_target_pairs={{8,0},{9,1},{10,2},{11,3},{12,4},{13,5},{14,6},{15,7},{16,8},{17,9... | collective-permute-start | bytes 110600 | tf_op jit(solution)/shard_map/ppermute | solution.py:343
  10.4 3.5 %collective-permute-start.2 = (bf16[6,6,512]{2,1,0:T(8,128)(2,1)S(1)}, bf16[6,6,512]{2,1,0:T(8,128)(2,1)S(1)}, u32[]{:S(2)}, u32[]{:S(2)}) collective-permute-start(bf16[6,6,512]{2,1,0:T(8,128)(2,1)S(1)} %get-tuple-element.19), channel_id=1, source_target_pairs={{9,0},{10,1},{11,2},{12,3},{13,4},{14,5},{15,6},{8,7},{17,8},{18,9... | collective-permute-start | bytes 110600 | tf_op jit(solution)/shard_map/ppermute | solution.py:343
  16.1 7.6 %collective-permute-start.3 = (bf16[6,6,512]{2,1,0:T(8,128)(2,1)S(1)}, bf16[6,6,512]{2,1,0:T(8,128)(2,1)S(1)}, u32[]{:S(2)}, u32[]{:S(2)}) collective-permute-start(bf16[6,6,512]{2,1,0:T(8,128)(2,1)S(1)} %get-tuple-element.23), channel_id=1, source_target_pairs={{31,0},{24,1},{25,2},{26,3},{27,4},{28,5},{29,6},{30,7},{7,8},{0,9... | collective-permute-start | bytes 110600 | tf_op jit(solution)/shard_map/ppermute | solution.py:343
  16.8 7.0 %collective-permute-start.4 = (bf16[6,6,512]{2,1,0:T(8,128)(2,1)S(1)}, bf16[6,6,512]{2,1,0:T(8,128)(2,1)S(1)}, u32[]{:S(2)}, u32[]{:S(2)}) collective-permute-start(bf16[6,6,512]{2,1,0:T(8,128)(2,1)S(1)} %get-tuple-element.24), channel_id=1, source_target_pairs={{24,0},{25,1},{26,2},{27,3},{28,4},{29,5},{30,6},{31,7},{0,8},{1,9... | collective-permute-start | bytes 110600 | tf_op jit(solution)/shard_map/ppermute | solution.py:343
  17.5 7.3 %collective-permute-start.5 = (bf16[6,6,512]{2,1,0:T(8,128)(2,1)S(1)}, bf16[6,6,512]{2,1,0:T(8,128)(2,1)S(1)}, u32[]{:S(2)}, u32[]{:S(2)}) collective-permute-start(bf16[6,6,512]{2,1,0:T(8,128)(2,1)S(1)} %get-tuple-element.25), channel_id=1, source_target_pairs={{7,0},{0,1},{1,2},{2,3},{3,4},{4,5},{5,6},{6,7},{15,8},{8,9},{9,10... | collective-permute-start | bytes 110600 | tf_op jit(solution)/shard_map/ppermute | solution.py:343

commit v7 on v6

--- a/solution.py
+++ b/solution.py
@@ -10,6 +10,7 @@
 
 
 HEADS = 16
+NEXT = 2
 CUTS = 4
 CUT_FROM = 1 << 19
 WH = 12
@@ -224,8 +225,11 @@
     return [(source.at[part], target.at[part]) for part in cuts(source.shape)]
 
 
-def first_kernel(tokens, table, gain, wqkv, wproj, nw, ne, sw, se, xs, ys, probs, tab, strips, *here):
-    here, sems = here[:-1], here[-1]
+def first_kernel(tokens, table, gain, wqkv, wproj, *rest):
+    nexts, (nw, ne, sw, se), rest = rest[:NEXT], rest[NEXT : NEXT + 4], rest[NEXT + 4 :]
+    next_here, (xs, ys, probs, tab, strips, *here, sems, next_sems) = rest[:NEXT], rest[NEXT:]
+    next_pairs = [pair for a, b in zip(nexts, next_here) for pair in pieces_of(a, b)]
+    next_copies = [pltpu.make_async_copy(a, b, next_sems.at[i]) for i, (a, b) in enumerate(next_pairs)]
     pairs = [pair for a, b in zip((table, tokens, gain, wqkv, wproj), here) for pair in pieces_of(a, b)]
     copies = [pltpu.make_async_copy(a, b, sems.at[i]) for i, (a, b) in enumerate(pairs)]
     for copy in copies:
@@ -240,24 +244,23 @@
     def weights(i):
         for copy in (copies[3:-1], copies[-1:])[i]:
             copy.wait()
+        if i == 0:
+            for copy in next_copies:
+                copy.start()
         return here[3 + i]
 
     attend(xs, ys, here[2], weights, functools.partial(bias_tiles, strips), probs, None)
     quadrants(ys, (nw, ne, sw, se))
-
-
-def bias_kernel(table, wqkv, wproj, out, wqkv_out, wproj_out, tab, strips, sems):
-    pairs = pieces_of(wqkv, wqkv_out) + pieces_of(wproj, wproj_out)
-    copies = [pltpu.make_async_copy(a, b, sems.at[i]) for i, (a, b) in enumerate(pairs)]
-    for copy in copies:
-        copy.start()
+    for copy in next_copies:
+        copy.wait()
+
+
+def bias_kernel(table, out, tab, strips):
     bias_strips(table, tab, strips)
     for pair in range(out.shape[0]):
         for t, tiles in enumerate(bias_tiles(strips, 2 * pair)):
             for u, tile in enumerate(tiles):
                 out[pair, t, u] = tile
-    for copy in copies:
-        copy.wait()
 
 
 def second_kernel(nw_in, ne_in, sw_in, se_in, bias, gain, wqkv, wproj, nw, ne, sw, se, xs, ys, probs):
@@ -287,27 +290,26 @@
     return [pltpu.VMEM((heads, lanes), F32), pltpu.VMEM((heads, 2, SUB, 3 * LANES), F32)]
 
 
-def expand(table, wqkv, wproj):
+def expand(table):
     heads = table.shape[1]
     lane_tiles = 2 * WH * PITCH // LANES
     shape = (heads // 2, lane_tiles, WH * WW // SUB, SUB, LANES)
     return pl.pallas_call(
         bias_kernel,
-        out_shape=(
-            jax.ShapeDtypeStruct(shape, F32),
-            jax.ShapeDtypeStruct(wqkv.shape, wqkv.dtype),
-            jax.ShapeDtypeStruct(wproj.shape, wproj.dtype),
-        ),
-        in_specs=[VMEM, HBM, HBM],
-        out_specs=(VMEM,) * 3,
-        scratch_shapes=bias_room(table)
-        + [pltpu.SemaphoreType.DMA((len(cuts(wqkv.shape)) + len(cuts(wproj.shape)),))],
+        out_shape=jax.ShapeDtypeStruct(shape, F32),
+        in_specs=[VMEM],
+        out_specs=VMEM,
+        scratch_shapes=bias_room(table),
         compiler_params=pltpu.CompilerParams(vmem_limit_bytes=8 << 20),
         cost_estimate=pl.CostEstimate(flops=2_000_000, bytes_accessed=1_800_000, transcendentals=0),
-    )(table, *(pltpu.with_memory_space_constraint(a, pltpu.HBM) for a in (wqkv, wproj)))
-
-
-def block(kernel, pieces, bias, gain, wqkv, wproj, fetch):
+    )(table)
+
+
+def copies_of(arrays):
+    return pltpu.SemaphoreType.DMA((sum(len(cuts(a.shape)) for a in arrays),))
+
+
+def block(kernel, pieces, bias, gain, wqkv, wproj, fetch=()):
     width = wproj.shape[0]
     group = LANES * HEADS // width
     piece = jax.ShapeDtypeStruct((HALF_R, HALF_C, width), BF16)
@@ -321,14 +323,14 @@
         order = (args[1], args[0], *args[2:])
         scratch += bias_room(bias)
         scratch += [pltpu.VMEM(a.shape, a.dtype) for a in order]
-        scratch += [pltpu.SemaphoreType.DMA((sum(len(cuts(a.shape)) for a in order),))]
-        args = tuple(pltpu.with_memory_space_constraint(a, pltpu.HBM) for a in args)
+        scratch += [copies_of(order), copies_of(fetch)]
+        args = tuple(pltpu.with_memory_space_constraint(a, pltpu.HBM) for a in (*args, *fetch))
     source = HBM if fetch else VMEM
     return pl.pallas_call(
         kernel,
-        out_shape=(piece,) * 4,
+        out_shape=(piece,) * 4 + tuple(jax.ShapeDtypeStruct(a.shape, a.dtype) for a in fetch),
         in_specs=[source] * len(args),
-        out_specs=(VMEM,) * 4,
+        out_specs=(VMEM,) * (4 + len(fetch)),
         scratch_shapes=scratch,
         compiler_params=pltpu.CompilerParams(vmem_limit_bytes=24 << 20),
         cost_estimate=pl.CostEstimate(flops=400_000_000, bytes_accessed=2_500_000, transcendentals=600_000),
@@ -354,10 +356,12 @@
     proj_second,
     bias_second,
 ):
-    nw, ne, sw, se = block(first_kernel, (tokens,), bias_first, gain_first, qkv_first, proj_first, True)
-    bias, qkv_second, proj_second = expand(bias_second, qkv_second, proj_second)
+    nw, ne, sw, se, qkv_second, proj_second = block(
+        first_kernel, (tokens,), bias_first, gain_first, qkv_first, proj_first, (qkv_second, proj_second)
+    )
+    bias = expand(bias_second)
     window = (se, moved(sw, 0, 1), moved(ne, 1, 0), moved(nw, 1, 1))
-    nw, ne, sw, se = block(second_kernel, window, bias, gain_second, qkv_second, proj_second, False)
+    nw, ne, sw, se = block(second_kernel, window, bias, gain_second, qkv_second, proj_second)
     west, north, corner = moved(ne, 0, -1), moved(sw, -1, 0), moved(se, -1, -1)
     upper = jnp.concatenate([corner, north], axis=1)
     lower = jnp.concatenate([west, nw], axis=1)

time: 25.8 us -> 26.2 us (1.016)
  waiting for transfers between devices: 7.54 us -> 9.14 us
  Pallas kernels: 8.14 us -> 7.54 us
  starting transfers between devices: 9.1 us -> 8.5 us
    ppermute x6, waiting for transfers between devices: 7.54 us -> 9.14 us  [moved(): return lax.ppermute(piece, ('lat', 'lon'), route)]
    pallas_call x3, Pallas kernels: 8.14 us -> 7.54 us  [the longest x2 6.62 us: block(): pl.pallas_call(kernel, out_shape=(piece,) * 4 + tuple((jax.ShapeDtypeStru...]
    ppermute x6, starting transfers between devices: 9.1 us -> 8.5 us  [moved(): return lax.ppermute(piece, ('lat', 'lon'), route)]
  transfers between devices with their start and end apart: 6 -> 6, of which waited for: 3 -> 3; matrix products, arithmetic and copies ran while one was open for 0% -> 0% of each run, Pallas kernels for 9% -> 4%
where the time goes in v7:
time: 26.2 us; the launch traced here: 26 us
  waiting for transfers between devices  9.14 us (35%)
  starting transfers between devices  8.5 us (32%)
  Pallas kernels  7.54 us (29%)
  other arithmetic  0.74 us (3%)
    ppermute x6, waiting for transfers between devices, moved(): return lax.ppermute(piece, ('lat', 'lon'), route)  9.14 us
    ppermute x6, starting transfers between devices, moved(): return lax.ppermute(piece, ('lat', 'lon'), route)  8.5 us
    pallas_call x2, Pallas kernels, block(): pl.pallas_call(kernel, out_shape=(piece,) * 4 + tuple((jax.ShapeDtypeStru...  6.62 us
    pallas_call x1, Pallas kernels, expand(): pl.pallas_call(bias_kernel, out_shape=jax.ShapeDtypeStruct(shape, F32), i...  0.92 us
    broadcast_in_dim x1, other arithmetic, shards(): return jnp.concatenate([upper, lower], axis=0)[None]  0.74 us
  transfers between devices with their start and end apart: 6, of which 3 were waited for; matrix products, arithmetic and copies ran while one was open for 0% of the time, Pallas kernels for 4%

profile of v7, /device:TPU:0, one launch (start us, length us, event | category | flops | bytes accessed | tf_op | source)
XLA Modules:
  0.0 26.0 jit_solution(14872422317159182454)
XLA Ops:
  0.0 0.0 copy-start
  0.0 4.5 %shard_map.91 = (bf16[6,6,512]{2,1,0:T(8,128)(2,1)S(1)}, bf16[6,6,512]{2,1,0:T(8,128)(2,1)S(1)}, bf16[6,6,512]{2,1,0:T(8,128)(2,1)S(1)}, bf16[6,6,512]{2,1,0:T(8...) custom-call(bf16[1,12,12,512]{3,2,1,0:T(8,128)(2,1)} %tokens.1, f32[1,16,529]{2,1,0:T(8,128)} %table.2, ...), custom_call_target="tpu_custom_call" | custom-call | flops 400000000 | bytes 2500000 | tf_op jit(solution)/shard_map/pallas_call | solution.py:329
  4.5 0.0 copy-start.1
  4.5 6.1 %collective-permute-start = (bf16[6,6,512]{2,1,0:T(8,128)(2,1)S(1)}, bf16[6,6,512]{2,1,0:T(8,128)(2,1)S(1)}, u32[]{:S(2)}, u32[]{:S(2)}) collective-permute-start(bf16[6,6,512]{2,1,0:T(8,128)(2,1)S(1)} %get-tuple-element.16), channel_id=1, source_target_pairs={{1,0},{2,1},{3,2},{4,3},{5,4},{6,5},{7,6},{0,7},{9,8},{10,9},{11,1... | collective-permute-start | bytes 110600 | tf_op jit(solution)/shard_map/ppermute | solution.py:345
  10.6 0.7 %collective-permute-start.1 = (bf16[6,6,512]{2,1,0:T(8,128)(2,1)S(1)}, bf16[6,6,512]{2,1,0:T(8,128)(2,1)S(1)}, u32[]{:S(2)}, u32[]{:S(2)}) collective-permute-start(bf16[6,6,512]{2,1,0:T(8,128)(2,1)S(1)} %get-tuple-element.17), channel_id=1, source_target_pairs={{8,0},{9,1},{10,2},{11,3},{12,4},{13,5},{14,6},{15,7},{16,8},{17,9... | collective-permute-start | bytes 110600 | tf_op jit(solution)/shard_map/ppermute | solution.py:345
  11.2 0.9 %collective-permute-start.2 = (bf16[6,6,512]{2,1,0:T(8,128)(2,1)S(1)}, bf16[6,6,512]{2,1,0:T(8,128)(2,1)S(1)}, u32[]{:S(2)}, u32[]{:S(2)}) collective-permute-start(bf16[6,6,512]{2,1,0:T(8,128)(2,1)S(1)} %get-tuple-element.18), channel_id=1, source_target_pairs={{9,0},{10,1},{11,2},{12,3},{13,4},{14,5},{15,6},{8,7},{17,8},{18,9... | collective-permute-start | bytes 110600 | tf_op jit(solution)/shard_map/ppermute | solution.py:345
  12.1 0.0 copy-done
  12.1 0.9 %shard_map.92.bias = f32[8,3,18,8,128]{4,3,2,1,0:T(8,128)S(1)} custom-call(f32[1,16,529]{2,1,0:T(8,128)S(1)} %copy-done), custom_call_target="tpu_custom_call" | custom-call | flops 2000000 | bytes 1800000 | tf_op jit(solution)/shard_map/pallas_call | solution.py:297
  13.1 0.0 collective-permute-done.ne_in
  13.1 0.0 collective-permute-done.1.sw_in
  13.1 1.7 %collective-permute-done.2.se_in = bf16[6,6,512]{2,1,0:T(8,128)(2,1)S(1)} collective-permute-done((bf16[6,6,512]{2,1,0:T(8,128)(2,1)S(1)}, bf16[6,6,512]{2,1,0:T(8,128)(2,1)S(1)}, u32[]{:S(2)}, u32[]{:S(2)}) %collective-permute-start.2) | collective-permute-done | bytes 36896 | tf_op jit(solution)/shard_map/ppermute | solution.py:345
  14.8 0.0 copy-done.1
  14.8 2.1 %shard_map.93 = (bf16[6,6,512]{2,1,0:T(8,128)(2,1)S(1)}, bf16[6,6,512]{2,1,0:T(8,128)(2,1)S(1)}, bf16[6,6,512]{2,1,0:T(8,128)(2,1)S(1)}, bf16[6,6,512]{2,1,0:T(8,128)(2,1)S(1)}) custom-call(bf16[6,6,512]{2,1,0:T(8,128)(2,1)S(1)} %get-tuple-element.15.nw_in, bf16[6,6,512]{2,1,0:T(8,128)(2,1)S(1)} %collective-permute-done.ne_in, ...), custom_call_target="tpu_custom_call" | custom-call | flops 400000000 | bytes 2500000 | tf_op jit(solution)/shard_map/pallas_call | solution.py:329
  16.9 0.1 collective-permute-start.3
  17.0 0.8 %collective-permute-start.4 = (bf16[6,6,512]{2,1,0:T(8,128)(2,1)S(1)}, bf16[6,6,512]{2,1,0:T(8,128)(2,1)S(1)}, u32[]{:S(2)}, u32[]{:S(2)}) collective-permute-start(bf16[6,6,512]{2,1,0:T(8,128)(2,1)S(1)} %get-tuple-element.22), channel_id=1, source_target_pairs={{24,0},{25,1},{26,2},{27,3},{28,4},{29,5},{30,6},{31,7},{0,8},{1,9... | collective-permute-start | bytes 110600 | tf_op jit(solution)/shard_map/ppermute | solution.py:345
  17.8 0.0 collective-permute-start.5
  17.8 6.8 %collective-permute-done.3 = bf16[6,6,512]{2,1,0:T(8,128)(2,1)S(1)} collective-permute-done((bf16[6,6,512]{2,1,0:T(8,128)(2,1)S(1)}, bf16[6,6,512]{2,1,0:T(8,128)(2,1)S(1)}, u32[]{:S(2)}, u32[]{:S(2)}) %collective-permute-start.3) | collective-permute-done | bytes 36896 | tf_op jit(solution)/shard_map/ppermute | solution.py:345
  24.6 0.0 collective-permute-done.4
  24.6 0.7 %collective-permute-done.5 = bf16[6,6,512]{2,1,0:T(8,128)(2,1)S(1)} collective-permute-done((bf16[6,6,512]{2,1,0:T(8,128)(2,1)S(1)}, bf16[6,6,512]{2,1,0:T(8,128)(2,1)S(1)}, u32[]{:S(2)}, u32[]{:S(2)}) %collective-permute-start.5) | collective-permute-done | bytes 36896 | tf_op jit(solution)/shard_map/ppermute | solution.py:345
  25.3 0.7 %maximum_bitcast_fusion = bf16[1,12,12,512]{3,2,1,0:T(8,128)(2,1)} fusion(bf16[6,6,512]{2,1,0:T(8,128)(2,1)S(1)} %get-tuple-element.24, bf16[6,6,512]{2,1,0:T(8,128)(2,1)S(1)} %collective-permute-done.5, bf16[6,6,512]{2,1,0:T(8,128)(2,1)S(1)} %collective-permute-done.4, bf16[6,6,512]{2,1,0:T(8,128)(2,1)S(1)} %collective-permute-done.3), kind=kLoop, calls=%fused_computation | loop fusion | flops 589824 | bytes 294912 | tf_op jit(solution)/shard_map/broadcast_in_dim | solution.py:368
Async XLA Ops:
  0.0 12.1 %copy-start = (f32[1,16,529]{2,1,0:T(8,128)S(1)}, f32[1,16,529]{2,1,0:T(8,128)}, u32[]{:S(2)}) copy-start(f32[1,16,529]{2,1,0:T(8,128)} %table.3) | copy-start | bytes 101572
  4.5 10.3 %copy-start.1 = (f32[512]{0:T(512)S(1)}, f32[512]{0:T(512)}, u32[]{:S(2)}) copy-start(f32[512]{0:T(512)} %param.14) | copy-start | bytes 6148
  4.5 8.6 %collective-permute-start = (bf16[6,6,512]{2,1,0:T(8,128)(2,1)S(1)}, bf16[6,6,512]{2,1,0:T(8,128)(2,1)S(1)}, u32[]{:S(2)}, u32[]{:S(2)}) collective-permute-start(bf16[6,6,512]{2,1,0:T(8,128)(2,1)S(1)} %get-tuple-element.16), channel_id=1, source_target_pairs={{1,0},{2,1},{3,2},{4,3},{5,4},{6,5},{7,6},{0,7},{9,8},{10,9},{11,1... | collective-permute-start | bytes 110600 | tf_op jit(solution)/shard_map/ppermute | solution.py:345
  10.6 2.5 %collective-permute-start.1 = (bf16[6,6,512]{2,1,0:T(8,128)(2,1)S(1)}, bf16[6,6,512]{2,1,0:T(8,128)(2,1)S(1)}, u32[]{:S(2)}, u32[]{:S(2)}) collective-permute-start(bf16[6,6,512]{2,1,0:T(8,128)(2,1)S(1)} %get-tuple-element.17), channel_id=1, source_target_pairs={{8,0},{9,1},{10,2},{11,3},{12,4},{13,5},{14,6},{15,7},{16,8},{17,9... | collective-permute-start | bytes 110600 | tf_op jit(solution)/shard_map/ppermute | solution.py:345
  11.2 3.5 %collective-permute-start.2 = (bf16[6,6,512]{2,1,0:T(8,128)(2,1)S(1)}, bf16[6,6,512]{2,1,0:T(8,128)(2,1)S(1)}, u32[]{:S(2)}, u32[]{:S(2)}) collective-permute-start(bf16[6,6,512]{2,1,0:T(8,128)(2,1)S(1)} %get-tuple-element.18), channel_id=1, source_target_pairs={{9,0},{10,1},{11,2},{12,3},{13,4},{14,5},{15,6},{8,7},{17,8},{18,9... | collective-permute-start | bytes 110600 | tf_op jit(solution)/shard_map/ppermute | solution.py:345
  16.9 7.7 %collective-permute-start.3 = (bf16[6,6,512]{2,1,0:T(8,128)(2,1)S(1)}, bf16[6,6,512]{2,1,0:T(8,128)(2,1)S(1)}, u32[]{:S(2)}, u32[]{:S(2)}) collective-permute-start(bf16[6,6,512]{2,1,0:T(8,128)(2,1)S(1)} %get-tuple-element.21), channel_id=1, source_target_pairs={{31,0},{24,1},{25,2},{26,3},{27,4},{28,5},{29,6},{30,7},{7,8},{0,9... | collective-permute-start | bytes 110600 | tf_op jit(solution)/shard_map/ppermute | solution.py:345
  17.0 7.6 %collective-permute-start.4 = (bf16[6,6,512]{2,1,0:T(8,128)(2,1)S(1)}, bf16[6,6,512]{2,1,0:T(8,128)(2,1)S(1)}, u32[]{:S(2)}, u32[]{:S(2)}) collective-permute-start(bf16[6,6,512]{2,1,0:T(8,128)(2,1)S(1)} %get-tuple-element.22), channel_id=1, source_target_pairs={{24,0},{25,1},{26,2},{27,3},{28,4},{29,5},{30,6},{31,7},{0,8},{1,9... | collective-permute-start | bytes 110600 | tf_op jit(solution)/shard_map/ppermute | solution.py:345
  17.8 7.5 %collective-permute-start.5 = (bf16[6,6,512]{2,1,0:T(8,128)(2,1)S(1)}, bf16[6,6,512]{2,1,0:T(8,128)(2,1)S(1)}, u32[]{:S(2)}, u32[]{:S(2)}) collective-permute-start(bf16[6,6,512]{2,1,0:T(8,128)(2,1)S(1)} %get-tuple-element.23), channel_id=1, source_target_pairs={{7,0},{0,1},{1,2},{2,3},{3,4},{4,5},{5,6},{6,7},{15,8},{8,9},{9,10... | collective-permute-start | bytes 110600 | tf_op jit(solution)/shard_map/ppermute | solution.py:345

commit v8 on v7

--- a/solution.py
+++ b/solution.py
@@ -10,7 +10,6 @@
 
 
 HEADS = 16
-NEXT = 2
 CUTS = 4
 CUT_FROM = 1 << 19
 WH = 12
@@ -206,12 +205,26 @@
     ys[...] = xs[...] + branch.reshape(xs.shape)
 
 
+CORNERS = [(r, c) for r in (0, HALF_R) for c in (0, HALF_C)]
+
+
 def quadrants(ys, outs):
-    at = 0
-    for r in (0, HALF_R):
-        for c in (0, HALF_C):
-            outs[at][...] = ys[r : r + HALF_R, c : c + HALF_C, :].astype(BF16)
-            at += 1
+    for at, (r, c) in enumerate(CORNERS):
+        outs[at][...] = ys[r : r + HALF_R, c : c + HALF_C, :].astype(BF16)
+
+
+def packed(ys, zs, outs):
+    for at, (r, c) in enumerate(CORNERS):
+        for i in range(HALF_R):
+            zs[at, i * HALF_C : (i + 1) * HALF_C, :] = ys[r + i, c : c + HALF_C, :]
+        outs[at][...] = zs[at].astype(BF16)
+
+
+def unpacked(pieces, zs, xs):
+    for at, (r, c) in enumerate(CORNERS):
+        zs[at] = pieces[at][...].astype(F32)
+        for i in range(HALF_R):
+            xs[r + i, c : c + HALF_C, :] = zs[at, i * HALF_C : (i + 1) * HALF_C, :]
 
 
 def cuts(shape):
@@ -225,11 +238,8 @@
     return [(source.at[part], target.at[part]) for part in cuts(source.shape)]
 
 
-def first_kernel(tokens, table, gain, wqkv, wproj, *rest):
-    nexts, (nw, ne, sw, se), rest = rest[:NEXT], rest[NEXT : NEXT + 4], rest[NEXT + 4 :]
-    next_here, (xs, ys, probs, tab, strips, *here, sems, next_sems) = rest[:NEXT], rest[NEXT:]
-    next_pairs = [pair for a, b in zip(nexts, next_here) for pair in pieces_of(a, b)]
-    next_copies = [pltpu.make_async_copy(a, b, next_sems.at[i]) for i, (a, b) in enumerate(next_pairs)]
+def first_kernel(tokens, table, gain, wqkv, wproj, nw, ne, sw, se, xs, ys, zs, probs, tab, strips, *here):
+    here, sems = here[:-1], here[-1]
     pairs = [pair for a, b in zip((table, tokens, gain, wqkv, wproj), here) for pair in pieces_of(a, b)]
     copies = [pltpu.make_async_copy(a, b, sems.at[i]) for i, (a, b) in enumerate(pairs)]
     for copy in copies:
@@ -244,15 +254,10 @@
     def weights(i):
         for copy in (copies[3:-1], copies[-1:])[i]:
             copy.wait()
-        if i == 0:
-            for copy in next_copies:
-                copy.start()
         return here[3 + i]
 
     attend(xs, ys, here[2], weights, functools.partial(bias_tiles, strips), probs, None)
-    quadrants(ys, (nw, ne, sw, se))
-    for copy in next_copies:
-        copy.wait()
+    packed(ys, zs, (nw, ne, sw, se))
 
 
 def bias_kernel(table, out, tab, strips):
@@ -263,15 +268,10 @@
                 out[pair, t, u] = tile
 
 
-def second_kernel(nw_in, ne_in, sw_in, se_in, bias, gain, wqkv, wproj, nw, ne, sw, se, xs, ys, probs):
+def second_kernel(nw_in, ne_in, sw_in, se_in, bias, gain, wqkv, wproj, nw, ne, sw, se, xs, ys, zs, probs):
     polar = lax.axis_index("lat") == lax.axis_size("lat") - 1
     xs[:, WW:, :] = jnp.zeros((WH, PITCH - WW, xs.shape[-1]), F32)
-    at = 0
-    pieces = (nw_in, ne_in, sw_in, se_in)
-    for r in (0, HALF_R):
-        for c in (0, HALF_C):
-            xs[r : r + HALF_R, c : c + HALF_C, :] = pieces[at][...].astype(F32)
-            at += 1
+    unpacked((nw_in, ne_in, sw_in, se_in), zs, xs)
 
     def tiles_of(h):
         return [[bias[h // 2, t, u] for u in range(bias.shape[2])] for t in range(bias.shape[1])]
@@ -305,32 +305,29 @@
     )(table)
 
 
-def copies_of(arrays):
-    return pltpu.SemaphoreType.DMA((sum(len(cuts(a.shape)) for a in arrays),))
-
-
-def block(kernel, pieces, bias, gain, wqkv, wproj, fetch=()):
+def block(kernel, pieces, bias, gain, wqkv, wproj, fetch, shape):
     width = wproj.shape[0]
     group = LANES * HEADS // width
-    piece = jax.ShapeDtypeStruct((HALF_R, HALF_C, width), BF16)
+    piece = jax.ShapeDtypeStruct(shape, BF16)
     args = (*pieces, bias, gain.reshape(1, width), wqkv, wproj)
     scratch = [
         pltpu.VMEM((WH, PITCH, width), F32),
         pltpu.VMEM((WH, PITCH, width), F32),
+        pltpu.VMEM((4, HALF_R * HALF_C, width), F32),
         pltpu.VMEM((HEADS // group, WH * WW, group * WH * PITCH), BF16),
     ]
     if fetch:
         order = (args[1], args[0], *args[2:])
         scratch += bias_room(bias)
         scratch += [pltpu.VMEM(a.shape, a.dtype) for a in order]
-        scratch += [copies_of(order), copies_of(fetch)]
-        args = tuple(pltpu.with_memory_space_constraint(a, pltpu.HBM) for a in (*args, *fetch))
+        scratch += [pltpu.SemaphoreType.DMA((sum(len(cuts(a.shape)) for a in order),))]
+        args = tuple(pltpu.with_memory_space_constraint(a, pltpu.HBM) for a in args)
     source = HBM if fetch else VMEM
     return pl.pallas_call(
         kernel,
-        out_shape=(piece,) * 4 + tuple(jax.ShapeDtypeStruct(a.shape, a.dtype) for a in fetch),
+        out_shape=(piece,) * 4,
         in_specs=[source] * len(args),
-        out_specs=(VMEM,) * (4 + len(fetch)),
+        out_specs=(VMEM,) * 4,
         scratch_shapes=scratch,
         compiler_params=pltpu.CompilerParams(vmem_limit_bytes=24 << 20),
         cost_estimate=pl.CostEstimate(flops=400_000_000, bytes_accessed=2_500_000, transcendentals=600_000),
@@ -356,12 +353,14 @@
     proj_second,
     bias_second,
 ):
-    nw, ne, sw, se, qkv_second, proj_second = block(
-        first_kernel, (tokens,), bias_first, gain_first, qkv_first, proj_first, (qkv_second, proj_second)
+    size = (HALF_R * HALF_C, tokens.shape[-1])
+    nw, ne, sw, se = block(
+        first_kernel, (tokens,), bias_first, gain_first, qkv_first, proj_first, True, size
     )
     bias = expand(bias_second)
     window = (se, moved(sw, 0, 1), moved(ne, 1, 0), moved(nw, 1, 1))
-    nw, ne, sw, se = block(second_kernel, window, bias, gain_second, qkv_second, proj_second)
+    size = (HALF_R, HALF_C, tokens.shape[-1])
+    nw, ne, sw, se = block(second_kernel, window, bias, gain_second, qkv_second, proj_second, False, size)
     west, north, corner = moved(ne, 0, -1), moved(sw, -1, 0), moved(se, -1, -1)
     upper = jnp.concatenate([corner, north], axis=1)
     lower = jnp.concatenate([west, nw], axis=1)

time: 26.2 us -> 25.5 us (0.973)
  Pallas kernels: 7.54 us -> 6.99 us
    pallas_call x2, Pallas kernels: 6.62 us -> 6.06 us  [block(): pl.pallas_call(kernel, out_shape=(piece,) * 4, in_specs=[source] * len(ar...]
where the time goes in v8:
time: 25.5 us; the launch traced here: 25.4 us
  waiting for transfers between devices  9.05 us (35%)
  starting transfers between devices  8.52 us (33%)
  Pallas kernels  6.99 us (27%)
  other arithmetic  0.74 us (3%)
    ppermute x6, waiting for transfers between devices, moved(): return lax.ppermute(piece, ('lat', 'lon'), route)  9.05 us
    ppermute x6, starting transfers between devices, moved(): return lax.ppermute(piece, ('lat', 'lon'), route)  8.52 us
    pallas_call x2, Pallas kernels, block(): pl.pallas_call(kernel, out_shape=(piece,) * 4, in_specs=[source] * len(ar...  6.06 us
    pallas_call x1, Pallas kernels, expand(): pl.pallas_call(bias_kernel, out_shape=jax.ShapeDtypeStruct(shape, F32), i...  0.92 us
    broadcast_in_dim x1, other arithmetic, shards(): return jnp.concatenate([upper, lower], axis=0)[None]  0.74 us
  transfers between devices with their start and end apart: 6, of which 3 were waited for; matrix products, arithmetic and copies ran while one was open for 0% of the time, Pallas kernels for 4%

profile of v8, /device:TPU:0, one launch (start us, length us, event | category | flops | bytes accessed | tf_op | source)
XLA Modules:
  0.0 25.4 jit_solution(13481911642819772167)
XLA Ops:
  0.0 0.0 copy-start.2
  0.0 0.0 copy-start
  0.0 0.0 copy-start.1
  0.0 0.0 copy-start.3
  0.0 3.8 %shard_map.91 = (bf16[36,512]{1,0:T(8,128)(2,1)S(1)}, bf16[36,512]{1,0:T(8,128)(2,1)S(1)}, bf16[36,512]{1,0:T(8,128)(2,1)S(1)}, bf16[36,512]{1,0:T(8,128)(2,1)S(1)}) custom-call(bf16[1,12,12,512]{3,2,1,0:T(8,128)(2,1)} %tokens.1, f32[1,16,529]{2,1,0:T(8,128)} %table.2, f32[1,512]{1,0:T(1,128)} %bitcast.5, bf16[512,1536]{1,0:T(8,128)(2,1)} %wqkv.2, ...), custom_call_target="tpu_custom_call" | custom-call | flops 400000000 | bytes 2500000 | tf_op jit(solution)/shard_map/pallas_call | solution.py:326
  3.9 6.1 %collective-permute-start = (bf16[36,512]{1,0:T(8,128)(2,1)S(1)}, bf16[36,512]{1,0:T(8,128)(2,1)S(1)}, u32[]{:S(2)}, u32[]{:S(2)}) collective-permute-start(bf16[36,512]{1,0:T(8,128)(2,1)S(1)} %get-tuple-element.14), channel_id=1, source_target_pairs={{1,0},{2,1},{3,2},{4,3},{5,4},{6,5},{7,6},{0,7},{9,8},{10,9},{11,1... | collective-permute-start | bytes 110600 | tf_op jit(solution)/shard_map/ppermute | solution.py:342
  10.0 0.7 %collective-permute-start.1 = (bf16[36,512]{1,0:T(8,128)(2,1)S(1)}, bf16[36,512]{1,0:T(8,128)(2,1)S(1)}, u32[]{:S(2)}, u32[]{:S(2)}) collective-permute-start(bf16[36,512]{1,0:T(8,128)(2,1)S(1)} %get-tuple-element.15), channel_id=1, source_target_pairs={{8,0},{9,1},{10,2},{11,3},{12,4},{13,5},{14,6},{15,7},{16,8},{17,9... | collective-permute-start | bytes 110600 | tf_op jit(solution)/shard_map/ppermute | solution.py:342
  10.6 0.9 %collective-permute-start.2 = (bf16[36,512]{1,0:T(8,128)(2,1)S(1)}, bf16[36,512]{1,0:T(8,128)(2,1)S(1)}, u32[]{:S(2)}, u32[]{:S(2)}) collective-permute-start(bf16[36,512]{1,0:T(8,128)(2,1)S(1)} %get-tuple-element.16), channel_id=1, source_target_pairs={{9,0},{10,1},{11,2},{12,3},{13,4},{14,5},{15,6},{8,7},{17,8},{18,9... | collective-permute-start | bytes 110600 | tf_op jit(solution)/shard_map/ppermute | solution.py:342
  11.5 0.0 copy-done.2
  11.5 0.9 %shard_map.92.bias = f32[8,3,18,8,128]{4,3,2,1,0:T(8,128)S(1)} custom-call(f32[1,16,529]{2,1,0:T(8,128)S(1)} %copy-done.2), custom_call_target="tpu_custom_call" | custom-call | flops 2000000 | bytes 1800000 | tf_op jit(solution)/shard_map/pallas_call | solution.py:297
  12.4 0.0 collective-permute-done.ne_in
  12.5 0.0 collective-permute-done.1.sw_in
  12.5 1.6 %collective-permute-done.2.se_in = bf16[36,512]{1,0:T(8,128)(2,1)S(1)} collective-permute-done((bf16[36,512]{1,0:T(8,128)(2,1)S(1)}, bf16[36,512]{1,0:T(8,128)(2,1)S(1)}, u32[]{:S(2)}, u32[]{:S(2)}) %collective-permute-start.2) | collective-permute-done | bytes 36896 | tf_op jit(solution)/shard_map/ppermute | solution.py:342
  14.0 0.0 copy-done
  14.0 0.0 copy-done.1
  14.0 0.0 copy-done.3
  14.1 2.2 %shard_map.93 = (bf16[6,6,512]{2,1,0:T(8,128)(2,1)S(1)}, bf16[6,6,512]{2,1,0:T(8,128)(2,1)S(1)}, bf16[6,6,512]{2,1,0:T(8,128)(2,1)S(1)}, bf16[6,6,512]{2,1,0:T(8,128)(2,1)S(1)}) custom-call(bf16[36,512]{1,0:T(8,128)(2,1)S(1)} %get-tuple-element.13.nw_in, bf16[36,512]{1,0:T(8,128)(2,1)S(1)} %collective-permute-done.ne_in, ...), custom_call_target="tpu_custom_call" | custom-call | flops 400000000 | bytes 2500000 | tf_op jit(solution)/shard_map/pallas_call | solution.py:326
  16.3 0.1 collective-permute-start.3
  16.3 0.8 %collective-permute-start.4 = (bf16[6,6,512]{2,1,0:T(8,128)(2,1)S(1)}, bf16[6,6,512]{2,1,0:T(8,128)(2,1)S(1)}, u32[]{:S(2)}, u32[]{:S(2)}) collective-permute-start(bf16[6,6,512]{2,1,0:T(8,128)(2,1)S(1)} %get-tuple-element.18), channel_id=1, source_target_pairs={{24,0},{25,1},{26,2},{27,3},{28,4},{29,5},{30,6},{31,7},{0,8},{1,9... | collective-permute-start | bytes 110600 | tf_op jit(solution)/shard_map/ppermute | solution.py:342
  17.1 0.0 collective-permute-start.5
  17.2 6.8 %collective-permute-done.3 = bf16[6,6,512]{2,1,0:T(8,128)(2,1)S(1)} collective-permute-done((bf16[6,6,512]{2,1,0:T(8,128)(2,1)S(1)}, bf16[6,6,512]{2,1,0:T(8,128)(2,1)S(1)}, u32[]{:S(2)}, u32[]{:S(2)}) %collective-permute-start.3) | collective-permute-done | bytes 36896 | tf_op jit(solution)/shard_map/ppermute | solution.py:342
  23.9 0.0 collective-permute-done.4
  23.9 0.7 %collective-permute-done.5 = bf16[6,6,512]{2,1,0:T(8,128)(2,1)S(1)} collective-permute-done((bf16[6,6,512]{2,1,0:T(8,128)(2,1)S(1)}, bf16[6,6,512]{2,1,0:T(8,128)(2,1)S(1)}, u32[]{:S(2)}, u32[]{:S(2)}) %collective-permute-start.5) | collective-permute-done | bytes 36896 | tf_op jit(solution)/shard_map/ppermute | solution.py:342
  24.6 0.7 %maximum_bitcast_fusion = bf16[1,12,12,512]{3,2,1,0:T(8,128)(2,1)} fusion(bf16[6,6,512]{2,1,0:T(8,128)(2,1)S(1)} %get-tuple-element.20, bf16[6,6,512]{2,1,0:T(8,128)(2,1)S(1)} %collective-permute-done.5, bf16[6,6,512]{2,1,0:T(8,128)(2,1)S(1)} %collective-permute-done.4, bf16[6,6,512]{2,1,0:T(8,128)(2,1)S(1)} %collective-permute-done.3), kind=kLoop, calls=%fused_computation | loop fusion | flops 589824 | bytes 294912 | tf_op jit(solution)/shard_map/broadcast_in_dim | solution.py:367
Async XLA Ops:
  0.0 11.5 %copy-start.2 = (f32[1,16,529]{2,1,0:T(8,128)S(1)}, f32[1,16,529]{2,1,0:T(8,128)}, u32[]{:S(2)}) copy-start(f32[1,16,529]{2,1,0:T(8,128)} %table.3) | copy-start | bytes 101572
  0.0 14.0 %copy-start = (bf16[512,1536]{1,0:T(8,128)(2,1)S(1)}, bf16[512,1536]{1,0:T(8,128)(2,1)}, u32[]{:S(2)}) copy-start(bf16[512,1536]{1,0:T(8,128)(2,1)} %wqkv.3) | copy-start | bytes 4718596
  0.0 14.0 %copy-start.1 = (bf16[512,512]{1,0:T(8,128)(2,1)S(1)}, bf16[512,512]{1,0:T(8,128)(2,1)}, u32[]{:S(2)}) copy-start(bf16[512,512]{1,0:T(8,128)(2,1)} %wproj.3) | copy-start | bytes 1572868
  0.0 14.0 %copy-start.3 = (f32[512]{0:T(512)S(1)}, f32[512]{0:T(512)}, u32[]{:S(2)}) copy-start(f32[512]{0:T(512)} %param.14) | copy-start | bytes 6148
  3.9 8.6 %collective-permute-start = (bf16[36,512]{1,0:T(8,128)(2,1)S(1)}, bf16[36,512]{1,0:T(8,128)(2,1)S(1)}, u32[]{:S(2)}, u32[]{:S(2)}) collective-permute-start(bf16[36,512]{1,0:T(8,128)(2,1)S(1)} %get-tuple-element.14), channel_id=1, source_target_pairs={{1,0},{2,1},{3,2},{4,3},{5,4},{6,5},{7,6},{0,7},{9,8},{10,9},{11,1... | collective-permute-start | bytes 110600 | tf_op jit(solution)/shard_map/ppermute | solution.py:342
  10.0 2.5 %collective-permute-start.1 = (bf16[36,512]{1,0:T(8,128)(2,1)S(1)}, bf16[36,512]{1,0:T(8,128)(2,1)S(1)}, u32[]{:S(2)}, u32[]{:S(2)}) collective-permute-start(bf16[36,512]{1,0:T(8,128)(2,1)S(1)} %get-tuple-element.15), channel_id=1, source_target_pairs={{8,0},{9,1},{10,2},{11,3},{12,4},{13,5},{14,6},{15,7},{16,8},{17,9... | collective-permute-start | bytes 110600 | tf_op jit(solution)/shard_map/ppermute | solution.py:342
  10.6 3.4 %collective-permute-start.2 = (bf16[36,512]{1,0:T(8,128)(2,1)S(1)}, bf16[36,512]{1,0:T(8,128)(2,1)S(1)}, u32[]{:S(2)}, u32[]{:S(2)}) collective-permute-start(bf16[36,512]{1,0:T(8,128)(2,1)S(1)} %get-tuple-element.16), channel_id=1, source_target_pairs={{9,0},{10,1},{11,2},{12,3},{13,4},{14,5},{15,6},{8,7},{17,8},{18,9... | collective-permute-start | bytes 110600 | tf_op jit(solution)/shard_map/ppermute | solution.py:342
  16.3 7.7 %collective-permute-start.3 = (bf16[6,6,512]{2,1,0:T(8,128)(2,1)S(1)}, bf16[6,6,512]{2,1,0:T(8,128)(2,1)S(1)}, u32[]{:S(2)}, u32[]{:S(2)}) collective-permute-start(bf16[6,6,512]{2,1,0:T(8,128)(2,1)S(1)} %get-tuple-element.17), channel_id=1, source_target_pairs={{31,0},{24,1},{25,2},{26,3},{27,4},{28,5},{29,6},{30,7},{7,8},{0,9... | collective-permute-start | bytes 110600 | tf_op jit(solution)/shard_map/ppermute | solution.py:342
  16.3 7.6 %collective-permute-start.4 = (bf16[6,6,512]{2,1,0:T(8,128)(2,1)S(1)}, bf16[6,6,512]{2,1,0:T(8,128)(2,1)S(1)}, u32[]{:S(2)}, u32[]{:S(2)}) collective-permute-start(bf16[6,6,512]{2,1,0:T(8,128)(2,1)S(1)} %get-tuple-element.18), channel_id=1, source_target_pairs={{24,0},{25,1},{26,2},{27,3},{28,4},{29,5},{30,6},{31,7},{0,8},{1,9... | collective-permute-start | bytes 110600 | tf_op jit(solution)/shard_map/ppermute | solution.py:342
  17.1 7.5 %collective-permute-start.5 = (bf16[6,6,512]{2,1,0:T(8,128)(2,1)S(1)}, bf16[6,6,512]{2,1,0:T(8,128)(2,1)S(1)}, u32[]{:S(2)}, u32[]{:S(2)}) collective-permute-start(bf16[6,6,512]{2,1,0:T(8,128)(2,1)S(1)} %get-tuple-element.19), channel_id=1, source_target_pairs={{7,0},{0,1},{1,2},{2,3},{3,4},{4,5},{5,6},{6,7},{15,8},{8,9},{9,10... | collective-permute-start | bytes 110600 | tf_op jit(solution)/shard_map/ppermute | solution.py:342

commit v9 on v8

--- a/solution.py
+++ b/solution.py
@@ -118,6 +118,16 @@
     return jnp.concatenate(parts, axis=0)
 
 
+def spread(value):
+    width = value.shape[-1]
+    tiles = value.reshape(WH * WW // SUB, SUB, width)
+    parts = []
+    for r in range(WH):
+        rest = tiles[WH + r // 2]
+        parts += [tiles[r], pltpu.roll(rest, REST, 0) if r % 2 else rest]
+    return jnp.concatenate(parts, axis=0)
+
+
 def split(value):
     high = value.astype(BF16)
     return high, (value - high.astype(F32)).astype(BF16)
@@ -147,16 +157,19 @@
     head_dim = width // HEADS
     group = LANES // head_dim
     per_head = WH * PITCH
-    x = xs[...].reshape(per_head, width)
+    x = compact(xs[...].reshape(per_head, width))
     mean = jnp.mean(x, axis=-1, keepdims=True)
     centred = x - mean
     var = jnp.mean(centred * centred, axis=-1, keepdims=True)
-    normed = (centred * lax.rsqrt(var + 1e-05) * gain[...]).astype(BF16)
+    normed = centred * lax.rsqrt(var + 1e-05) * gain[...]
+    spread_out = spread(normed).astype(BF16)
+    normed = normed.astype(BF16)
     wqkv = weights(0)
-    mixed = jnp.dot(normed, wqkv[...], preferred_element_type=F32)
-    q_hi, q_lo = split(mixed[:, :width] * (head_dim ** (-0.5) * LOG2E))
-    k_hi, k_lo = split(compact(mixed[:, width : 2 * width]))
-    values = compact(mixed[:, 2 * width :]).astype(BF16)
+    query = jnp.dot(spread_out, wqkv[:, :width], preferred_element_type=F32)
+    mixed = jnp.dot(normed, wqkv[:, width:], preferred_element_type=F32)
+    q_hi, q_lo = split(query * (head_dim ** (-0.5) * LOG2E))
+    k_hi, k_lo = split(mixed[:, :width])
+    values = mixed[:, width:].astype(BF16)
     lane = iota((1, LANES), 1)
     masks = None if polar is None else halves(polar)
 

time: 25.5 us -> 25.4 us (level)
  no operation moved by 1% of the time
where the time goes in v9:
time: 25.4 us; the launch traced here: 25.3 us
  waiting for transfers between devices  9.06 us (36%)
  starting transfers between devices  8.51 us (34%)
  Pallas kernels  6.9 us (27%)
  other arithmetic  0.74 us (3%)
    ppermute x6, waiting for transfers between devices, moved(): return lax.ppermute(piece, ('lat', 'lon'), route)  9.06 us
    ppermute x6, starting transfers between devices, moved(): return lax.ppermute(piece, ('lat', 'lon'), route)  8.51 us
    pallas_call x2, Pallas kernels, block(): pl.pallas_call(kernel, out_shape=(piece,) * 4, in_specs=[source] * len(ar...  5.98 us
    pallas_call x1, Pallas kernels, expand(): pl.pallas_call(bias_kernel, out_shape=jax.ShapeDtypeStruct(shape, F32), i...  0.92 us
    broadcast_in_dim x1, other arithmetic, shards(): return jnp.concatenate([upper, lower], axis=0)[None]  0.74 us
  transfers between devices with their start and end apart: 6, of which 3 were waited for; matrix products, arithmetic and copies ran while one was open for 0% of the time, Pallas kernels for 4%

profile of v9, /device:TPU:0, one launch (start us, length us, event | category | flops | bytes accessed | tf_op | source)
XLA Modules:
  0.0 25.3 jit_solution(3939893614338222752)
XLA Ops:
  0.0 0.0 copy-start.2
  0.0 0.0 copy-start
  0.0 0.0 copy-start.1
  0.0 0.0 copy-start.3
  0.0 3.8 %shard_map.91 = (bf16[36,512]{1,0:T(8,128)(2,1)S(1)}, bf16[36,512]{1,0:T(8,128)(2,1)S(1)}, bf16[36,512]{1,0:T(8,128)(2,1)S(1)}, bf16[36,512]{1,0:T(8,128)(2,1)S(1)}) custom-call(bf16[1,12,12,512]{3,2,1,0:T(8,128)(2,1)} %tokens.1, f32[1,16,529]{2,1,0:T(8,128)} %table.2, f32[1,512]{1,0:T(1,128)} %bitcast.5, bf16[512,1536]{1,0:T(8,128)(2,1)} %wqkv.2, ...), custom_call_target="tpu_custom_call" | custom-call | flops 400000000 | bytes 2500000 | tf_op jit(solution)/shard_map/pallas_call | solution.py:339
  3.8 6.1 %collective-permute-start = (bf16[36,512]{1,0:T(8,128)(2,1)S(1)}, bf16[36,512]{1,0:T(8,128)(2,1)S(1)}, u32[]{:S(2)}, u32[]{:S(2)}) collective-permute-start(bf16[36,512]{1,0:T(8,128)(2,1)S(1)} %get-tuple-element.14), channel_id=1, source_target_pairs={{1,0},{2,1},{3,2},{4,3},{5,4},{6,5},{7,6},{0,7},{9,8},{10,9},{11,1... | collective-permute-start | bytes 110600 | tf_op jit(solution)/shard_map/ppermute | solution.py:355
  9.9 0.7 %collective-permute-start.1 = (bf16[36,512]{1,0:T(8,128)(2,1)S(1)}, bf16[36,512]{1,0:T(8,128)(2,1)S(1)}, u32[]{:S(2)}, u32[]{:S(2)}) collective-permute-start(bf16[36,512]{1,0:T(8,128)(2,1)S(1)} %get-tuple-element.15), channel_id=1, source_target_pairs={{8,0},{9,1},{10,2},{11,3},{12,4},{13,5},{14,6},{15,7},{16,8},{17,9... | collective-permute-start | bytes 110600 | tf_op jit(solution)/shard_map/ppermute | solution.py:355
  10.6 0.9 %collective-permute-start.2 = (bf16[36,512]{1,0:T(8,128)(2,1)S(1)}, bf16[36,512]{1,0:T(8,128)(2,1)S(1)}, u32[]{:S(2)}, u32[]{:S(2)}) collective-permute-start(bf16[36,512]{1,0:T(8,128)(2,1)S(1)} %get-tuple-element.16), channel_id=1, source_target_pairs={{9,0},{10,1},{11,2},{12,3},{13,4},{14,5},{15,6},{8,7},{17,8},{18,9... | collective-permute-start | bytes 110600 | tf_op jit(solution)/shard_map/ppermute | solution.py:355
  11.4 0.0 copy-done.2
  11.5 0.9 %shard_map.92.bias = f32[8,3,18,8,128]{4,3,2,1,0:T(8,128)S(1)} custom-call(f32[1,16,529]{2,1,0:T(8,128)S(1)} %copy-done.2), custom_call_target="tpu_custom_call" | custom-call | flops 2000000 | bytes 1800000 | tf_op jit(solution)/shard_map/pallas_call | solution.py:310
  12.4 0.0 collective-permute-done.ne_in
  12.4 0.0 collective-permute-done.1.sw_in
  12.4 1.6 %collective-permute-done.2.se_in = bf16[36,512]{1,0:T(8,128)(2,1)S(1)} collective-permute-done((bf16[36,512]{1,0:T(8,128)(2,1)S(1)}, bf16[36,512]{1,0:T(8,128)(2,1)S(1)}, u32[]{:S(2)}, u32[]{:S(2)}) %collective-permute-start.2) | collective-permute-done | bytes 36896 | tf_op jit(solution)/shard_map/ppermute | solution.py:355
  14.0 0.0 copy-done
  14.0 0.0 copy-done.1
  14.0 0.0 copy-done.3
  14.0 2.2 %shard_map.93 = (bf16[6,6,512]{2,1,0:T(8,128)(2,1)S(1)}, bf16[6,6,512]{2,1,0:T(8,128)(2,1)S(1)}, bf16[6,6,512]{2,1,0:T(8,128)(2,1)S(1)}, bf16[6,6,512]{2,1,0:T(8,128)(2,1)S(1)}) custom-call(bf16[36,512]{1,0:T(8,128)(2,1)S(1)} %get-tuple-element.13.nw_in, bf16[36,512]{1,0:T(8,128)(2,1)S(1)} %collective-permute-done.ne_in, ...), custom_call_target="tpu_custom_call" | custom-call | flops 400000000 | bytes 2500000 | tf_op jit(solution)/shard_map/pallas_call | solution.py:339
  16.2 0.1 collective-permute-start.3
  16.3 0.8 %collective-permute-start.4 = (bf16[6,6,512]{2,1,0:T(8,128)(2,1)S(1)}, bf16[6,6,512]{2,1,0:T(8,128)(2,1)S(1)}, u32[]{:S(2)}, u32[]{:S(2)}) collective-permute-start(bf16[6,6,512]{2,1,0:T(8,128)(2,1)S(1)} %get-tuple-element.18), channel_id=1, source_target_pairs={{24,0},{25,1},{26,2},{27,3},{28,4},{29,5},{30,6},{31,7},{0,8},{1,9... | collective-permute-start | bytes 110600 | tf_op jit(solution)/shard_map/ppermute | solution.py:355
  17.1 0.0 collective-permute-start.5
  17.1 6.8 %collective-permute-done.3 = bf16[6,6,512]{2,1,0:T(8,128)(2,1)S(1)} collective-permute-done((bf16[6,6,512]{2,1,0:T(8,128)(2,1)S(1)}, bf16[6,6,512]{2,1,0:T(8,128)(2,1)S(1)}, u32[]{:S(2)}, u32[]{:S(2)}) %collective-permute-start.3) | collective-permute-done | bytes 36896 | tf_op jit(solution)/shard_map/ppermute | solution.py:355
  23.8 0.0 collective-permute-done.4
  23.9 0.7 %collective-permute-done.5 = bf16[6,6,512]{2,1,0:T(8,128)(2,1)S(1)} collective-permute-done((bf16[6,6,512]{2,1,0:T(8,128)(2,1)S(1)}, bf16[6,6,512]{2,1,0:T(8,128)(2,1)S(1)}, u32[]{:S(2)}, u32[]{:S(2)}) %collective-permute-start.5) | collective-permute-done | bytes 36896 | tf_op jit(solution)/shard_map/ppermute | solution.py:355
  24.5 0.7 %maximum_bitcast_fusion = bf16[1,12,12,512]{3,2,1,0:T(8,128)(2,1)} fusion(bf16[6,6,512]{2,1,0:T(8,128)(2,1)S(1)} %get-tuple-element.20, bf16[6,6,512]{2,1,0:T(8,128)(2,1)S(1)} %collective-permute-done.5, bf16[6,6,512]{2,1,0:T(8,128)(2,1)S(1)} %collective-permute-done.4, bf16[6,6,512]{2,1,0:T(8,128)(2,1)S(1)} %collective-permute-done.3), kind=kLoop, calls=%fused_computation | loop fusion | flops 589824 | bytes 294912 | tf_op jit(solution)/shard_map/broadcast_in_dim | solution.py:380
Async XLA Ops:
  0.0 11.5 %copy-start.2 = (f32[1,16,529]{2,1,0:T(8,128)S(1)}, f32[1,16,529]{2,1,0:T(8,128)}, u32[]{:S(2)}) copy-start(f32[1,16,529]{2,1,0:T(8,128)} %table.3) | copy-start | bytes 101572
  0.0 14.0 %copy-start = (bf16[512,1536]{1,0:T(8,128)(2,1)S(1)}, bf16[512,1536]{1,0:T(8,128)(2,1)}, u32[]{:S(2)}) copy-start(bf16[512,1536]{1,0:T(8,128)(2,1)} %wqkv.3) | copy-start | bytes 4718596
  0.0 14.0 %copy-start.1 = (bf16[512,512]{1,0:T(8,128)(2,1)S(1)}, bf16[512,512]{1,0:T(8,128)(2,1)}, u32[]{:S(2)}) copy-start(bf16[512,512]{1,0:T(8,128)(2,1)} %wproj.3) | copy-start | bytes 1572868
  0.0 14.0 %copy-start.3 = (f32[512]{0:T(512)S(1)}, f32[512]{0:T(512)}, u32[]{:S(2)}) copy-start(f32[512]{0:T(512)} %param.14) | copy-start | bytes 6148
  3.8 8.6 %collective-permute-start = (bf16[36,512]{1,0:T(8,128)(2,1)S(1)}, bf16[36,512]{1,0:T(8,128)(2,1)S(1)}, u32[]{:S(2)}, u32[]{:S(2)}) collective-permute-start(bf16[36,512]{1,0:T(8,128)(2,1)S(1)} %get-tuple-element.14), channel_id=1, source_target_pairs={{1,0},{2,1},{3,2},{4,3},{5,4},{6,5},{7,6},{0,7},{9,8},{10,9},{11,1... | collective-permute-start | bytes 110600 | tf_op jit(solution)/shard_map/ppermute | solution.py:355
  9.9 2.5 %collective-permute-start.1 = (bf16[36,512]{1,0:T(8,128)(2,1)S(1)}, bf16[36,512]{1,0:T(8,128)(2,1)S(1)}, u32[]{:S(2)}, u32[]{:S(2)}) collective-permute-start(bf16[36,512]{1,0:T(8,128)(2,1)S(1)} %get-tuple-element.15), channel_id=1, source_target_pairs={{8,0},{9,1},{10,2},{11,3},{12,4},{13,5},{14,6},{15,7},{16,8},{17,9... | collective-permute-start | bytes 110600 | tf_op jit(solution)/shard_map/ppermute | solution.py:355
  10.6 3.4 %collective-permute-start.2 = (bf16[36,512]{1,0:T(8,128)(2,1)S(1)}, bf16[36,512]{1,0:T(8,128)(2,1)S(1)}, u32[]{:S(2)}, u32[]{:S(2)}) collective-permute-start(bf16[36,512]{1,0:T(8,128)(2,1)S(1)} %get-tuple-element.16), channel_id=1, source_target_pairs={{9,0},{10,1},{11,2},{12,3},{13,4},{14,5},{15,6},{8,7},{17,8},{18,9... | collective-permute-start | bytes 110600 | tf_op jit(solution)/shard_map/ppermute | solution.py:355
  16.2 7.7 %collective-permute-start.3 = (bf16[6,6,512]{2,1,0:T(8,128)(2,1)S(1)}, bf16[6,6,512]{2,1,0:T(8,128)(2,1)S(1)}, u32[]{:S(2)}, u32[]{:S(2)}) collective-permute-start(bf16[6,6,512]{2,1,0:T(8,128)(2,1)S(1)} %get-tuple-element.17), channel_id=1, source_target_pairs={{31,0},{24,1},{25,2},{26,3},{27,4},{28,5},{29,6},{30,7},{7,8},{0,9... | collective-permute-start | bytes 110600 | tf_op jit(solution)/shard_map/ppermute | solution.py:355
  16.3 7.6 %collective-permute-start.4 = (bf16[6,6,512]{2,1,0:T(8,128)(2,1)S(1)}, bf16[6,6,512]{2,1,0:T(8,128)(2,1)S(1)}, u32[]{:S(2)}, u32[]{:S(2)}) collective-permute-start(bf16[6,6,512]{2,1,0:T(8,128)(2,1)S(1)} %get-tuple-element.18), channel_id=1, source_target_pairs={{24,0},{25,1},{26,2},{27,3},{28,4},{29,5},{30,6},{31,7},{0,8},{1,9... | collective-permute-start | bytes 110600 | tf_op jit(solution)/shard_map/ppermute | solution.py:355
  17.1 7.5 %collective-permute-start.5 = (bf16[6,6,512]{2,1,0:T(8,128)(2,1)S(1)}, bf16[6,6,512]{2,1,0:T(8,128)(2,1)S(1)}, u32[]{:S(2)}, u32[]{:S(2)}) collective-permute-start(bf16[6,6,512]{2,1,0:T(8,128)(2,1)S(1)} %get-tuple-element.19), channel_id=1, source_target_pairs={{7,0},{0,1},{1,2},{2,3},{3,4},{4,5},{5,6},{6,7},{15,8},{8,9},{9,10... | collective-permute-start | bytes 110600 | tf_op jit(solution)/shard_map/ppermute | solution.py:355

commit v10 on v9

--- a/solution.py
+++ b/solution.py
@@ -10,8 +10,6 @@
 
 
 HEADS = 16
-CUTS = 4
-CUT_FROM = 1 << 19
 WH = 12
 WW = 12
 LANES = 128
@@ -164,12 +162,11 @@
     normed = centred * lax.rsqrt(var + 1e-05) * gain[...]
     spread_out = spread(normed).astype(BF16)
     normed = normed.astype(BF16)
-    wqkv = weights(0)
-    query = jnp.dot(spread_out, wqkv[:, :width], preferred_element_type=F32)
-    mixed = jnp.dot(normed, wqkv[:, width:], preferred_element_type=F32)
+    query = jnp.dot(spread_out, weights(0)[...], preferred_element_type=F32)
+    keys = jnp.dot(normed, weights(1)[...], preferred_element_type=F32)
+    values = jnp.dot(normed, weights(2)[...], preferred_element_type=F32).astype(BF16)
     q_hi, q_lo = split(query * (head_dim ** (-0.5) * LOG2E))
-    k_hi, k_lo = split(mixed[:, :width])
-    values = mixed[:, width:].astype(BF16)
+    k_hi, k_lo = split(keys)
     lane = iota((1, LANES), 1)
     masks = None if polar is None else halves(polar)
 
@@ -213,7 +210,7 @@
                 soft(scores[:, at : at + LANES], tiles[t], masks and masks[t], probs.at[g], at)
     outs.append(gather(groups - 1))
     heads_out = jnp.concatenate(outs, axis=1)[:per_head].astype(BF16)
-    wproj = weights(1)
+    wproj = weights(3)
     branch = jnp.dot(heads_out, wproj[...], preferred_element_type=F32)
     ys[...] = xs[...] + branch.reshape(xs.shape)
 
@@ -240,21 +237,16 @@
             xs[r + i, c : c + HALF_C, :] = zs[at, i * HALF_C : (i + 1) * HALF_C, :]
 
 
-def cuts(shape):
-    if len(shape) == 2 and shape[0] * shape[1] >= CUT_FROM:
-        rows = shape[0] // CUTS
-        return [pl.ds(i * rows, rows) for i in range(CUTS)]
-    return [slice(None)]
-
-
-def pieces_of(source, target):
-    return [(source.at[part], target.at[part]) for part in cuts(source.shape)]
+def parts_of(wqkv, wproj):
+    width = wproj.shape[0]
+    return [wqkv.at[:, i * width : (i + 1) * width] for i in range(3)] + [wproj]
 
 
 def first_kernel(tokens, table, gain, wqkv, wproj, nw, ne, sw, se, xs, ys, zs, probs, tab, strips, *here):
     here, sems = here[:-1], here[-1]
-    pairs = [pair for a, b in zip((table, tokens, gain, wqkv, wproj), here) for pair in pieces_of(a, b)]
-    copies = [pltpu.make_async_copy(a, b, sems.at[i]) for i, (a, b) in enumerate(pairs)]
+    sources = (table, tokens, gain, *parts_of(wqkv, wproj))
+    targets = (*here[:3], *parts_of(*here[3:]))
+    copies = [pltpu.make_async_copy(a, b, sems.at[i]) for i, (a, b) in enumerate(zip(sources, targets))]
     for copy in copies:
         copy.start()
     xs[:, WW:, :] = jnp.zeros((WH, PITCH - WW, xs.shape[-1]), F32)
@@ -265,9 +257,8 @@
     copies[2].wait()
 
     def weights(i):
-        for copy in (copies[3:-1], copies[-1:])[i]:
-            copy.wait()
-        return here[3 + i]
+        copies[3 + i].wait()
+        return targets[3 + i]
 
     attend(xs, ys, here[2], weights, functools.partial(bias_tiles, strips), probs, None)
     packed(ys, zs, (nw, ne, sw, se))
@@ -289,7 +280,7 @@
     def tiles_of(h):
         return [[bias[h // 2, t, u] for u in range(bias.shape[2])] for t in range(bias.shape[1])]
 
-    attend(xs, ys, gain, lambda i: (wqkv, wproj)[i], tiles_of, probs, polar)
+    attend(xs, ys, gain, lambda i: parts_of(wqkv, wproj)[i], tiles_of, probs, polar)
     quadrants(ys, (nw, ne, sw, se))
 
 
@@ -333,7 +324,7 @@
         order = (args[1], args[0], *args[2:])
         scratch += bias_room(bias)
         scratch += [pltpu.VMEM(a.shape, a.dtype) for a in order]
-        scratch += [pltpu.SemaphoreType.DMA((sum(len(cuts(a.shape)) for a in order),))]
+        scratch += [pltpu.SemaphoreType.DMA((len(order) + 2,))]
         args = tuple(pltpu.with_memory_space_constraint(a, pltpu.HBM) for a in args)
     source = HBM if fetch else VMEM
     return pl.pallas_call(

time: 25.4 us -> 25.7 us (1.012)
  no operation moved by 1% of the time
where the time goes in v10:
time: 25.7 us; the launch traced here: 25.5 us
  waiting for transfers between devices  9.05 us (35%)
  starting transfers between devices  8.52 us (33%)
  Pallas kernels  7.12 us (28%)
  other arithmetic  0.74 us (3%)
    ppermute x6, waiting for transfers between devices, moved(): return lax.ppermute(piece, ('lat', 'lon'), route)  9.05 us
    ppermute x6, starting transfers between devices, moved(): return lax.ppermute(piece, ('lat', 'lon'), route)  8.52 us
    pallas_call x2, Pallas kernels, block(): pl.pallas_call(kernel, out_shape=(piece,) * 4, in_specs=[source] * len(ar...  6.2 us
    pallas_call x1, Pallas kernels, expand(): pl.pallas_call(bias_kernel, out_shape=jax.ShapeDtypeStruct(shape, F32), i...  0.92 us
    broadcast_in_dim x1, other arithmetic, shards(): return jnp.concatenate([upper, lower], axis=0)[None]  0.74 us
  transfers between devices with their start and end apart: 6, of which 3 were waited for; matrix products, arithmetic and copies ran while one was open for 0% of the time, Pallas kernels for 4%

profile of v10, /device:TPU:0, one launch (start us, length us, event | category | flops | bytes accessed | tf_op | source)
XLA Modules:
  0.0 25.5 jit_solution(11623992848287793098)
XLA Ops:
  0.0 0.0 copy-start.2
  0.0 0.0 copy-start
  0.0 0.0 copy-start.1
  0.0 0.0 copy-start.3
  0.0 4.0 %shard_map.91 = (bf16[36,512]{1,0:T(8,128)(2,1)S(1)}, bf16[36,512]{1,0:T(8,128)(2,1)S(1)}, bf16[36,512]{1,0:T(8,128)(2,1)S(1)}, bf16[36,512]{1,0:T(8,128)(2,1)S(1)}) custom-call(bf16[1,12,12,512]{3,2,1,0:T(8,128)(2,1)} %tokens.1, f32[1,16,529]{2,1,0:T(8,128)} %table.2, f32[1,512]{1,0:T(1,128)} %bitcast.5, bf16[512,1536]{1,0:T(8,128)(2,1)} %wqkv.2, ...), custom_call_target="tpu_custom_call" | custom-call | flops 400000000 | bytes 2500000 | tf_op jit(solution)/shard_map/pallas_call | solution.py:330
  4.0 6.1 %collective-permute-start = (bf16[36,512]{1,0:T(8,128)(2,1)S(1)}, bf16[36,512]{1,0:T(8,128)(2,1)S(1)}, u32[]{:S(2)}, u32[]{:S(2)}) collective-permute-start(bf16[36,512]{1,0:T(8,128)(2,1)S(1)} %get-tuple-element.14), channel_id=1, source_target_pairs={{1,0},{2,1},{3,2},{4,3},{5,4},{6,5},{7,6},{0,7},{9,8},{10,9},{11,1... | collective-permute-start | bytes 110600 | tf_op jit(solution)/shard_map/ppermute | solution.py:346
  10.1 0.7 %collective-permute-start.1 = (bf16[36,512]{1,0:T(8,128)(2,1)S(1)}, bf16[36,512]{1,0:T(8,128)(2,1)S(1)}, u32[]{:S(2)}, u32[]{:S(2)}) collective-permute-start(bf16[36,512]{1,0:T(8,128)(2,1)S(1)} %get-tuple-element.15), channel_id=1, source_target_pairs={{8,0},{9,1},{10,2},{11,3},{12,4},{13,5},{14,6},{15,7},{16,8},{17,9... | collective-permute-start | bytes 110600 | tf_op jit(solution)/shard_map/ppermute | solution.py:346
  10.8 0.9 %collective-permute-start.2 = (bf16[36,512]{1,0:T(8,128)(2,1)S(1)}, bf16[36,512]{1,0:T(8,128)(2,1)S(1)}, u32[]{:S(2)}, u32[]{:S(2)}) collective-permute-start(bf16[36,512]{1,0:T(8,128)(2,1)S(1)} %get-tuple-element.16), channel_id=1, source_target_pairs={{9,0},{10,1},{11,2},{12,3},{13,4},{14,5},{15,6},{8,7},{17,8},{18,9... | collective-permute-start | bytes 110600 | tf_op jit(solution)/shard_map/ppermute | solution.py:346
  11.7 0.0 copy-done.2
  11.7 0.9 %shard_map.92.bias = f32[8,3,18,8,128]{4,3,2,1,0:T(8,128)S(1)} custom-call(f32[1,16,529]{2,1,0:T(8,128)S(1)} %copy-done.2), custom_call_target="tpu_custom_call" | custom-call | flops 2000000 | bytes 1800000 | tf_op jit(solution)/shard_map/pallas_call | solution.py:301
  12.6 0.0 collective-permute-done.ne_in
  12.6 0.0 collective-permute-done.1.sw_in
  12.6 1.6 %collective-permute-done.2.se_in = bf16[36,512]{1,0:T(8,128)(2,1)S(1)} collective-permute-done((bf16[36,512]{1,0:T(8,128)(2,1)S(1)}, bf16[36,512]{1,0:T(8,128)(2,1)S(1)}, u32[]{:S(2)}, u32[]{:S(2)}) %collective-permute-start.2) | collective-permute-done | bytes 36896 | tf_op jit(solution)/shard_map/ppermute | solution.py:346
  14.2 0.0 copy-done
  14.2 0.0 copy-done.1
  14.2 0.0 copy-done.3
  14.2 2.2 %shard_map.93 = (bf16[6,6,512]{2,1,0:T(8,128)(2,1)S(1)}, bf16[6,6,512]{2,1,0:T(8,128)(2,1)S(1)}, bf16[6,6,512]{2,1,0:T(8,128)(2,1)S(1)}, bf16[6,6,512]{2,1,0:T(8,128)(2,1)S(1)}) custom-call(bf16[36,512]{1,0:T(8,128)(2,1)S(1)} %get-tuple-element.13.nw_in, bf16[36,512]{1,0:T(8,128)(2,1)S(1)} %collective-permute-done.ne_in, ...), custom_call_target="tpu_custom_call" | custom-call | flops 400000000 | bytes 2500000 | tf_op jit(solution)/shard_map/pallas_call | solution.py:330
  16.4 0.1 collective-permute-start.3
  16.5 0.8 %collective-permute-start.4 = (bf16[6,6,512]{2,1,0:T(8,128)(2,1)S(1)}, bf16[6,6,512]{2,1,0:T(8,128)(2,1)S(1)}, u32[]{:S(2)}, u32[]{:S(2)}) collective-permute-start(bf16[6,6,512]{2,1,0:T(8,128)(2,1)S(1)} %get-tuple-element.18), channel_id=1, source_target_pairs={{24,0},{25,1},{26,2},{27,3},{28,4},{29,5},{30,6},{31,7},{0,8},{1,9... | collective-permute-start | bytes 110600 | tf_op jit(solution)/shard_map/ppermute | solution.py:346
  17.3 0.0 collective-permute-start.5
  17.3 6.8 %collective-permute-done.3 = bf16[6,6,512]{2,1,0:T(8,128)(2,1)S(1)} collective-permute-done((bf16[6,6,512]{2,1,0:T(8,128)(2,1)S(1)}, bf16[6,6,512]{2,1,0:T(8,128)(2,1)S(1)}, u32[]{:S(2)}, u32[]{:S(2)}) %collective-permute-start.3) | collective-permute-done | bytes 36896 | tf_op jit(solution)/shard_map/ppermute | solution.py:346
  24.1 0.0 collective-permute-done.4
  24.1 0.7 %collective-permute-done.5 = bf16[6,6,512]{2,1,0:T(8,128)(2,1)S(1)} collective-permute-done((bf16[6,6,512]{2,1,0:T(8,128)(2,1)S(1)}, bf16[6,6,512]{2,1,0:T(8,128)(2,1)S(1)}, u32[]{:S(2)}, u32[]{:S(2)}) %collective-permute-start.5) | collective-permute-done | bytes 36896 | tf_op jit(solution)/shard_map/ppermute | solution.py:346
  24.8 0.7 %maximum_bitcast_fusion = bf16[1,12,12,512]{3,2,1,0:T(8,128)(2,1)} fusion(bf16[6,6,512]{2,1,0:T(8,128)(2,1)S(1)} %get-tuple-element.20, bf16[6,6,512]{2,1,0:T(8,128)(2,1)S(1)} %collective-permute-done.5, bf16[6,6,512]{2,1,0:T(8,128)(2,1)S(1)} %collective-permute-done.4, bf16[6,6,512]{2,1,0:T(8,128)(2,1)S(1)} %collective-permute-done.3), kind=kLoop, calls=%fused_computation | loop fusion | flops 589824 | bytes 294912 | tf_op jit(solution)/shard_map/broadcast_in_dim | solution.py:371
Async XLA Ops:
  0.0 11.7 %copy-start.2 = (f32[1,16,529]{2,1,0:T(8,128)S(1)}, f32[1,16,529]{2,1,0:T(8,128)}, u32[]{:S(2)}) copy-start(f32[1,16,529]{2,1,0:T(8,128)} %table.3) | copy-start | bytes 101572
  0.0 14.2 %copy-start = (bf16[512,1536]{1,0:T(8,128)(2,1)S(1)}, bf16[512,1536]{1,0:T(8,128)(2,1)}, u32[]{:S(2)}) copy-start(bf16[512,1536]{1,0:T(8,128)(2,1)} %wqkv.3) | copy-start | bytes 4718596
  0.0 14.2 %copy-start.1 = (bf16[512,512]{1,0:T(8,128)(2,1)S(1)}, bf16[512,512]{1,0:T(8,128)(2,1)}, u32[]{:S(2)}) copy-start(bf16[512,512]{1,0:T(8,128)(2,1)} %wproj.3) | copy-start | bytes 1572868
  0.0 14.2 %copy-start.3 = (f32[512]{0:T(512)S(1)}, f32[512]{0:T(512)}, u32[]{:S(2)}) copy-start(f32[512]{0:T(512)} %param.14) | copy-start | bytes 6148
  4.0 8.6 %collective-permute-start = (bf16[36,512]{1,0:T(8,128)(2,1)S(1)}, bf16[36,512]{1,0:T(8,128)(2,1)S(1)}, u32[]{:S(2)}, u32[]{:S(2)}) collective-permute-start(bf16[36,512]{1,0:T(8,128)(2,1)S(1)} %get-tuple-element.14), channel_id=1, source_target_pairs={{1,0},{2,1},{3,2},{4,3},{5,4},{6,5},{7,6},{0,7},{9,8},{10,9},{11,1... | collective-permute-start | bytes 110600 | tf_op jit(solution)/shard_map/ppermute | solution.py:346
  10.1 2.5 %collective-permute-start.1 = (bf16[36,512]{1,0:T(8,128)(2,1)S(1)}, bf16[36,512]{1,0:T(8,128)(2,1)S(1)}, u32[]{:S(2)}, u32[]{:S(2)}) collective-permute-start(bf16[36,512]{1,0:T(8,128)(2,1)S(1)} %get-tuple-element.15), channel_id=1, source_target_pairs={{8,0},{9,1},{10,2},{11,3},{12,4},{13,5},{14,6},{15,7},{16,8},{17,9... | collective-permute-start | bytes 110600 | tf_op jit(solution)/shard_map/ppermute | solution.py:346
  10.8 3.4 %collective-permute-start.2 = (bf16[36,512]{1,0:T(8,128)(2,1)S(1)}, bf16[36,512]{1,0:T(8,128)(2,1)S(1)}, u32[]{:S(2)}, u32[]{:S(2)}) collective-permute-start(bf16[36,512]{1,0:T(8,128)(2,1)S(1)} %get-tuple-element.16), channel_id=1, source_target_pairs={{9,0},{10,1},{11,2},{12,3},{13,4},{14,5},{15,6},{8,7},{17,8},{18,9... | collective-permute-start | bytes 110600 | tf_op jit(solution)/shard_map/ppermute | solution.py:346
  16.4 7.7 %collective-permute-start.3 = (bf16[6,6,512]{2,1,0:T(8,128)(2,1)S(1)}, bf16[6,6,512]{2,1,0:T(8,128)(2,1)S(1)}, u32[]{:S(2)}, u32[]{:S(2)}) collective-permute-start(bf16[6,6,512]{2,1,0:T(8,128)(2,1)S(1)} %get-tuple-element.17), channel_id=1, source_target_pairs={{31,0},{24,1},{25,2},{26,3},{27,4},{28,5},{29,6},{30,7},{7,8},{0,9... | collective-permute-start | bytes 110600 | tf_op jit(solution)/shard_map/ppermute | solution.py:346
  16.5 7.6 %collective-permute-start.4 = (bf16[6,6,512]{2,1,0:T(8,128)(2,1)S(1)}, bf16[6,6,512]{2,1,0:T(8,128)(2,1)S(1)}, u32[]{:S(2)}, u32[]{:S(2)}) collective-permute-start(bf16[6,6,512]{2,1,0:T(8,128)(2,1)S(1)} %get-tuple-element.18), channel_id=1, source_target_pairs={{24,0},{25,1},{26,2},{27,3},{28,4},{29,5},{30,6},{31,7},{0,8},{1,9... | collective-permute-start | bytes 110600 | tf_op jit(solution)/shard_map/ppermute | solution.py:346
  17.3 7.5 %collective-permute-start.5 = (bf16[6,6,512]{2,1,0:T(8,128)(2,1)S(1)}, bf16[6,6,512]{2,1,0:T(8,128)(2,1)S(1)}, u32[]{:S(2)}, u32[]{:S(2)}) collective-permute-start(bf16[6,6,512]{2,1,0:T(8,128)(2,1)S(1)} %get-tuple-element.19), channel_id=1, source_target_pairs={{7,0},{0,1},{1,2},{2,3},{3,4},{4,5},{5,6},{6,7},{15,8},{8,9},{9,10... | collective-permute-start | bytes 110600 | tf_op jit(solution)/shard_map/ppermute | solution.py:346
